TPU v7x, 512 devices: a whole 4x8x8 slice. The times are simulated.
512 devices in a mesh: freq: 32 (over z, x), bfly: 16 (over y, core).
Axes of the slice: x: 4, y: 8, z: 8, core: 2. Of those that a mesh axis runs over, the one named last changes fastest.
Arguments:
- sources: bfloat16 [2, 2048, 8192], P(None, 'bfly', 'freq'), may hold values from -6 to 6
- observed: bfloat16 [2, 2048, 8192], P(None, 'bfly', 'freq'), may hold values from -4 to 4
- receivers: int32 [2048], P('bfly'), may hold values from 0 to 127
- model: float32 [2048], P('bfly'), may hold values from 0.25 to 1.75
- phases: float32 [4, 2048, 128], P(None, 'bfly', 'freq'), may hold values from -3.140625 to 3.140625
- near_blocks: bfloat16 [4, 2, 2048, 128], P(None, None, 'bfly'), may hold values from -0.25 to 0.25
- far_blocks: bfloat16 [4, 2, 2048, 128], P(None, None, 'bfly'), may hold values from -0.25 to 0.25
- pattern: int32 [4, 2, 32, 2], P(None, None, 'bfly'), may hold values 0 or 1
Outputs:
- gradient: float32 [2048], P('bfly')
- residual: float32 [2, 2048, 8192], P(None, 'bfly', 'freq')
Inputs may be any that keep to these rules, and one draw needn't show every extreme that they name: `receivers`: entries may repeat; receiver j belongs to block j // 128.
All inputs are finite; a program needn't handle non-finite values. No bound on the sum of `pattern` on one device may be relied on, other than what follows from the above.
Results may differ from a plain program's by a relative error of at most 0.0055.
Values may be sent and summed in bfloat16 or wider, within the bound.
No kernel may reach another device: no remote copies, remote signals or barrier semaphores. Data moves between devices by JAX's collectives and lax.ppermute only.
A program may use at most 64 MiB of HBM per device.

v0:
```python
import jax
import jax.numpy as jnp
from jax import lax
from jax.sharding import PartitionSpec as P

epsilon = 1e-05


def swapped(block, axis, stride):
    count = lax.axis_size(axis)
    route = []
    for low in range(count):
        high = low | 1 << stride
        if high != low and high < count:
            route += [(low, high), (high, low)]
    return lax.ppermute(block, axis, route)


def forward_mul(blocks, values):
    real_part = jnp.dot(blocks[0], values[0], preferred_element_type=jnp.float32) - jnp.dot(
        blocks[1], values[1], preferred_element_type=jnp.float32
    )
    imag_part = jnp.dot(blocks[0], values[1], preferred_element_type=jnp.float32) + jnp.dot(
        blocks[1], values[0], preferred_element_type=jnp.float32
    )
    return jnp.stack([real_part, imag_part])


def transposed(blocks, values):
    contract = (((0,), (0,)), ((), ()))
    return lax.dot_general(blocks, values, contract, preferred_element_type=jnp.float32)


def adjoint_mul(blocks, values):
    real_part = transposed(blocks[0], values[0]) + transposed(blocks[1], values[1])
    imag_part = transposed(blocks[0], values[1]) - transposed(blocks[1], values[0])
    return jnp.stack([real_part, imag_part])


def expand(phases, level, repeats):
    angle = jnp.repeat(phases[level], repeats, axis=-1)
    return (jnp.cos(angle), jnp.sin(angle))


def local(sources, observed, receivers, model, phases, near_blocks, far_blocks, pattern):
    columns = sources.shape[-1]
    levels = near_blocks.shape[0]
    width = near_blocks.shape[-1]
    rank = width // pattern.shape[-1]
    repeats = columns // phases.shape[-1]
    mask = jnp.repeat(jnp.repeat(pattern, rank, axis=2), rank, axis=3).astype(jnp.bfloat16)
    near = near_blocks * mask[:, 0:1]
    far = far_blocks * mask[:, 1:2]
    source_wide = sources.astype(jnp.float32)
    field = (model[None, :, None] * source_wide).astype(jnp.bfloat16)
    for level in range(levels):
        partner_field = swapped(field, "bfly", level)
        mixed = forward_mul(near[level], field) + forward_mul(far[level], partner_field)
        cosine, sine = expand(phases, level, repeats)
        field = jnp.stack(
            [cosine * mixed[0] - sine * mixed[1], sine * mixed[0] + cosine * mixed[1]]
        ).astype(jnp.bfloat16)
    selector = (receivers[:, None] == jnp.arange(width, dtype=jnp.int32)[None, :]).astype(
        jnp.bfloat16
    )
    picked = jnp.einsum("rs,psc->prc", selector, field, preferred_element_type=jnp.float32)
    residual = picked - observed.astype(jnp.float32)
    back = jnp.einsum(
        "rs,prc->psc", selector, residual.astype(jnp.bfloat16), preferred_element_type=jnp.float32
    )
    adjoint = back.astype(jnp.bfloat16)
    for level in reversed(range(levels)):
        cosine, sine = expand(phases, level, repeats)
        adjoint_wide = adjoint.astype(jnp.float32)
        turned = jnp.stack(
            [
                cosine * adjoint_wide[0] + sine * adjoint_wide[1],
                cosine * adjoint_wide[1] - sine * adjoint_wide[0],
            ]
        ).astype(jnp.bfloat16)
        local_term = adjoint_mul(near[level], turned)
        far_term = swapped(adjoint_mul(far[level], turned).astype(jnp.bfloat16), "bfly", level)
        adjoint = (local_term + far_term.astype(jnp.float32)).astype(jnp.bfloat16)
    adjoint_wide = adjoint.astype(jnp.float32)
    gradient_part = jnp.sum(
        source_wide[0] * adjoint_wide[0] + source_wide[1] * adjoint_wide[1], axis=-1
    )
    illumination = jnp.sum(
        source_wide[0] * source_wide[0] + source_wide[1] * source_wide[1], axis=-1
    )
    gradient_part, illumination = lax.psum((gradient_part, illumination), "freq")
    gradient = gradient_part / jnp.sqrt(illumination + epsilon)
    return (gradient, residual)


def solution(mesh):
    return jax.shard_map(
        local,
        mesh=mesh,
        in_specs=(
            P(None, "bfly", "freq"),
            P(None, "bfly", "freq"),
            P("bfly"),
            P("bfly"),
            P(None, "bfly", "freq"),
            P(None, None, "bfly", None),
            P(None, None, "bfly", None),
            P(None, None, "bfly", None),
        ),
        out_specs=(P("bfly"), P(None, "bfly", "freq")),
        check_vma=False,
    )
```

profile of v0, /device:TPU:24, one launch (start us, length us, event | category | flops | bytes accessed | tf_op | source)
XLA Modules:
  0.0 162.8 jit_solution(2418208753072402871)
XLA Ops:
  0.6 1.0 multiply_convert_fusion
  1.7 1.9 %collective-permute-start = (bf16[2,128,256]{2,1,0:T(8,128)(2,1)S(1)}, bf16[2,128,256]{2,1,0:T(8,128)(2,1)S(1)}, u32[]{:S(2)}, u32[]{:S(2)}) collective-permute-start(bf16[2,128,256]{2,1,0:T(8,128)(2,1)S(1)} %multiply_convert_fusion), channel_id=1, source_target_pairs={{0,1},{1,0},{2,3},{3,2},{4,5},{5,4},{6,7},{7,6},{8,9},{9,8},{10,11... | collective-permute-start | bytes 393224 | tf_op jit(solution)/shard_map/ppermute | solution.py:16
  4.1 0.8 copy-done.1
  5.4 0.6 copy-done.4
  6.3 0.7 copy-done
  8.0 0.8 copy-done.3
  10.1 2.4 %collective-permute-start.1 = (bf16[2,128,256]{2,1,0:T(8,128)(2,1)S(1)}, bf16[2,128,256]{2,1,0:T(8,128)(2,1)S(1)}, u32[]{:S(2)}, u32[]{:S(2)}) collective-permute-start(bf16[2,128,256]{2,1,0:T(8,128)(2,1)S(1)} %pad_maximum_fusion), channel_id=1, source_target_pairs={{0,2},{2,0},{1,3},{3,1},{4,6},{6,4},{5,7},{7,5},{8,10},{10,8},{9,1... | collective-permute-start | bytes 393224 | tf_op jit(solution)/shard_map/ppermute | solution.py:16
  12.8 5.1 %collective-permute-done.1 = bf16[2,128,256]{2,1,0:T(8,128)(2,1)S(1)} collective-permute-done((bf16[2,128,256]{2,1,0:T(8,128)(2,1)S(1)}, bf16[2,128,256]{2,1,0:T(8,128)(2,1)S(1)}, u32[]{:S(2)}, u32[]{:S(2)}) %collective-permute-start.1) | collective-permute-done | bytes 131104 | tf_op jit(solution)/shard_map/ppermute | solution.py:16
  18.9 6.3 %collective-permute-start.2 = (bf16[2,128,256]{2,1,0:T(8,128)(2,1)S(1)}, bf16[2,128,256]{2,1,0:T(8,128)(2,1)S(1)}, u32[]{:S(2)}, u32[]{:S(2)}) collective-permute-start(bf16[2,128,256]{2,1,0:T(8,128)(2,1)S(1)} %pad_maximum_fusion.1), channel_id=1, source_target_pairs={{0,4},{4,0},{1,5},{5,1},{2,6},{6,2},{3,7},{7,3},{8,12},{12,8},{9,1... | collective-permute-start | bytes 393224 | tf_op jit(solution)/shard_map/ppermute | solution.py:16
  25.5 6.1 %collective-permute-done.2 = bf16[2,128,256]{2,1,0:T(8,128)(2,1)S(1)} collective-permute-done((bf16[2,128,256]{2,1,0:T(8,128)(2,1)S(1)}, bf16[2,128,256]{2,1,0:T(8,128)(2,1)S(1)}, u32[]{:S(2)}, u32[]{:S(2)}) %collective-permute-start.2) | collective-permute-done | bytes 131104 | tf_op jit(solution)/shard_map/ppermute | solution.py:16
  32.6 3.0 %collective-permute-start.3 = (bf16[2,128,256]{2,1,0:T(8,128)(2,1)S(1)}, bf16[2,128,256]{2,1,0:T(8,128)(2,1)S(1)}, u32[]{:S(2)}, u32[]{:S(2)}) collective-permute-start(bf16[2,128,256]{2,1,0:T(8,128)(2,1)S(1)} %pad_maximum_fusion.2), channel_id=1, source_target_pairs={{0,8},{8,0},{1,9},{9,1},{2,10},{10,2},{3,11},{11,3},{4,12},{12,4},... | collective-permute-start | bytes 393224 | tf_op jit(solution)/shard_map/ppermute | solution.py:16
  36.0 8.0 %collective-permute-done.3 = bf16[2,128,256]{2,1,0:T(8,128)(2,1)S(1)} collective-permute-done((bf16[2,128,256]{2,1,0:T(8,128)(2,1)S(1)}, bf16[2,128,256]{2,1,0:T(8,128)(2,1)S(1)}, u32[]{:S(2)}, u32[]{:S(2)}) %collective-permute-start.3) | collective-permute-done | bytes 131104 | tf_op jit(solution)/shard_map/ppermute | solution.py:16
  44.7 0.6 copy-done.6
  45.3 0.3 fusion
  45.6 0.2 fusion.2
  46.1 0.2 fusion.74
  46.3 0.2 fusion.70
  46.7 0.2 fusion.42
  46.9 0.2 fusion.41
  47.1 5.1 %collective-permute-start.4 = (bf16[2,128,256]{2,1,0:T(8,128)(2,1)S(1)}, bf16[2,128,256]{2,1,0:T(8,128)(2,1)S(1)}, u32[]{:S(2)}, u32[]{:S(2)}) collective-permute-start(bf16[2,128,256]{2,1,0:T(8,128)(2,1)S(1)} %pad_maximum_fusion.3), channel_id=1, source_target_pairs={{0,8},{8,0},{1,9},{9,1},{2,10},{10,2},{3,11},{11,3},{4,12},{12,4},... | collective-permute-start | bytes 393224 | tf_op jit(solution)/shard_map/ppermute | solution.py:16
  52.4 0.8 copy.56
  53.5 5.2 %collective-permute-done.4 = bf16[2,128,256]{2,1,0:T(8,128)(2,1)S(1)} collective-permute-done((bf16[2,128,256]{2,1,0:T(8,128)(2,1)S(1)}, bf16[2,128,256]{2,1,0:T(8,128)(2,1)S(1)}, u32[]{:S(2)}, u32[]{:S(2)}) %collective-permute-start.4) | collective-permute-done | bytes 131104 | tf_op jit(solution)/shard_map/ppermute | solution.py:16
  58.9 0.2 fusion.123
  59.1 0.2 fusion.116
  59.3 0.2 fusion.122
  59.5 0.2 fusion.40
  59.7 0.2 fusion.39
  59.9 1.9 %collective-permute-start.5 = (bf16[2,128,256]{2,1,0:T(8,128)(2,1)S(1)}, bf16[2,128,256]{2,1,0:T(8,128)(2,1)S(1)}, u32[]{:S(2)}, u32[]{:S(2)}) collective-permute-start(bf16[2,128,256]{2,1,0:T(8,128)(2,1)S(1)} %pad_maximum_fusion.4), channel_id=1, source_target_pairs={{0,4},{4,0},{1,5},{5,1},{2,6},{6,2},{3,7},{7,3},{8,12},{12,8},{9,1... | collective-permute-start | bytes 393224 | tf_op jit(solution)/shard_map/ppermute | solution.py:16
  62.0 0.2 fusion.7
  62.3 5.8 %collective-permute-done.5 = bf16[2,128,256]{2,1,0:T(8,128)(2,1)S(1)} collective-permute-done((bf16[2,128,256]{2,1,0:T(8,128)(2,1)S(1)}, bf16[2,128,256]{2,1,0:T(8,128)(2,1)S(1)}, u32[]{:S(2)}, u32[]{:S(2)}) %collective-permute-start.5) | collective-permute-done | bytes 131104 | tf_op jit(solution)/shard_map/ppermute | solution.py:16
  68.3 0.2 fusion.121
  68.5 0.2 fusion.114
  68.7 0.2 fusion.120
  68.9 0.2 fusion.38
  69.1 0.2 fusion.37
  69.3 4.3 %collective-permute-start.6 = (bf16[2,128,256]{2,1,0:T(8,128)(2,1)S(1)}, bf16[2,128,256]{2,1,0:T(8,128)(2,1)S(1)}, u32[]{:S(2)}, u32[]{:S(2)}) collective-permute-start(bf16[2,128,256]{2,1,0:T(8,128)(2,1)S(1)} %pad_maximum_fusion.5), channel_id=1, source_target_pairs={{0,2},{2,0},{1,3},{3,1},{4,6},{6,4},{5,7},{7,5},{8,10},{10,8},{9,1... | collective-permute-start | bytes 393224 | tf_op jit(solution)/shard_map/ppermute | solution.py:16
  73.9 0.2 fusion.5
  74.1 2.5 %collective-permute-done.6 = bf16[2,128,256]{2,1,0:T(8,128)(2,1)S(1)} collective-permute-done((bf16[2,128,256]{2,1,0:T(8,128)(2,1)S(1)}, bf16[2,128,256]{2,1,0:T(8,128)(2,1)S(1)}, u32[]{:S(2)}, u32[]{:S(2)}) %collective-permute-start.6) | collective-permute-done | bytes 131104 | tf_op jit(solution)/shard_map/ppermute | solution.py:16
  76.9 0.2 fusion.119
  77.1 0.2 fusion.112
  77.3 0.2 fusion.118
  77.5 0.2 fusion.36
  77.7 0.2 fusion.35
  77.9 1.9 %collective-permute-start.7 = (bf16[2,128,256]{2,1,0:T(8,128)(2,1)S(1)}, bf16[2,128,256]{2,1,0:T(8,128)(2,1)S(1)}, u32[]{:S(2)}, u32[]{:S(2)}) collective-permute-start(bf16[2,128,256]{2,1,0:T(8,128)(2,1)S(1)} %pad_maximum_fusion.6), channel_id=1, source_target_pairs={{0,1},{1,0},{2,3},{3,2},{4,5},{5,4},{6,7},{7,6},{8,9},{9,8},{10,11... | collective-permute-start | bytes 393224 | tf_op jit(solution)/shard_map/ppermute | solution.py:16
  80.0 0.2 fusion.3
  80.2 0.9 collective-permute-done.7
  81.3 81.0 %all-reduce = (f32[128]{0:T(128)S(1)}, f32[128]{0:T(128)S(1)}) all-reduce(f32[128]{0:T(128)S(1)} %get-tuple-element.7, f32[128]{0:T(128)S(1)} %get-tuple-element.6), channel_id=1, replica_groups=mesh['freq'=32,'bfly'=16] {'freq'}, use_global_device_ids=true, to_apply=%region_1.0 | all-reduce | flops 256 | bytes 2048 | tf_op jit(solution)/shard_map/psum | solution.py:91
  162.3 0.5 rsqrt_multiply_fusion
  (105 shorter events, 9.1 us)
Async XLA Ops:
  0.6 3.0 %copy-start.5 = (s32[4,2,2,2]{0,3,2,1:T(2,128)S(1)}, s32[4,2,2,2]{0,3,2,1:T(2,128)}, u32[]{:S(2)}) copy-start(s32[4,2,2,2]{0,3,2,1:T(2,128)} %param.15) | copy-start | bytes 388
  1.7 7.4 %collective-permute-start = (bf16[2,128,256]{2,1,0:T(8,128)(2,1)S(1)}, bf16[2,128,256]{2,1,0:T(8,128)(2,1)S(1)}, u32[]{:S(2)}, u32[]{:S(2)}) collective-permute-start(bf16[2,128,256]{2,1,0:T(8,128)(2,1)S(1)} %multiply_convert_fusion), channel_id=1, source_target_pairs={{0,1},{1,0},{2,3},{3,2},{4,5},{5,4},{6,7},{7,6},{8,9},{9,8},{10,11... | collective-permute-start | bytes 393224 | tf_op jit(solution)/shard_map/ppermute | solution.py:16
  4.0 1.0 copy-start.1
  5.1 1.0 copy-start.2
  5.3 0.7 copy-start.4
  6.1 0.9 copy-start
  7.9 0.9 copy-start.3
  10.1 7.8 %collective-permute-start.1 = (bf16[2,128,256]{2,1,0:T(8,128)(2,1)S(1)}, bf16[2,128,256]{2,1,0:T(8,128)(2,1)S(1)}, u32[]{:S(2)}, u32[]{:S(2)}) collective-permute-start(bf16[2,128,256]{2,1,0:T(8,128)(2,1)S(1)} %pad_maximum_fusion), channel_id=1, source_target_pairs={{0,2},{2,0},{1,3},{3,1},{4,6},{6,4},{5,7},{7,5},{8,10},{10,8},{9,1... | collective-permute-start | bytes 393224 | tf_op jit(solution)/shard_map/ppermute | solution.py:16
  18.9 12.7 %collective-permute-start.2 = (bf16[2,128,256]{2,1,0:T(8,128)(2,1)S(1)}, bf16[2,128,256]{2,1,0:T(8,128)(2,1)S(1)}, u32[]{:S(2)}, u32[]{:S(2)}) collective-permute-start(bf16[2,128,256]{2,1,0:T(8,128)(2,1)S(1)} %pad_maximum_fusion.1), channel_id=1, source_target_pairs={{0,4},{4,0},{1,5},{5,1},{2,6},{6,2},{3,7},{7,3},{8,12},{12,8},{9,1... | collective-permute-start | bytes 393224 | tf_op jit(solution)/shard_map/ppermute | solution.py:16
  32.6 11.4 %collective-permute-start.3 = (bf16[2,128,256]{2,1,0:T(8,128)(2,1)S(1)}, bf16[2,128,256]{2,1,0:T(8,128)(2,1)S(1)}, u32[]{:S(2)}, u32[]{:S(2)}) collective-permute-start(bf16[2,128,256]{2,1,0:T(8,128)(2,1)S(1)} %pad_maximum_fusion.2), channel_id=1, source_target_pairs={{0,8},{8,0},{1,9},{9,1},{2,10},{10,2},{3,11},{11,3},{4,12},{12,4},... | collective-permute-start | bytes 393224 | tf_op jit(solution)/shard_map/ppermute | solution.py:16
  44.7 0.7 copy-start.6
  47.1 11.5 %collective-permute-start.4 = (bf16[2,128,256]{2,1,0:T(8,128)(2,1)S(1)}, bf16[2,128,256]{2,1,0:T(8,128)(2,1)S(1)}, u32[]{:S(2)}, u32[]{:S(2)}) collective-permute-start(bf16[2,128,256]{2,1,0:T(8,128)(2,1)S(1)} %pad_maximum_fusion.3), channel_id=1, source_target_pairs={{0,8},{8,0},{1,9},{9,1},{2,10},{10,2},{3,11},{11,3},{4,12},{12,4},... | collective-permute-start | bytes 393224 | tf_op jit(solution)/shard_map/ppermute | solution.py:16
  59.9 8.1 %collective-permute-start.5 = (bf16[2,128,256]{2,1,0:T(8,128)(2,1)S(1)}, bf16[2,128,256]{2,1,0:T(8,128)(2,1)S(1)}, u32[]{:S(2)}, u32[]{:S(2)}) collective-permute-start(bf16[2,128,256]{2,1,0:T(8,128)(2,1)S(1)} %pad_maximum_fusion.4), channel_id=1, source_target_pairs={{0,4},{4,0},{1,5},{5,1},{2,6},{6,2},{3,7},{7,3},{8,12},{12,8},{9,1... | collective-permute-start | bytes 393224 | tf_op jit(solution)/shard_map/ppermute | solution.py:16
  69.3 7.3 %collective-permute-start.6 = (bf16[2,128,256]{2,1,0:T(8,128)(2,1)S(1)}, bf16[2,128,256]{2,1,0:T(8,128)(2,1)S(1)}, u32[]{:S(2)}, u32[]{:S(2)}) collective-permute-start(bf16[2,128,256]{2,1,0:T(8,128)(2,1)S(1)} %pad_maximum_fusion.5), channel_id=1, source_target_pairs={{0,2},{2,0},{1,3},{3,1},{4,6},{6,4},{5,7},{7,5},{8,10},{10,8},{9,1... | collective-permute-start | bytes 393224 | tf_op jit(solution)/shard_map/ppermute | solution.py:16
  77.9 3.2 %collective-permute-start.7 = (bf16[2,128,256]{2,1,0:T(8,128)(2,1)S(1)}, bf16[2,128,256]{2,1,0:T(8,128)(2,1)S(1)}, u32[]{:S(2)}, u32[]{:S(2)}) collective-permute-start(bf16[2,128,256]{2,1,0:T(8,128)(2,1)S(1)} %pad_maximum_fusion.6), channel_id=1, source_target_pairs={{0,1},{1,0},{2,3},{3,2},{4,5},{5,4},{6,7},{7,6},{8,9},{9,8},{10,11... | collective-permute-start | bytes 393224 | tf_op jit(solution)/shard_map/ppermute | solution.py:16
where the time goes:
time: 163 us
  blocking collectives  81 us (50%)
  waiting for transfers between devices  33.6 us (21%)
  starting transfers between devices  26.9 us (17%)
  matrix products  11.5 us (7%)
  local copies, waits for them, and re-layouts  6.08 us (4%)
  other arithmetic  2.42 us (1%)
    psum x1, blocking collectives, local(): lax.psum((gradient_part, illumination), 'freq')  81 us
    ppermute x8, waiting for transfers between devices, swapped(): return lax.ppermute(block, axis, route)  33.6 us
    ppermute x8, starting transfers between devices, swapped(): return lax.ppermute(block, axis, route)  26.9 us
    dot_general x32, matrix products, transposed(): lax.dot_general(blocks, values, contract, preferred_element_type=jnp.floa...  6.36 us
    unnamed x16, local copies, waits for them, and re-layouts  4.56 us
  transfers between devices with their start and end apart: 8, of which 7 were waited for; matrix products, arithmetic and copies ran while one was open for 3% of the time, Pallas kernels for 0%

commit v1 on v0

v1 whole, which is shorter than its diff:
```python
import jax
import jax.numpy as jnp
from jax import lax
from jax.sharding import PartitionSpec as P

epsilon = 1e-05


def swapped(block, stride):
    count = lax.axis_size("bfly")
    route = [(place, place ^ 1 << stride) for place in range(count)]
    return lax.ppermute(block, "bfly", route)


def stacked(blocks):
    real, imag = blocks[:, 0], blocks[:, 1]
    top = jnp.concatenate([real, -imag], axis=-1)
    bottom = jnp.concatenate([imag, real], axis=-1)
    return jnp.concatenate([top, bottom], axis=-2)


def mul(matrix, values):
    return jnp.dot(matrix, values, preferred_element_type=jnp.float32)


def mul_t(matrix, values):
    contract = (((0,), (0,)), ((), ()))
    return lax.dot_general(matrix, values, contract, preferred_element_type=jnp.float32)


def turn(values, cosine, sine):
    rows = values.shape[0] // 2
    real, imag = values[:rows], values[rows:]
    return jnp.concatenate([cosine * real - sine * imag, sine * real + cosine * imag])


def turn_back(values, cosine, sine):
    rows = values.shape[0] // 2
    real, imag = values[:rows], values[rows:]
    return jnp.concatenate([cosine * real + sine * imag, cosine * imag - sine * real])


def row_dot(left, right):
    rows = left.shape[0] // 2
    product = left * right
    return jnp.sum(product[:rows] + product[rows:], axis=-1)


def local(sources, observed, receivers, model, phases, near_blocks, far_blocks, pattern):
    rows, columns = sources.shape[1:]
    levels = near_blocks.shape[0]
    rank = rows // pattern.shape[-1]
    repeats = columns // phases.shape[-1]
    bf16 = jnp.bfloat16

    sources = sources.reshape(2 * rows, columns)
    partner_sources = swapped(sources, 0)
    partner_model = swapped(model, 0)

    mask = jnp.repeat(jnp.repeat(pattern, rank, axis=2), rank, axis=3).astype(bf16)
    near = stacked(near_blocks * mask[:, 0:1])
    far = stacked(far_blocks * mask[:, 1:2])
    cosine = jnp.repeat(jnp.cos(phases), repeats, axis=-1)
    sine = jnp.repeat(jnp.sin(phases), repeats, axis=-1)

    selector = (receivers[:, None] == jnp.arange(rows, dtype=jnp.int32)[None, :]).astype(bf16)
    counts = jnp.sum(selector.astype(jnp.float32), axis=0)
    counts = jnp.concatenate([counts, counts])[:, None]
    spread = jnp.concatenate([mul_t(selector, observed[0]), mul_t(selector, observed[1])])
    data = turn_back(spread, cosine[-1], sine[-1])

    def start_field(values, factor):
        factor = jnp.concatenate([factor, factor])[:, None]
        return (factor * values.astype(jnp.float32)).astype(bf16)

    field = start_field(sources, model)
    partner_field = start_field(partner_sources, partner_model)
    for level in range(levels):
        if level:
            partner_field = swapped(field, level)
        mixed = mul(near[level], field) + mul(far[level], partner_field)
        if level < levels - 1:
            field = turn(mixed, cosine[level], sine[level]).astype(bf16)

    turned = (counts * mixed - data).astype(bf16)
    for level in reversed(range(1, levels)):
        far_term = swapped(mul_t(far[level], turned).astype(bf16), level)
        adjoint = mul_t(near[level], turned) + far_term.astype(jnp.float32)
        turned = turn_back(adjoint, cosine[level - 1], sine[level - 1]).astype(bf16)
    wide = sources.astype(jnp.float32)
    partial = row_dot(wide, mul_t(near[0], turned))
    partner_partial = row_dot(partner_sources.astype(jnp.float32), mul_t(far[0], turned))

    last = turn(mixed, cosine[-1], sine[-1]).astype(bf16)
    picked = jnp.stack([mul(selector, last[:rows]), mul(selector, last[rows:])])
    residual = picked - observed.astype(jnp.float32)

    illumination = row_dot(wide, wide)
    own = jnp.concatenate([partial, illumination])
    other = jnp.concatenate([partner_partial, jnp.zeros_like(illumination)])
    n_bfly, n_freq = lax.axis_size("bfly"), lax.axis_size("freq")
    first = lax.axis_index("bfly") % 2 == 0
    pair = jnp.stack([jnp.where(first, own, other), jnp.where(first, other, own)])
    terms = jnp.broadcast_to(pair[None], (n_freq, 2, 2 * rows)).reshape(2 * n_freq, 2 * rows)
    groups = [
        [f * n_bfly + high + low for f in range(n_freq) for low in range(2)]
        for high in range(0, n_bfly, 2)
    ]
    terms = lax.all_to_all(terms, ("freq", "bfly"), 0, 0, axis_index_groups=groups)
    total = jnp.sum(terms, axis=0)
    gradient = total[:rows] / jnp.sqrt(total[rows:] + epsilon)
    return (gradient, residual)


def solution(mesh):
    return jax.shard_map(
        local,
        mesh=mesh,
        in_specs=(
            P(None, "bfly", "freq"),
            P(None, "bfly", "freq"),
            P("bfly"),
            P("bfly"),
            P(None, "bfly", "freq"),
            P(None, None, "bfly", None),
            P(None, None, "bfly", None),
            P(None, None, "bfly", None),
        ),
        out_specs=(P("bfly"), P(None, "bfly", "freq")),
        check_vma=False,
    )
```

time: 163 us -> 102 us (0.63)
  the two profiles are of different devices: /device:TPU:24 before, /device:TPU:1 now
where the time goes in v1:
time: 102 us; the launch traced here: 101 us
  waiting for transfers between devices  46.8 us (46%)
  starting transfers between devices  39.4 us (39%)
  local copies, waits for them, and re-layouts  7.06 us (7%)
  matrix products  4.31 us (4%)
  other arithmetic  2.24 us (2%)
  between operations  1.29 us (1%)
    ppermute x8, waiting for transfers between devices, swapped(): return lax.ppermute(block, 'bfly', route)  37.4 us
    ppermute x8, starting transfers between devices, swapped(): return lax.ppermute(block, 'bfly', route)  22.2 us
    all_to_all x1, starting transfers between devices, local(): lax.all_to_all(terms, ('freq', 'bfly'), 0, 0, axis_index_groups=groups)  17.1 us
    all_to_all x1, waiting for transfers between devices, local(): lax.all_to_all(terms, ('freq', 'bfly'), 0, 0, axis_index_groups=groups)  9.36 us
    unnamed x16, local copies, waits for them, and re-layouts  3.75 us
    dot_general x10, matrix products, mul_t(): lax.dot_general(matrix, values, contract, preferred_element_type=jnp.floa...  2.37 us
  transfers between devices with their start and end apart: 9, of which 7 were waited for; matrix products, arithmetic and copies ran while one was open for 4% of the time, Pallas kernels for 0%

profile of v1, /device:TPU:1, one launch (start us, length us, event | category | flops | bytes accessed | tf_op | source)
XLA Modules:
  0.0 101.1 jit_solution(16241945202079784696)
XLA Ops:
  0.6 1.0 %copy.136 = bf16[256,256]{0,1:T(8,128)(2,1)S(1)} copy(bf16[256,256]{1,0:T(8,128)(2,1)} %bitcast.115) | data formatting | bytes 262144 | tf_op jit(solution)/shard_map/reshape | solution.py:56
  1.7 8.8 %collective-permute-start.1 = (bf16[256,256]{0,1:T(8,128)(2,1)S(1)}, bf16[256,256]{0,1:T(8,128)(2,1)S(1)}, u32[]{:S(2)}, u32[]{:S(2)}) collective-permute-start(bf16[256,256]{0,1:T(8,128)(2,1)S(1)} %copy.136), channel_id=1, source_target_pairs={{0,1},{1,0},{2,3},{3,2},{4,5},{5,4},{6,7},{7,6},{8,9},{9,8},{10,11... | collective-permute-start | bytes 393224 | tf_op jit(solution)/shard_map/ppermute | solution.py:12
  10.5 1.9 %collective-permute-start = (f32[128]{0:T(128)S(1)}, f32[128]{0:T(128)S(1)}, u32[]{:S(2)}, u32[]{:S(2)}) collective-permute-start(f32[128]{0:T(128)S(1)} %copy-done.7), channel_id=1, source_target_pairs={{0,1},{1,0},{2,3},{3,2},{4,5},{5,4},{6,7},{7,6},{8,9},{9,8},{10,11... | collective-permute-start | bytes 1544 | tf_op jit(solution)/shard_map/ppermute | solution.py:12
  12.8 0.1 copy.100
  12.9 0.8 copy-done.2
  13.9 0.1 copy.102
  14.0 0.8 copy-done.3
  14.9 0.9 copy-done.1
  15.8 0.6 copy-done.5
  16.7 0.5 copy-done.4
  17.4 0.2 copy-done
  17.5 0.3 fusion.16
  17.9 0.2 fusion.7
  18.1 0.3 multiply_add_fusion
  19.2 0.2 convolution_add_fusion.3
  19.5 1.9 %collective-permute-start.2 = (bf16[256,256]{1,0:T(8,128)(2,1)S(1)}, bf16[256,256]{1,0:T(8,128)(2,1)S(1)}, u32[]{:S(2)}, u32[]{:S(2)}) collective-permute-start(bf16[256,256]{1,0:T(8,128)(2,1)S(1)} %pad_maximum_fusion), channel_id=1, source_target_pairs={{0,2},{1,3},{2,0},{3,1},{4,6},{5,7},{6,4},{7,5},{8,10},{9,11},{10,... | collective-permute-start | bytes 393224 | tf_op jit(solution)/shard_map/ppermute | solution.py:12
  21.4 0.2 fusion.9
  21.6 4.3 %collective-permute-done.2 = bf16[256,256]{1,0:T(8,128)(2,1)S(1)} collective-permute-done((bf16[256,256]{1,0:T(8,128)(2,1)S(1)}, bf16[256,256]{1,0:T(8,128)(2,1)S(1)}, u32[]{:S(2)}, u32[]{:S(2)}) %collective-permute-start.2) | collective-permute-done | bytes 131104 | tf_op jit(solution)/shard_map/ppermute | solution.py:12
  26.0 0.2 convolution_add_fusion.2
  26.2 1.9 %collective-permute-start.3 = (bf16[256,256]{1,0:T(8,128)(2,1)S(1)}, bf16[256,256]{1,0:T(8,128)(2,1)S(1)}, u32[]{:S(2)}, u32[]{:S(2)}) collective-permute-start(bf16[256,256]{1,0:T(8,128)(2,1)S(1)} %pad_maximum_fusion.1), channel_id=1, source_target_pairs={{0,4},{1,5},{2,6},{3,7},{4,0},{5,1},{6,2},{7,3},{8,12},{9,13},{10,... | collective-permute-start | bytes 393224 | tf_op jit(solution)/shard_map/ppermute | solution.py:12
  28.1 0.2 fusion.11
  28.3 8.8 %collective-permute-done.3 = bf16[256,256]{1,0:T(8,128)(2,1)S(1)} collective-permute-done((bf16[256,256]{1,0:T(8,128)(2,1)S(1)}, bf16[256,256]{1,0:T(8,128)(2,1)S(1)}, u32[]{:S(2)}, u32[]{:S(2)}) %collective-permute-start.3) | collective-permute-done | bytes 131104 | tf_op jit(solution)/shard_map/ppermute | solution.py:12
  37.2 0.2 convolution_add_fusion.1
  37.4 1.9 %collective-permute-start.4 = (bf16[256,256]{1,0:T(8,128)(2,1)S(1)}, bf16[256,256]{1,0:T(8,128)(2,1)S(1)}, u32[]{:S(2)}, u32[]{:S(2)}) collective-permute-start(bf16[256,256]{1,0:T(8,128)(2,1)S(1)} %pad_maximum_fusion.2), channel_id=1, source_target_pairs={{0,8},{1,9},{2,10},{3,11},{4,12},{5,13},{6,14},{7,15},{8,0},{9,1},... | collective-permute-start | bytes 393224 | tf_op jit(solution)/shard_map/ppermute | solution.py:12
  39.4 0.2 fusion.13
  39.6 8.2 %collective-permute-done.4 = bf16[256,256]{1,0:T(8,128)(2,1)S(1)} collective-permute-done((bf16[256,256]{1,0:T(8,128)(2,1)S(1)}, bf16[256,256]{1,0:T(8,128)(2,1)S(1)}, u32[]{:S(2)}, u32[]{:S(2)}) %collective-permute-start.4) | collective-permute-done | bytes 131104 | tf_op jit(solution)/shard_map/ppermute | solution.py:12
  47.8 0.2 fusion.1
  48.0 0.2 convolution_convert_fusion.2
  48.2 1.9 %collective-permute-start.5 = (bf16[256,256]{1,0:T(8,128)(2,1)S(1)}, bf16[256,256]{1,0:T(8,128)(2,1)S(1)}, u32[]{:S(2)}, u32[]{:S(2)}) collective-permute-start(bf16[256,256]{1,0:T(8,128)(2,1)S(1)} %convolution_convert_fusion.2), channel_id=1, source_target_pairs={{0,8},{1,9},{2,10},{3,11},{4,12},{5,13},{6,14},{7,15},{8,0},{9,1},... | collective-permute-start | bytes 393224 | tf_op jit(solution)/shard_map/ppermute | solution.py:12
  50.1 8.1 %collective-permute-done.5 = bf16[256,256]{1,0:T(8,128)(2,1)S(1)} collective-permute-done((bf16[256,256]{1,0:T(8,128)(2,1)S(1)}, bf16[256,256]{1,0:T(8,128)(2,1)S(1)}, u32[]{:S(2)}, u32[]{:S(2)}) %collective-permute-start.5) | collective-permute-done | bytes 131104 | tf_op jit(solution)/shard_map/ppermute | solution.py:12
  58.2 0.2 convert_add_fusion.2
  58.5 0.2 convolution_convert_fusion.1
  58.7 1.9 %collective-permute-start.6 = (bf16[256,256]{1,0:T(8,128)(2,1)S(1)}, bf16[256,256]{1,0:T(8,128)(2,1)S(1)}, u32[]{:S(2)}, u32[]{:S(2)}) collective-permute-start(bf16[256,256]{1,0:T(8,128)(2,1)S(1)} %convolution_convert_fusion.1), channel_id=1, source_target_pairs={{0,4},{1,5},{2,6},{3,7},{4,0},{5,1},{6,2},{7,3},{8,12},{9,13},{10,... | collective-permute-start | bytes 393224 | tf_op jit(solution)/shard_map/ppermute | solution.py:12
  60.7 4.6 %collective-permute-done.6 = bf16[256,256]{1,0:T(8,128)(2,1)S(1)} collective-permute-done((bf16[256,256]{1,0:T(8,128)(2,1)S(1)}, bf16[256,256]{1,0:T(8,128)(2,1)S(1)}, u32[]{:S(2)}, u32[]{:S(2)}) %collective-permute-start.6) | collective-permute-done | bytes 131104 | tf_op jit(solution)/shard_map/ppermute | solution.py:12
  65.3 0.2 convert_add_fusion.1
  65.6 0.2 convolution_convert_fusion
  65.8 1.9 %collective-permute-start.7 = (bf16[256,256]{1,0:T(8,128)(2,1)S(1)}, bf16[256,256]{1,0:T(8,128)(2,1)S(1)}, u32[]{:S(2)}, u32[]{:S(2)}) collective-permute-start(bf16[256,256]{1,0:T(8,128)(2,1)S(1)} %convolution_convert_fusion), channel_id=1, source_target_pairs={{0,2},{1,3},{2,0},{3,1},{4,6},{5,7},{6,4},{7,5},{8,10},{9,11},{10,... | collective-permute-start | bytes 393224 | tf_op jit(solution)/shard_map/ppermute | solution.py:12
  67.8 0.2 convolution_bitcast_fusion
  68.0 0.2 convolution_bitcast_fusion.1
  68.2 3.4 %collective-permute-done.7 = bf16[256,256]{1,0:T(8,128)(2,1)S(1)} collective-permute-done((bf16[256,256]{1,0:T(8,128)(2,1)S(1)}, bf16[256,256]{1,0:T(8,128)(2,1)S(1)}, u32[]{:S(2)}, u32[]{:S(2)}) %collective-permute-start.7) | collective-permute-done | bytes 131104 | tf_op jit(solution)/shard_map/ppermute | solution.py:12
  71.6 0.2 convert_add_fusion
  71.8 0.2 convolution_multiply_fusion.1
  72.1 0.2 convolution_multiply_fusion
  72.5 0.7 all_to_all.6
  73.2 17.1 %all-to-all-start = ((f32[64,1,256]{2,1,0:T(1,128)}), f32[64,1,256]{2,1,0:T(1,128)S(1)}, u32[]{:S(2)}, u32[]{:S(2)}) async-start(f32[64,1,256]{2,1,0:T(1,128)} %all_to_all.6), calls=%async_computation | async-start | bytes 131072 | tf_op jit(solution)/shard_map/all_to_all | solution.py:109
  90.3 0.7 maximum_subtract_fusion.1
  91.1 9.4 %all-to-all-done = f32[64,1,256]{2,1,0:T(1,128)S(1)} async-done(((f32[64,1,256]{2,1,0:T(1,128)}), f32[64,1,256]{2,1,0:T(1,128)S(1)}, u32[]{:S(2)}, u32[]{:S(2)}) %all-to-all-start) | async-done | bytes 65568 | tf_op jit(solution)/shard_map/all_to_all | solution.py:109
  100.5 0.5 rsqrt_multiply_fusion
  (66 shorter events, 2.3 us)
Async XLA Ops:
  0.6 9.8 %copy-start.7 = (f32[128]{0:T(128)S(1)}, f32[128]{0:T(128)}, u32[]{:S(2)}) copy-start(f32[128]{0:T(128)} %param.11) | copy-start | bytes 1540
  0.6 11.8 %copy-start.6 = (s32[4,2,2,2]{0,3,2,1:T(2,128)S(1)}, s32[4,2,2,2]{0,3,2,1:T(2,128)}, u32[]{:S(2)}) copy-start(s32[4,2,2,2]{0,3,2,1:T(2,128)} %param.15) | copy-start | bytes 388
  1.7 17.5 %collective-permute-start.1 = (bf16[256,256]{0,1:T(8,128)(2,1)S(1)}, bf16[256,256]{0,1:T(8,128)(2,1)S(1)}, u32[]{:S(2)}, u32[]{:S(2)}) collective-permute-start(bf16[256,256]{0,1:T(8,128)(2,1)S(1)} %copy.136), channel_id=1, source_target_pairs={{0,1},{1,0},{2,3},{3,2},{4,5},{5,4},{6,7},{7,6},{8,9},{9,8},{10,11... | collective-permute-start | bytes 393224 | tf_op jit(solution)/shard_map/ppermute | solution.py:12
  10.5 8.7 %collective-permute-start = (f32[128]{0:T(128)S(1)}, f32[128]{0:T(128)S(1)}, u32[]{:S(2)}, u32[]{:S(2)}) collective-permute-start(f32[128]{0:T(128)S(1)} %copy-done.7), channel_id=1, source_target_pairs={{0,1},{1,0},{2,3},{3,2},{4,5},{5,4},{6,7},{7,6},{8,9},{9,8},{10,11... | collective-permute-start | bytes 1544 | tf_op jit(solution)/shard_map/ppermute | solution.py:12
  12.8 1.0 copy-start.2
  13.8 1.0 copy-start.3
  14.8 0.9 copy-start.1
  15.7 0.7 copy-start.5
  16.6 0.7 copy-start.4
  16.6 0.9 copy-start
  19.5 6.5 %collective-permute-start.2 = (bf16[256,256]{1,0:T(8,128)(2,1)S(1)}, bf16[256,256]{1,0:T(8,128)(2,1)S(1)}, u32[]{:S(2)}, u32[]{:S(2)}) collective-permute-start(bf16[256,256]{1,0:T(8,128)(2,1)S(1)} %pad_maximum_fusion), channel_id=1, source_target_pairs={{0,2},{1,3},{2,0},{3,1},{4,6},{5,7},{6,4},{7,5},{8,10},{9,11},{10,... | collective-permute-start | bytes 393224 | tf_op jit(solution)/shard_map/ppermute | solution.py:12
  26.2 11.0 %collective-permute-start.3 = (bf16[256,256]{1,0:T(8,128)(2,1)S(1)}, bf16[256,256]{1,0:T(8,128)(2,1)S(1)}, u32[]{:S(2)}, u32[]{:S(2)}) collective-permute-start(bf16[256,256]{1,0:T(8,128)(2,1)S(1)} %pad_maximum_fusion.1), channel_id=1, source_target_pairs={{0,4},{1,5},{2,6},{3,7},{4,0},{5,1},{6,2},{7,3},{8,12},{9,13},{10,... | collective-permute-start | bytes 393224 | tf_op jit(solution)/shard_map/ppermute | solution.py:12
  37.4 10.3 %collective-permute-start.4 = (bf16[256,256]{1,0:T(8,128)(2,1)S(1)}, bf16[256,256]{1,0:T(8,128)(2,1)S(1)}, u32[]{:S(2)}, u32[]{:S(2)}) collective-permute-start(bf16[256,256]{1,0:T(8,128)(2,1)S(1)} %pad_maximum_fusion.2), channel_id=1, source_target_pairs={{0,8},{1,9},{2,10},{3,11},{4,12},{5,13},{6,14},{7,15},{8,0},{9,1},... | collective-permute-start | bytes 393224 | tf_op jit(solution)/shard_map/ppermute | solution.py:12
  48.2 10.0 %collective-permute-start.5 = (bf16[256,256]{1,0:T(8,128)(2,1)S(1)}, bf16[256,256]{1,0:T(8,128)(2,1)S(1)}, u32[]{:S(2)}, u32[]{:S(2)}) collective-permute-start(bf16[256,256]{1,0:T(8,128)(2,1)S(1)} %convolution_convert_fusion.2), channel_id=1, source_target_pairs={{0,8},{1,9},{2,10},{3,11},{4,12},{5,13},{6,14},{7,15},{8,0},{9,1},... | collective-permute-start | bytes 393224 | tf_op jit(solution)/shard_map/ppermute | solution.py:12
  58.7 6.6 %collective-permute-start.6 = (bf16[256,256]{1,0:T(8,128)(2,1)S(1)}, bf16[256,256]{1,0:T(8,128)(2,1)S(1)}, u32[]{:S(2)}, u32[]{:S(2)}) collective-permute-start(bf16[256,256]{1,0:T(8,128)(2,1)S(1)} %convolution_convert_fusion.1), channel_id=1, source_target_pairs={{0,4},{1,5},{2,6},{3,7},{4,0},{5,1},{6,2},{7,3},{8,12},{9,13},{10,... | collective-permute-start | bytes 393224 | tf_op jit(solution)/shard_map/ppermute | solution.py:12
  65.8 5.7 %collective-permute-start.7 = (bf16[256,256]{1,0:T(8,128)(2,1)S(1)}, bf16[256,256]{1,0:T(8,128)(2,1)S(1)}, u32[]{:S(2)}, u32[]{:S(2)}) collective-permute-start(bf16[256,256]{1,0:T(8,128)(2,1)S(1)} %convolution_convert_fusion), channel_id=1, source_target_pairs={{0,2},{1,3},{2,0},{3,1},{4,6},{5,7},{6,4},{7,5},{8,10},{9,11},{10,... | collective-permute-start | bytes 393224 | tf_op jit(solution)/shard_map/ppermute | solution.py:12
  73.2 27.2 %all-to-all-start = ((f32[64,1,256]{2,1,0:T(1,128)}), f32[64,1,256]{2,1,0:T(1,128)S(1)}, u32[]{:S(2)}, u32[]{:S(2)}) async-start(f32[64,1,256]{2,1,0:T(1,128)} %all_to_all.6), calls=%async_computation | async-start | bytes 131072 | tf_op jit(solution)/shard_map/all_to_all | solution.py:109

commit v2 on v1

v2 whole, which is shorter than its diff:
```python
import jax
import jax.numpy as jnp
from jax import lax
from jax.experimental import pallas as pl
from jax.experimental.pallas import tpu as pltpu
from jax.sharding import PartitionSpec as P

epsilon = 1e-05
bf16, f32 = jnp.bfloat16, jnp.float32
VMEM = pl.BlockSpec(memory_space=pltpu.VMEM)
SMEM = pl.BlockSpec(memory_space=pltpu.SMEM)


def swapped(block, stride):
    count = lax.axis_size("bfly")
    route = [(place, place ^ 1 << stride) for place in range(count)]
    return lax.ppermute(block, "bfly", route)


def after(values, *done):
    return lax.optimization_barrier((values, *done))[0]


def stacked(block):
    real, imag = block[0], block[1]
    top = jnp.concatenate([real, -imag], axis=-1)
    bottom = jnp.concatenate([imag, real], axis=-1)
    return jnp.concatenate([top, bottom], axis=-2)


def mul(matrix, values):
    return jnp.dot(matrix, values, preferred_element_type=f32)


def mul_t(matrix, values):
    contract = (((0,), (0,)), ((), ()))
    return lax.dot_general(matrix, values, contract, preferred_element_type=f32)


def turn(values, cosine, sine):
    rows = values.shape[0] // 2
    real, imag = values[:rows], values[rows:]
    return jnp.concatenate([cosine * real - sine * imag, sine * real + cosine * imag])


def turn_back(values, cosine, sine):
    rows = values.shape[0] // 2
    real, imag = values[:rows], values[rows:]
    return jnp.concatenate([cosine * real + sine * imag, cosine * imag - sine * real])


def masked(blocks, pattern_ref, level, kind):
    rows = blocks.shape[-1]
    half = rows // 2

    def band(side):
        keep = [
            jnp.broadcast_to(pattern_ref[kind, side, part : part + 1, level : level + 1], (half, half))
            for part in range(2)
        ]
        return jnp.concatenate(keep, axis=1).astype(f32).astype(bf16)

    mask = jnp.concatenate([band(0), band(1)])
    return [blocks[part] * mask for part in range(2)]


def waves(angles, columns):
    count = angles.shape[0]
    both = jnp.concatenate([jnp.cos(angles), jnp.sin(angles)])
    place = lax.broadcasted_iota(jnp.int32, (2 * count, 2 * columns), 1) // (columns // count)
    pick = (place == lax.broadcasted_iota(jnp.int32, place.shape, 0)).astype(f32)
    contract = (((0,), (0,)), ((), ()))
    return lax.dot_general(
        both, pick, contract, precision=lax.Precision.HIGHEST, preferred_element_type=f32
    )


def first_field(sources_ref, model_ref, field_out):
    rows = model_ref.shape[-1]
    place = lax.broadcasted_iota(jnp.int32, (rows, rows), 0)
    diagonal = place == lax.broadcasted_iota(jnp.int32, (rows, rows), 1)
    factor = jnp.sum(jnp.where(diagonal, model_ref[...], 0.0), axis=1, keepdims=True)
    for part in range(2):
        field = factor * sources_ref[part].astype(f32)
        field_out[part * rows : (part + 1) * rows] = field.astype(bf16)


def first_maps(near_ref, far_ref, pattern_ref, phases_ref, near_out, far_out, waves_out):
    near_out[...] = stacked(masked(near_ref[0], pattern_ref, 0, 0))
    far_out[...] = stacked(masked(far_ref[0], pattern_ref, 0, 1))
    waves_out[...] = waves(phases_ref[0], waves_out.shape[-1] // 2)


def later_maps(
    near_ref, far_ref, pattern_ref, phases_ref, observed_ref, receivers_ref,
    near_out, far_out, waves_out, select_out, counts_out, data_out,
):
    rows, columns = observed_ref.shape[1:]
    for level in range(1, 4):
        near_out[level - 1] = stacked(masked(near_ref[level], pattern_ref, level, 0))
        far_out[level - 1] = stacked(masked(far_ref[level], pattern_ref, level, 1))
        waves_out[level - 1] = waves(phases_ref[level], columns)
    select = receivers_ref[...] == lax.broadcasted_iota(jnp.int32, (rows, rows), 0)
    select = select.astype(f32)
    counts = jnp.broadcast_to(jnp.sum(select, axis=1, keepdims=True), (rows, columns))
    counts_out[...] = jnp.concatenate([counts, counts])
    select = select.astype(bf16)
    select_out[...] = select
    spread = jnp.concatenate([mul(select, observed_ref[0]), mul(select, observed_ref[1])])
    cosine, sine = waves_out[2, :, :columns], waves_out[2, :, columns:]
    data_out[...] = turn_back(spread, cosine, sine)


def last_terms(turned_ref, near_ref, far_ref, sources_ref, partner_ref, first_ref, terms_out):
    rows = sources_ref.shape[0] // 2
    wide = sources_ref[...].astype(f32)
    partner = partner_ref[...].astype(f32)
    turned = turned_ref[...]

    def row_sums(product):
        total = product[:rows] + product[rows:]
        return jnp.sum(total.T, axis=0, keepdims=True)

    own = row_sums(wide * mul_t(near_ref[...], turned))
    other = row_sums(partner * mul_t(far_ref[...], turned))
    own = jnp.concatenate([own, row_sums(wide * wide)], axis=1)
    other = jnp.concatenate([other, jnp.zeros_like(other)], axis=1)
    first = first_ref[0] == 0
    even, odd = jnp.where(first, own, other), jnp.where(first, other, own)
    n_freq = terms_out.shape[0] // 2
    pair = jnp.concatenate([even, odd])
    terms_out[...] = jnp.concatenate([pair[None]] * n_freq).reshape(terms_out.shape)


def local(sources, observed, receivers, model, phases, near_blocks, far_blocks, pattern):
    rows, columns = sources.shape[1:]
    shape = pltpu.VMEM
    phases = phases.transpose(0, 2, 1)
    pattern = pattern.transpose(1, 2, 3, 0)

    field = pl.pallas_call(
        first_field,
        out_shape=shape((2 * rows, columns), bf16),
        in_specs=[VMEM, VMEM],
        out_specs=VMEM,
        name="first_field",
    )(sources, model[None])
    partner = swapped(field, 0)
    blocks = pl.BlockSpec((1, 2, rows, rows), lambda step: (0, 0, 0, 0))
    angles = pl.BlockSpec((1, *phases.shape[1:]), lambda step: (0, 0, 0))
    near_0, far_0, waves_0 = pl.pallas_call(
        first_maps,
        out_shape=(
            shape((2 * rows, 2 * rows), bf16),
            shape((2 * rows, 2 * rows), bf16),
            shape((rows, 2 * columns), f32),
        ),
        grid=(1,),
        in_specs=[blocks, blocks, VMEM, angles],
        out_specs=(VMEM,) * 3,
        name="first_maps",
    )(near_blocks, far_blocks, pattern, phases)
    cosine_0, sine_0 = waves_0[:, :columns], waves_0[:, columns:]
    mixed = mul(near_0, field) + mul(far_0, partner)
    field = turn(mixed, cosine_0, sine_0).astype(bf16)

    partner = swapped(field, 1)
    near, far, wave, select, counts, data = pl.pallas_call(
        later_maps,
        out_shape=(
            shape((3, 2 * rows, 2 * rows), bf16),
            shape((3, 2 * rows, 2 * rows), bf16),
            shape((3, rows, 2 * columns), f32),
            shape((rows, rows), bf16),
            shape((2 * rows, columns), f32),
            shape((2 * rows, columns), f32),
        ),
        in_specs=[VMEM] * 6,
        out_specs=(VMEM,) * 6,
        name="later_maps",
    )(near_blocks, far_blocks, pattern, phases, observed, after(receivers, field)[None])
    near_1, near_2, near_3 = near
    far_1, far_2, far_3 = far
    (cosine_1, sine_1), (cosine_2, sine_2), (cosine_3, sine_3) = (
        (each[:, :columns], each[:, columns:]) for each in wave
    )
    mixed = mul(near_1, field) + mul(far_1, partner)
    field = turn(mixed, cosine_1, sine_1).astype(bf16)

    partner = swapped(field, 2)
    mixed = mul(near_2, field) + mul(far_2, partner)
    field = turn(mixed, cosine_2, sine_2).astype(bf16)

    partner = swapped(field, 3)
    sources = sources.reshape(2 * rows, columns)
    partner_sources = swapped(after(sources, field), 0)
    mixed = mul(near_3, field) + mul(far_3, partner)
    turned = (counts * mixed - data).astype(bf16)

    far_term = swapped(mul_t(far_3, turned).astype(bf16), 3)
    last = turn(mixed, cosine_3, sine_3).astype(bf16)
    picked = jnp.stack([mul_t(select, last[:rows]), mul_t(select, last[rows:])])
    residual = picked - observed.astype(f32)
    adjoint = mul_t(near_3, turned) + far_term.astype(f32)
    turned = turn_back(adjoint, cosine_2, sine_2).astype(bf16)

    far_term = swapped(mul_t(far_2, turned).astype(bf16), 2)
    adjoint = mul_t(near_2, turned) + far_term.astype(f32)
    turned = turn_back(adjoint, cosine_1, sine_1).astype(bf16)

    far_term = swapped(mul_t(far_1, turned).astype(bf16), 1)
    adjoint = mul_t(near_1, turned) + far_term.astype(f32)
    turned = turn_back(adjoint, cosine_0, sine_0).astype(bf16)

    n_bfly, n_freq = lax.axis_size("bfly"), lax.axis_size("freq")
    terms = pl.pallas_call(
        last_terms,
        out_shape=jax.ShapeDtypeStruct((2 * n_freq, 1, 2 * rows), f32),
        in_specs=[VMEM] * 5 + [SMEM],
        out_specs=VMEM,
        name="last_terms",
    )(
        *(
            pltpu.with_memory_space_constraint(each, pltpu.VMEM)
            for each in (turned, near_0, far_0, sources, partner_sources)
        ),
        (lax.axis_index("bfly") & 1)[None],
    )
    groups = [
        [f * n_bfly + high + low for f in range(n_freq) for low in range(2)]
        for high in range(0, n_bfly, 2)
    ]
    terms = lax.all_to_all(terms, ("freq", "bfly"), 0, 0, axis_index_groups=groups)
    total = jnp.sum(terms, axis=(0, 1))
    gradient = total[:rows] / jnp.sqrt(total[rows:] + epsilon)
    return (gradient, residual)


def solution(mesh):
    return jax.shard_map(
        local,
        mesh=mesh,
        in_specs=(
            P(None, "bfly", "freq"),
            P(None, "bfly", "freq"),
            P("bfly"),
            P("bfly"),
            P(None, "bfly", "freq"),
            P(None, None, "bfly", None),
            P(None, None, "bfly", None),
            P(None, None, "bfly", None),
        ),
        out_specs=(P("bfly"), P(None, "bfly", "freq")),
        check_vma=False,
    )
```

time: 102 us -> 95.5 us (0.936)
  local copies, waits for them, and re-layouts: 7.06 us -> 0.06 us
  Pallas kernels: 0 us -> 5.45 us
  waiting for transfers between devices: 46.8 us -> 42.1 us
  starting transfers between devices: 39.4 us -> 40.7 us
    pallas_call x0 -> x4, Pallas kernels: none -> 5.45 us  [the longest x1 2.03 us: local(): pl.pallas_call(later_maps, out_shape=(shape((3, 2 * rows, 2 * rows), bf16...]
    ppermute x8, waiting for transfers between devices: 37.4 us -> 32.8 us  [swapped(): return lax.ppermute(block, 'bfly', route)]
    ppermute x8, starting transfers between devices: 22.2 us -> 26.8 us  [swapped(): return lax.ppermute(block, 'bfly', route)]
    unnamed x16 -> x4, local copies, waits for them, and re-layouts: 3.75 us -> 0.01 us
    all_to_all x1, starting transfers between devices: 17.1 us -> 13.9 us  [local(): lax.all_to_all(terms, ('freq', 'bfly'), 0, 0, axis_index_groups=groups)]
    dot_general x20 -> x16, matrix products: 4.31 us -> 4.12 us  [the longest x8 2.39 us: mul(): return jnp.dot(matrix, values, preferred_element_type=f32)]
  transfers between devices with their start and end apart: 9 -> 9, of which waited for: 7 -> 7; matrix products, arithmetic and copies ran while one was open for 4% -> 3% of each run, Pallas kernels for 0% -> 4%
where the time goes in v2:
time: 95.5 us; the launch traced here: 95 us
  waiting for transfers between devices  42.1 us (44%)
  starting transfers between devices  40.7 us (43%)
  Pallas kernels  5.45 us (6%)
  matrix products  4.12 us (4%)
  other arithmetic  1.64 us (2%)
  between operations  0.96 us (1%)
    ppermute x8, waiting for transfers between devices, swapped(): return lax.ppermute(block, 'bfly', route)  32.8 us
    ppermute x8, starting transfers between devices, swapped(): return lax.ppermute(block, 'bfly', route)  26.8 us
    all_to_all x1, starting transfers between devices, local(): lax.all_to_all(terms, ('freq', 'bfly'), 0, 0, axis_index_groups=groups)  13.9 us
    all_to_all x1, waiting for transfers between devices, local(): lax.all_to_all(terms, ('freq', 'bfly'), 0, 0, axis_index_groups=groups)  9.35 us
    dot_general x8, matrix products, mul(): return jnp.dot(matrix, values, preferred_element_type=f32)  2.39 us
    pallas_call x1, Pallas kernels, local(): pl.pallas_call(later_maps, out_shape=(shape((3, 2 * rows, 2 * rows), bf16...  2.03 us
  transfers between devices with their start and end apart: 9, of which 7 were waited for; matrix products, arithmetic and copies ran while one was open for 3% of the time, Pallas kernels for 4%

profile of v2, /device:TPU:1, one launch (start us, length us, event | category | flops | bytes accessed | tf_op | source)
XLA Modules:
  0.0 95.0 jit_solution(3139659806197258301)
XLA Ops:
  0.6 1.0 %first_field.1 = bf16[256,256]{1,0:T(8,128)(2,1)S(1)} custom-call(bf16[2,128,256]{2,1,0:T(8,128)(2,1)} %sources_ref.1, f32[1,128]{1,0:T(1,128)} %bitcast.71), custom_call_target="tpu_custom_call" | custom-call | tf_op jit(solution)/shard_map/first_field/pallas_call | solution.py:141
  1.6 8.8 %collective-permute-start = (bf16[256,256]{1,0:T(8,128)(2,1)S(1)}, bf16[256,256]{1,0:T(8,128)(2,1)S(1)}, u32[]{:S(2)}, u32[]{:S(2)}) collective-permute-start(bf16[256,256]{1,0:T(8,128)(2,1)S(1)} %first_field.1), channel_id=1, source_target_pairs={{0,1},{1,0},{2,3},{3,2},{4,5},{5,4},{6,7},{7,6},{8,9},{9,8},{10,11... | collective-permute-start | bytes 393224 | tf_op jit(solution)/shard_map/ppermute | solution.py:17
  10.4 1.3 %first_maps.1 = (bf16[256,256]{1,0:T(8,128)(2,1)S(1)}, bf16[256,256]{1,0:T(8,128)(2,1)S(1)}, f32[128,512]{1,0:T(8,128)S(1)}) custom-call(bf16[4,2,128,128]{3,2,1,0:T(8,128)(2,1)} %near_ref.3, bf16[4,2,128,128]{3,2,1,0:T(8,128)(2,1)} %far_ref.3, s32[2,2,2,4]{3,2,1,0:T(2,128)} %bitcast.69, f32[4,4,128]{2,1,0:T(4,128)} %bitcast.67), custom_call_target="tpu_custom_call" | custom-call | tf_op jit(solution)/shard_map/first_maps/pallas_call | solution.py:151
  11.8 0.2 fusion.40
  12.0 0.0 collective-permute-done
  12.0 0.2 convolution_add_fusion.3
  12.2 1.9 %collective-permute-start.1 = (bf16[256,256]{1,0:T(8,128)(2,1)S(1)}, bf16[256,256]{1,0:T(8,128)(2,1)}, u32[]{:S(2)}, u32[]{:S(2)}) collective-permute-start(bf16[256,256]{1,0:T(8,128)(2,1)S(1)} %pad_maximum_fusion), channel_id=1, source_target_pairs={{0,2},{1,3},{2,0},{3,1},{4,6},{5,7},{6,4},{7,5},{8,10},{9,11},{10,... | collective-permute-start | bytes 393224 | tf_op jit(solution)/shard_map/ppermute | solution.py:17
  14.2 2.0 %later_maps.1 = (bf16[3,256,256]{2,1,0:T(8,128)(2,1)S(1)}, bf16[3,256,256]{2,1,0:T(8,128)(2,1)S(1)}, f32[3,128,512]{2,1,0:T(8,128)S(1)}, bf16[128,128]{1,0:T(8,1...) custom-call(bf16[4,2,128,128]{3,2,1,0:T(8,128)(2,1)} %near_ref.3, bf16[4,2,128,128]{3,2,1,0:T(8,128)(2,1)} %far_ref.3, ...), custom_call_target="tpu_custom_call" | custom-call | tf_op jit(solution)/shard_map/later_maps/pallas_call | solution.py:168
  16.2 0.1 slice_bitcast_fusion
  16.3 0.2 fusion.20
  16.5 2.9 %collective-permute-done.1 = bf16[256,256]{1,0:T(8,128)(2,1)} collective-permute-done((bf16[256,256]{1,0:T(8,128)(2,1)S(1)}, bf16[256,256]{1,0:T(8,128)(2,1)}, u32[]{:S(2)}, u32[]{:S(2)}) %collective-permute-start.1) | collective-permute-done | bytes 131104 | tf_op jit(solution)/shard_map/ppermute | solution.py:17
  19.4 1.1 %convolution_add_fusion.2 = f32[256,256]{1,0:T(8,128)S(1)} fusion(f32[256,256]{1,0:T(8,128)S(1)} %fusion.20, bf16[256,256]{1,0:T(8,128)(2,1)} %collective-permute-done.1, bf16[3,256,256]{2,1,0:T(8,128)(2,1)S(1)} %get-tuple-element.20), kind=kOutput, calls=%fused_computation.2 | convolution fusion | flops 33619968 | bytes 786432 | tf_op jit(solution)/shard_map/dot_general | solution.py:32
  20.5 1.9 %collective-permute-start.2 = (bf16[256,256]{1,0:T(8,128)(2,1)S(1)}, bf16[256,256]{1,0:T(8,128)(2,1)S(1)}, u32[]{:S(2)}, u32[]{:S(2)}) collective-permute-start(bf16[256,256]{1,0:T(8,128)(2,1)S(1)} %pad_maximum_fusion.1), channel_id=1, source_target_pairs={{0,4},{1,5},{2,6},{3,7},{4,0},{5,1},{6,2},{7,3},{8,12},{9,13},{10,... | collective-permute-start | bytes 393224 | tf_op jit(solution)/shard_map/ppermute | solution.py:17
  22.4 0.2 fusion.14
  22.6 8.8 %collective-permute-done.2 = bf16[256,256]{1,0:T(8,128)(2,1)S(1)} collective-permute-done((bf16[256,256]{1,0:T(8,128)(2,1)S(1)}, bf16[256,256]{1,0:T(8,128)(2,1)S(1)}, u32[]{:S(2)}, u32[]{:S(2)}) %collective-permute-start.2) | collective-permute-done | bytes 131104 | tf_op jit(solution)/shard_map/ppermute | solution.py:17
  31.5 0.2 convolution_add_fusion.1
  31.7 2.1 %collective-permute-start.3 = (bf16[256,256]{1,0:T(8,128)(2,1)S(1)}, bf16[256,256]{1,0:T(8,128)(2,1)S(1)}, u32[]{:S(2)}, u32[]{:S(2)}) collective-permute-start(bf16[256,256]{1,0:T(8,128)(2,1)S(1)} %pad_maximum_fusion.2), channel_id=1, source_target_pairs={{0,8},{1,9},{2,10},{3,11},{4,12},{5,13},{6,14},{7,15},{8,0},{9,1},... | collective-permute-start | bytes 393224 | tf_op jit(solution)/shard_map/ppermute | solution.py:17
  33.8 0.2 fusion.8
  34.0 8.1 %collective-permute-done.3 = bf16[256,256]{1,0:T(8,128)(2,1)S(1)} collective-permute-done((bf16[256,256]{1,0:T(8,128)(2,1)S(1)}, bf16[256,256]{1,0:T(8,128)(2,1)S(1)}, u32[]{:S(2)}, u32[]{:S(2)}) %collective-permute-start.3) | collective-permute-done | bytes 131104 | tf_op jit(solution)/shard_map/ppermute | solution.py:17
  42.1 0.2 subtract_convert_fusion
  42.3 0.2 convolution_convert_fusion.2
  42.5 1.9 %collective-permute-start.4 = (bf16[256,256]{1,0:T(8,128)(2,1)S(1)}, bf16[256,256]{1,0:T(8,128)(2,1)S(1)}, u32[]{:S(2)}, u32[]{:S(2)}) collective-permute-start(bf16[256,256]{1,0:T(8,128)(2,1)S(1)} %convolution_convert_fusion.2), channel_id=1, source_target_pairs={{0,8},{1,9},{2,10},{3,11},{4,12},{5,13},{6,14},{7,15},{8,0},{9,1},... | collective-permute-start | bytes 393224 | tf_op jit(solution)/shard_map/ppermute | solution.py:17
  44.5 8.2 %collective-permute-done.4 = bf16[256,256]{1,0:T(8,128)(2,1)S(1)} collective-permute-done((bf16[256,256]{1,0:T(8,128)(2,1)S(1)}, bf16[256,256]{1,0:T(8,128)(2,1)S(1)}, u32[]{:S(2)}, u32[]{:S(2)}) %collective-permute-start.4) | collective-permute-done | bytes 131104 | tf_op jit(solution)/shard_map/ppermute | solution.py:17
  52.6 0.2 convert_add_fusion.2
  52.9 0.0 copy-start
  52.9 0.2 convolution_convert_fusion.1
  53.2 1.9 %collective-permute-start.5 = (bf16[256,256]{1,0:T(8,128)(2,1)S(1)}, bf16[256,256]{1,0:T(8,128)(2,1)S(1)}, u32[]{:S(2)}, u32[]{:S(2)}) collective-permute-start(bf16[256,256]{1,0:T(8,128)(2,1)S(1)} %convolution_convert_fusion.1), channel_id=1, source_target_pairs={{0,4},{1,5},{2,6},{3,7},{4,0},{5,1},{6,2},{7,3},{8,12},{9,13},{10,... | collective-permute-start | bytes 393224 | tf_op jit(solution)/shard_map/ppermute | solution.py:17
  55.1 0.0 copy-done
  55.1 6.4 %collective-permute-start.7 = (bf16[256,256]{1,0:T(8,128)(2,1)S(1)}, bf16[256,256]{1,0:T(8,128)(2,1)S(1)}, u32[]{:S(2)}, u32[]{:S(2)}) collective-permute-start(bf16[256,256]{1,0:T(8,128)(2,1)S(1)} %bitcast.65), channel_id=1, source_target_pairs={{0,1},{1,0},{2,3},{3,2},{4,5},{5,4},{6,7},{7,6},{8,9},{9,8},{10,11... | collective-permute-start | bytes 393224 | tf_op jit(solution)/shard_map/ppermute | solution.py:17
  61.5 1.3 %collective-permute-done.5 = bf16[256,256]{1,0:T(8,128)(2,1)S(1)} collective-permute-done((bf16[256,256]{1,0:T(8,128)(2,1)S(1)}, bf16[256,256]{1,0:T(8,128)(2,1)S(1)}, u32[]{:S(2)}, u32[]{:S(2)}) %collective-permute-start.5) | collective-permute-done | bytes 131104 | tf_op jit(solution)/shard_map/ppermute | solution.py:17
  62.8 0.2 convert_add_fusion.1
  63.1 0.2 convolution_convert_fusion
  63.3 1.9 %collective-permute-start.6 = (bf16[256,256]{1,0:T(8,128)(2,1)S(1)}, bf16[256,256]{1,0:T(8,128)(2,1)S(1)}, u32[]{:S(2)}, u32[]{:S(2)}) collective-permute-start(bf16[256,256]{1,0:T(8,128)(2,1)S(1)} %convolution_convert_fusion), channel_id=1, source_target_pairs={{0,2},{1,3},{2,0},{3,1},{4,6},{5,7},{6,4},{7,5},{8,10},{9,11},{10,... | collective-permute-start | bytes 393224 | tf_op jit(solution)/shard_map/ppermute | solution.py:17
  65.3 0.2 convolution_bitcast_fusion.1
  65.5 0.2 convolution_bitcast_fusion
  65.6 3.4 %collective-permute-done.6 = bf16[256,256]{1,0:T(8,128)(2,1)S(1)} collective-permute-done((bf16[256,256]{1,0:T(8,128)(2,1)S(1)}, bf16[256,256]{1,0:T(8,128)(2,1)S(1)}, u32[]{:S(2)}, u32[]{:S(2)}) %collective-permute-start.6) | collective-permute-done | bytes 131104 | tf_op jit(solution)/shard_map/ppermute | solution.py:17
  69.0 0.2 convert_add_fusion
  69.3 0.0 collective-permute-done.7.partner_ref
  69.4 1.1 %last_terms.1 = f32[64,1,256]{2,1,0:T(1,128)} custom-call(bf16[256,256]{1,0:T(8,128)(2,1)S(1)} %pad_maximum_fusion.5.turned_ref, bf16[256,256]{1,0:T(8,128)(2,1)S(1)} %get-tuple-element.14.near_ref, bf16[256,256]{1,0:T(8,128)(2,1)S(1)} %get-tuple-element.15.far_ref, bf16[256,256]{1,0:T(8,128)(2,1)S(1)} %bitcast.66, ...), custom_call_target="tpu_custom_call" | custom-call | tf_op jit(solution)/shard_map/last_terms/pallas_call | solution.py:216
  70.4 0.0 copy-start.1
  70.4 13.9 %all-to-all-start = ((f32[64,1,256]{2,1,0:T(1,128)}), f32[64,1,256]{2,1,0:T(1,128)S(1)}, u32[]{:S(2)}, u32[]{:S(2)}) async-start(f32[64,1,256]{2,1,0:T(1,128)} %last_terms.1), calls=%async_computation | async-start | bytes 131072 | tf_op jit(solution)/shard_map/all_to_all | solution.py:233
  84.3 0.0 copy-done.1
  84.3 0.7 maximum_subtract_fusion
  85.1 9.3 %all-to-all-done = f32[64,1,256]{2,1,0:T(1,128)S(1)} async-done(((f32[64,1,256]{2,1,0:T(1,128)}), f32[64,1,256]{2,1,0:T(1,128)S(1)}, u32[]{:S(2)}, u32[]{:S(2)}) %all-to-all-start) | async-done | bytes 65568 | tf_op jit(solution)/shard_map/all_to_all | solution.py:233
  94.4 0.1 reduce_sum.9
  94.5 0.5 rsqrt_multiply_fusion
  (10 shorter events, 0.3 us)
Async XLA Ops:
  1.6 10.3 %collective-permute-start = (bf16[256,256]{1,0:T(8,128)(2,1)S(1)}, bf16[256,256]{1,0:T(8,128)(2,1)S(1)}, u32[]{:S(2)}, u32[]{:S(2)}) collective-permute-start(bf16[256,256]{1,0:T(8,128)(2,1)S(1)} %first_field.1), channel_id=1, source_target_pairs={{0,1},{1,0},{2,3},{3,2},{4,5},{5,4},{6,7},{7,6},{8,9},{9,8},{10,11... | collective-permute-start | bytes 393224 | tf_op jit(solution)/shard_map/ppermute | solution.py:17
  12.2 7.1 %collective-permute-start.1 = (bf16[256,256]{1,0:T(8,128)(2,1)S(1)}, bf16[256,256]{1,0:T(8,128)(2,1)}, u32[]{:S(2)}, u32[]{:S(2)}) collective-permute-start(bf16[256,256]{1,0:T(8,128)(2,1)S(1)} %pad_maximum_fusion), channel_id=1, source_target_pairs={{0,2},{1,3},{2,0},{3,1},{4,6},{5,7},{6,4},{7,5},{8,10},{9,11},{10,... | collective-permute-start | bytes 393224 | tf_op jit(solution)/shard_map/ppermute | solution.py:17
  20.5 11.0 %collective-permute-start.2 = (bf16[256,256]{1,0:T(8,128)(2,1)S(1)}, bf16[256,256]{1,0:T(8,128)(2,1)S(1)}, u32[]{:S(2)}, u32[]{:S(2)}) collective-permute-start(bf16[256,256]{1,0:T(8,128)(2,1)S(1)} %pad_maximum_fusion.1), channel_id=1, source_target_pairs={{0,4},{1,5},{2,6},{3,7},{4,0},{5,1},{6,2},{7,3},{8,12},{9,13},{10,... | collective-permute-start | bytes 393224 | tf_op jit(solution)/shard_map/ppermute | solution.py:17
  31.7 10.4 %collective-permute-start.3 = (bf16[256,256]{1,0:T(8,128)(2,1)S(1)}, bf16[256,256]{1,0:T(8,128)(2,1)S(1)}, u32[]{:S(2)}, u32[]{:S(2)}) collective-permute-start(bf16[256,256]{1,0:T(8,128)(2,1)S(1)} %pad_maximum_fusion.2), channel_id=1, source_target_pairs={{0,8},{1,9},{2,10},{3,11},{4,12},{5,13},{6,14},{7,15},{8,0},{9,1},... | collective-permute-start | bytes 393224 | tf_op jit(solution)/shard_map/ppermute | solution.py:17
  42.5 10.1 %collective-permute-start.4 = (bf16[256,256]{1,0:T(8,128)(2,1)S(1)}, bf16[256,256]{1,0:T(8,128)(2,1)S(1)}, u32[]{:S(2)}, u32[]{:S(2)}) collective-permute-start(bf16[256,256]{1,0:T(8,128)(2,1)S(1)} %convolution_convert_fusion.2), channel_id=1, source_target_pairs={{0,8},{1,9},{2,10},{3,11},{4,12},{5,13},{6,14},{7,15},{8,0},{9,1},... | collective-permute-start | bytes 393224 | tf_op jit(solution)/shard_map/ppermute | solution.py:17
  52.9 2.2 %copy-start = (bf16[2,128,256]{2,1,0:T(8,128)(2,1)S(1)}, bf16[2,128,256]{2,1,0:T(8,128)(2,1)}, u32[]{:S(2)}) copy-start(bf16[2,128,256]{2,1,0:T(8,128)(2,1)} %sources_ref.1) | copy-start | bytes 393220
  53.2 9.7 %collective-permute-start.5 = (bf16[256,256]{1,0:T(8,128)(2,1)S(1)}, bf16[256,256]{1,0:T(8,128)(2,1)S(1)}, u32[]{:S(2)}, u32[]{:S(2)}) collective-permute-start(bf16[256,256]{1,0:T(8,128)(2,1)S(1)} %convolution_convert_fusion.1), channel_id=1, source_target_pairs={{0,4},{1,5},{2,6},{3,7},{4,0},{5,1},{6,2},{7,3},{8,12},{9,13},{10,... | collective-permute-start | bytes 393224 | tf_op jit(solution)/shard_map/ppermute | solution.py:17
  55.1 14.2 %collective-permute-start.7 = (bf16[256,256]{1,0:T(8,128)(2,1)S(1)}, bf16[256,256]{1,0:T(8,128)(2,1)S(1)}, u32[]{:S(2)}, u32[]{:S(2)}) collective-permute-start(bf16[256,256]{1,0:T(8,128)(2,1)S(1)} %bitcast.65), channel_id=1, source_target_pairs={{0,1},{1,0},{2,3},{3,2},{4,5},{5,4},{6,7},{7,6},{8,9},{9,8},{10,11... | collective-permute-start | bytes 393224 | tf_op jit(solution)/shard_map/ppermute | solution.py:17
  63.3 5.7 %collective-permute-start.6 = (bf16[256,256]{1,0:T(8,128)(2,1)S(1)}, bf16[256,256]{1,0:T(8,128)(2,1)S(1)}, u32[]{:S(2)}, u32[]{:S(2)}) collective-permute-start(bf16[256,256]{1,0:T(8,128)(2,1)S(1)} %convolution_convert_fusion), channel_id=1, source_target_pairs={{0,2},{1,3},{2,0},{3,1},{4,6},{5,7},{6,4},{7,5},{8,10},{9,11},{10,... | collective-permute-start | bytes 393224 | tf_op jit(solution)/shard_map/ppermute | solution.py:17
  70.4 13.9 %copy-start.1 = (bf16[2,128,256]{2,1,0:T(8,128)(2,1)S(1)}, bf16[2,128,256]{2,1,0:T(8,128)(2,1)}, u32[]{:S(2)}) copy-start(bf16[2,128,256]{2,1,0:T(8,128)(2,1)} %observed_ref.1) | copy-start | bytes 393220
  70.4 24.0 %all-to-all-start = ((f32[64,1,256]{2,1,0:T(1,128)}), f32[64,1,256]{2,1,0:T(1,128)S(1)}, u32[]{:S(2)}, u32[]{:S(2)}) async-start(f32[64,1,256]{2,1,0:T(1,128)} %last_terms.1), calls=%async_computation | async-start | bytes 131072 | tf_op jit(solution)/shard_map/all_to_all | solution.py:233

commit v3 on v2

--- a/solution.py
+++ b/solution.py
@@ -85,10 +85,38 @@
         field_out[part * rows : (part + 1) * rows] = field.astype(bf16)
 
 
-def first_maps(near_ref, far_ref, pattern_ref, phases_ref, near_out, far_out, waves_out):
-    near_out[...] = stacked(masked(near_ref[0], pattern_ref, 0, 0))
-    far_out[...] = stacked(masked(far_ref[0], pattern_ref, 0, 1))
-    waves_out[...] = waves(phases_ref[0], waves_out.shape[-1] // 2)
+def first_maps(
+    sources_ref, near_ref, far_ref, pattern_ref, phases_ref, near_out, far_out, waves_out, lend_out
+):
+    rows, columns = sources_ref.shape[1:]
+    near = masked(near_ref[0], pattern_ref, 0, 0)
+    far = masked(far_ref[0], pattern_ref, 0, 1)
+    near_out[...] = stacked(near)
+    far_out[...] = stacked(far)
+    angles = phases_ref[0]
+    waves_out[...] = waves(angles, columns)
+    for part in range(2):
+        lend_out[part * rows : (part + 1) * rows] = sources_ref[part]
+        both = jnp.concatenate([near[part], far[part]], axis=1)
+        lend_out[(2 + part) * rows : (3 + part) * rows] = both
+    high = angles.astype(bf16).astype(f32)
+    middle = (angles - high).astype(bf16).astype(f32)
+    low = angles - high - middle
+    low = jnp.concatenate([low, jnp.zeros_like(low)], axis=1)
+    split = jnp.concatenate([jnp.concatenate([high, middle], axis=1), low])
+    lend_out[4 * rows :] = jnp.concatenate([split, jnp.zeros_like(split)]).astype(bf16)
+
+
+def lent_maps(lent_ref, near_out, far_out, waves_out):
+    columns = lent_ref.shape[1]
+    rows = near_out.shape[0] // 2
+    split = lent_ref[4 * rows :].astype(f32)
+    count = split.shape[0] // 4
+    angles = split[:count, :rows] + split[:count, rows:] + split[count : 2 * count, :rows]
+    waves_out[...] = waves(angles, columns)
+    real, imag = lent_ref[2 * rows : 3 * rows], lent_ref[3 * rows : 4 * rows]
+    near_out[...] = stacked([real[:, :rows], imag[:, :rows]])
+    far_out[...] = stacked([real[:, rows:], imag[:, rows:]])
 
 
 def later_maps(
@@ -111,25 +139,50 @@
     data_out[...] = turn_back(spread, cosine, sine)
 
 
-def last_terms(turned_ref, near_ref, far_ref, sources_ref, partner_ref, first_ref, terms_out):
+def last_terms(
+    turned_ref, near_1_ref, far_1_ref, near_ref, far_ref, waves_ref, near_2_ref, far_2_ref,
+    waves_2_ref, sources_ref, lent_ref, across_ref, place_ref, terms_out,
+):
     rows = sources_ref.shape[0] // 2
-    wide = sources_ref[...].astype(f32)
-    partner = partner_ref[...].astype(f32)
-    turned = turned_ref[...]
+    columns = sources_ref.shape[1]
 
     def row_sums(product):
         total = product[:rows] + product[rows:]
         return jnp.sum(total.T, axis=0, keepdims=True)
 
-    own = row_sums(wide * mul_t(near_ref[...], turned))
-    other = row_sums(partner * mul_t(far_ref[...], turned))
-    own = jnp.concatenate([own, row_sums(wide * wide)], axis=1)
-    other = jnp.concatenate([other, jnp.zeros_like(other)], axis=1)
-    first = first_ref[0] == 0
-    even, odd = jnp.where(first, own, other), jnp.where(first, other, own)
-    n_freq = terms_out.shape[0] // 2
-    pair = jnp.concatenate([even, odd])
-    terms_out[...] = jnp.concatenate([pair[None]] * n_freq).reshape(terms_out.shape)
+    def term(sources, maps_ref, turned):
+        return row_sums(sources.astype(f32) * mul_t(maps_ref[...], turned))
+
+    def turned_by(values, wave_ref):
+        return turn_back(values, wave_ref[:, :columns], wave_ref[:, columns:]).astype(bf16)
+
+    turned = turned_ref[...]
+    own = turned_by(mul_t(near_1_ref[...], turned), waves_ref)
+    other = turned_by(mul_t(far_1_ref[...], turned), waves_2_ref)
+    terms = [
+        term(sources_ref[...], near_ref, own),
+        term(across_ref[: 2 * rows], far_ref, own),
+        term(lent_ref[: 2 * rows], near_2_ref, other),
+        term(across_ref[2 * rows :], far_2_ref, other),
+    ]
+    wide = sources_ref[...].astype(f32)
+    light = row_sums(wide * wide)
+    lights = [light] + [jnp.zeros_like(light)] * 3
+    terms = [jnp.concatenate(pair, axis=1) for pair in zip(terms, lights)]
+    for bit in (1, 2):
+        swap = place_ref[0] & bit != 0
+        terms = [jnp.where(swap, terms[n ^ bit], terms[n]) for n in range(4)]
+    quad = jnp.concatenate(terms)
+    n_freq = terms_out.shape[0] // 4
+    terms_out[...] = jnp.concatenate([quad[None]] * n_freq).reshape(terms_out.shape)
+
+
+def in_hbm(values):
+    return pltpu.with_memory_space_constraint(values, pltpu.HBM)
+
+
+def in_vmem(values):
+    return pltpu.with_memory_space_constraint(values, pltpu.VMEM)
 
 
 def local(sources, observed, receivers, model, phases, near_blocks, far_blocks, pattern):
@@ -143,28 +196,32 @@
         out_shape=shape((2 * rows, columns), bf16),
         in_specs=[VMEM, VMEM],
         out_specs=VMEM,
+        compiler_params=pltpu.CompilerParams(vmem_limit_bytes=16 << 20),
         name="first_field",
-    )(sources, model[None])
+    )(in_hbm(sources), in_hbm(model[None]))
     partner = swapped(field, 0)
     blocks = pl.BlockSpec((1, 2, rows, rows), lambda step: (0, 0, 0, 0))
     angles = pl.BlockSpec((1, *phases.shape[1:]), lambda step: (0, 0, 0))
-    near_0, far_0, waves_0 = pl.pallas_call(
+    near_0, far_0, waves_0, lend = pl.pallas_call(
         first_maps,
         out_shape=(
             shape((2 * rows, 2 * rows), bf16),
             shape((2 * rows, 2 * rows), bf16),
             shape((rows, 2 * columns), f32),
+            shape((4 * rows + 16, columns), bf16),
         ),
         grid=(1,),
-        in_specs=[blocks, blocks, VMEM, angles],
-        out_specs=(VMEM,) * 3,
+        in_specs=[VMEM, blocks, blocks, VMEM, angles],
+        out_specs=(VMEM,) * 4,
+        compiler_params=pltpu.CompilerParams(vmem_limit_bytes=16 << 20),
         name="first_maps",
-    )(near_blocks, far_blocks, pattern, phases)
+    )(*map(in_hbm, (sources, near_blocks, far_blocks, pattern, phases)))
     cosine_0, sine_0 = waves_0[:, :columns], waves_0[:, columns:]
     mixed = mul(near_0, field) + mul(far_0, partner)
     field = turn(mixed, cosine_0, sine_0).astype(bf16)
 
     partner = swapped(field, 1)
+    lent = swapped(after(lend, field), 1)
     near, far, wave, select, counts, data = pl.pallas_call(
         later_maps,
         out_shape=(
@@ -177,8 +234,9 @@
         ),
         in_specs=[VMEM] * 6,
         out_specs=(VMEM,) * 6,
+        compiler_params=pltpu.CompilerParams(vmem_limit_bytes=16 << 20),
         name="later_maps",
-    )(near_blocks, far_blocks, pattern, phases, observed, after(receivers, field)[None])
+    )(*map(in_hbm, (near_blocks, far_blocks, pattern, phases, observed)), after(receivers, field)[None])
     near_1, near_2, near_3 = near
     far_1, far_2, far_3 = far
     (cosine_1, sine_1), (cosine_2, sine_2), (cosine_3, sine_3) = (
@@ -193,7 +251,20 @@
 
     partner = swapped(field, 3)
     sources = sources.reshape(2 * rows, columns)
-    partner_sources = swapped(after(sources, field), 0)
+    lent = after(lent, field)
+    across = swapped(jnp.concatenate([sources, lent[: 2 * rows]]), 0)
+    near_lent, far_lent, waves_lent = pl.pallas_call(
+        lent_maps,
+        out_shape=(
+            shape((2 * rows, 2 * rows), bf16),
+            shape((2 * rows, 2 * rows), bf16),
+            shape((rows, 2 * columns), f32),
+        ),
+        in_specs=[VMEM],
+        out_specs=(VMEM,) * 3,
+        compiler_params=pltpu.CompilerParams(vmem_limit_bytes=16 << 20),
+        name="lent_maps",
+    )(in_vmem(lent))
     mixed = mul(near_3, field) + mul(far_3, partner)
     turned = (counts * mixed - data).astype(bf16)
 
@@ -201,34 +272,26 @@
     last = turn(mixed, cosine_3, sine_3).astype(bf16)
     picked = jnp.stack([mul_t(select, last[:rows]), mul_t(select, last[rows:])])
     residual = picked - observed.astype(f32)
-    adjoint = mul_t(near_3, turned) + far_term.astype(f32)
+    adjoint = lax.optimization_barrier(mul_t(near_3, turned)) + far_term.astype(f32)
     turned = turn_back(adjoint, cosine_2, sine_2).astype(bf16)
 
     far_term = swapped(mul_t(far_2, turned).astype(bf16), 2)
-    adjoint = mul_t(near_2, turned) + far_term.astype(f32)
+    adjoint = lax.optimization_barrier(mul_t(near_2, turned)) + far_term.astype(f32)
     turned = turn_back(adjoint, cosine_1, sine_1).astype(bf16)
 
-    far_term = swapped(mul_t(far_1, turned).astype(bf16), 1)
-    adjoint = mul_t(near_1, turned) + far_term.astype(f32)
-    turned = turn_back(adjoint, cosine_0, sine_0).astype(bf16)
-
     n_bfly, n_freq = lax.axis_size("bfly"), lax.axis_size("freq")
+    inputs = (turned, near_1, far_1, near_0, far_0, waves_0, near_lent, far_lent, waves_lent)
     terms = pl.pallas_call(
         last_terms,
-        out_shape=jax.ShapeDtypeStruct((2 * n_freq, 1, 2 * rows), f32),
-        in_specs=[VMEM] * 5 + [SMEM],
+        out_shape=jax.ShapeDtypeStruct((4 * n_freq, 1, 2 * rows), f32),
+        in_specs=[VMEM] * 12 + [SMEM],
         out_specs=VMEM,
+        compiler_params=pltpu.CompilerParams(vmem_limit_bytes=16 << 20),
         name="last_terms",
-    )(
-        *(
-            pltpu.with_memory_space_constraint(each, pltpu.VMEM)
-            for each in (turned, near_0, far_0, sources, partner_sources)
-        ),
-        (lax.axis_index("bfly") & 1)[None],
-    )
+    )(*map(in_vmem, (*inputs, sources, lent, across)), (lax.axis_index("bfly") & 3)[None])
     groups = [
-        [f * n_bfly + high + low for f in range(n_freq) for low in range(2)]
-        for high in range(0, n_bfly, 2)
+        [f * n_bfly + high + low for f in range(n_freq) for low in range(4)]
+        for high in range(0, n_bfly, 4)
     ]
     terms = lax.all_to_all(terms, ("freq", "bfly"), 0, 0, axis_index_groups=groups)
     total = jnp.sum(terms, axis=(0, 1))

time: 95.5 us -> 89.7 us (0.939)
  waiting for transfers between devices: 42.1 us -> 33.8 us
  starting transfers between devices: 40.7 us -> 42.4 us
  matrix products: 4.12 us -> 2.77 us
  local copies, waits for them, and re-layouts: 0.06 us -> 1.24 us
    ppermute x8, waiting for transfers between devices: 32.8 us -> 24.4 us  [swapped(): return lax.ppermute(block, 'bfly', route)]
    all_to_all x1, starting transfers between devices: 13.9 us -> 16.9 us  [local(): lax.all_to_all(terms, ('freq', 'bfly'), 0, 0, axis_index_groups=groups)]
    ppermute x8, starting transfers between devices: 26.8 us -> 25.5 us  [swapped(): return lax.ppermute(block, 'bfly', route)]
    unnamed x4 -> x6, local copies, waits for them, and re-layouts: 0.01 us -> 1.16 us
  transfers between devices with their start and end apart: 9 -> 9, of which waited for: 7 -> 5; matrix products, arithmetic and copies ran while one was open for 3% -> 4% of each run, Pallas kernels for 4% -> 4%
where the time goes in v3:
time: 89.7 us; the launch traced here: 89.3 us
  starting transfers between devices  42.4 us (47%)
  waiting for transfers between devices  33.8 us (38%)
  Pallas kernels  6.33 us (7%)
  matrix products  2.77 us (3%)
  other arithmetic  1.73 us (2%)
  local copies, waits for them, and re-layouts  1.24 us (1%)
  between operations  0.98 us (1%)
    ppermute x8, starting transfers between devices, swapped(): return lax.ppermute(block, 'bfly', route)  25.5 us
    ppermute x8, waiting for transfers between devices, swapped(): return lax.ppermute(block, 'bfly', route)  24.4 us
    all_to_all x1, starting transfers between devices, local(): lax.all_to_all(terms, ('freq', 'bfly'), 0, 0, axis_index_groups=groups)  16.9 us
    all_to_all x1, waiting for transfers between devices, local(): lax.all_to_all(terms, ('freq', 'bfly'), 0, 0, axis_index_groups=groups)  9.45 us
    pallas_call x1, Pallas kernels, local(): pl.pallas_call(later_maps, out_shape=(shape((3, 2 * rows, 2 * rows), bf16...  2.03 us
  transfers between devices with their start and end apart: 9, of which 5 were waited for; matrix products, arithmetic and copies ran while one was open for 4% of the time, Pallas kernels for 4%

profile of v3, /device:TPU:1, one launch (start us, length us, event | category | flops | bytes accessed | tf_op | source)
XLA Modules:
  0.0 89.3 jit_solution(9433184027829751350)
XLA Ops:
  0.6 1.0 %first_field.1 = bf16[256,256]{1,0:T(8,128)(2,1)S(1)} custom-call(bf16[2,128,256]{2,1,0:T(8,128)(2,1)} %sources_ref.3, f32[1,128]{1,0:T(1,128)} %bitcast.62), custom_call_target="tpu_custom_call" | custom-call | tf_op jit(solution)/shard_map/first_field/pallas_call | solution.py:194
  1.6 8.8 %collective-permute-start = (bf16[256,256]{1,0:T(8,128)(2,1)S(1)}, bf16[256,256]{1,0:T(8,128)(2,1)S(1)}, u32[]{:S(2)}, u32[]{:S(2)}) collective-permute-start(bf16[256,256]{1,0:T(8,128)(2,1)S(1)} %first_field.1), channel_id=1, source_target_pairs={{0,1},{1,0},{2,3},{3,2},{4,5},{5,4},{6,7},{7,6},{8,9},{9,8},{10,11... | collective-permute-start | bytes 393224 | tf_op jit(solution)/shard_map/ppermute | solution.py:17
  10.4 1.4 %first_maps.1 = (bf16[256,256]{1,0:T(8,128)(2,1)S(1)}, bf16[256,256]{1,0:T(8,128)(2,1)S(1)}, f32[128,512]{1,0:T(8,128)S(1)}, bf16[528,256]{1,0:T(8,128)(2,1)S(1)}) custom-call(bf16[2,128,256]{2,1,0:T(8,128)(2,1)} %sources_ref.3, bf16[4,2,128,128]{3,2,1,0:T(8,128)(2,1)} %near_ref.3, bf16[4,2,128,128]{3,2,1,0:T(8,128)(2,1)} %far_ref.3, ...), custom_call_target="tpu_custom_call" | custom-call | tf_op jit(solution)/shard_map/first_maps/pallas_call | solution.py:205
  11.9 0.2 fusion.23
  12.1 0.0 collective-permute-done
  12.1 0.2 convolution_add_fusion.3
  12.3 1.9 %collective-permute-start.1 = (bf16[256,256]{1,0:T(8,128)(2,1)S(1)}, bf16[256,256]{1,0:T(8,128)(2,1)S(1)}, u32[]{:S(2)}, u32[]{:S(2)}) collective-permute-start(bf16[256,256]{1,0:T(8,128)(2,1)S(1)} %pad_maximum_fusion.1), channel_id=1, source_target_pairs={{0,2},{1,3},{2,0},{3,1},{4,6},{5,7},{6,4},{7,5},{8,10},{9,11},{10,... | collective-permute-start | bytes 393224 | tf_op jit(solution)/shard_map/ppermute | solution.py:17
  14.3 0.0 copy-start.1
  14.3 3.4 %collective-permute-start.6 = (bf16[528,256]{1,0:T(8,128)(2,1)S(1)}, bf16[528,256]{1,0:T(8,128)(2,1)S(1)}, u32[]{:S(2)}, u32[]{:S(2)}) collective-permute-start(bf16[528,256]{1,0:T(8,128)(2,1)S(1)} %get-tuple-element.28), channel_id=1, source_target_pairs={{0,2},{1,3},{2,0},{3,1},{4,6},{5,7},{6,4},{7,5},{8,10},{9,11},{10,... | collective-permute-start | bytes 811016 | tf_op jit(solution)/shard_map/ppermute | solution.py:17
  17.7 0.0 copy-done.1
  17.7 2.0 %later_maps.1 = (bf16[3,256,256]{2,1,0:T(8,128)(2,1)S(1)}, bf16[3,256,256]{2,1,0:T(8,128)(2,1)S(1)}, f32[3,128,512]{2,1,0:T(8,128)S(1)}, bf16[128,128]{1,0:T(8,1...) custom-call(bf16[4,2,128,128]{3,2,1,0:T(8,128)(2,1)} %near_ref.3, bf16[4,2,128,128]{3,2,1,0:T(8,128)(2,1)} %far_ref.3, ...), custom_call_target="tpu_custom_call" | custom-call | tf_op jit(solution)/shard_map/later_maps/pallas_call | solution.py:225
  19.7 0.1 slice_bitcast_fusion
  19.8 0.2 fusion.22
  20.0 0.0 collective-permute-done.1
  20.0 0.2 convolution_add_fusion.2
  20.2 1.9 %collective-permute-start.2 = (bf16[256,256]{1,0:T(8,128)(2,1)S(1)}, bf16[256,256]{1,0:T(8,128)(2,1)S(1)}, u32[]{:S(2)}, u32[]{:S(2)}) collective-permute-start(bf16[256,256]{1,0:T(8,128)(2,1)S(1)} %pad_maximum_fusion.2), channel_id=1, source_target_pairs={{0,4},{1,5},{2,6},{3,7},{4,0},{5,1},{6,2},{7,3},{8,12},{9,13},{10,... | collective-permute-start | bytes 393224 | tf_op jit(solution)/shard_map/ppermute | solution.py:17
  22.2 0.2 fusion.10
  22.4 8.6 %collective-permute-done.2 = bf16[256,256]{1,0:T(8,128)(2,1)S(1)} collective-permute-done((bf16[256,256]{1,0:T(8,128)(2,1)S(1)}, bf16[256,256]{1,0:T(8,128)(2,1)S(1)}, u32[]{:S(2)}, u32[]{:S(2)}) %collective-permute-start.2) | collective-permute-done | bytes 131104 | tf_op jit(solution)/shard_map/ppermute | solution.py:17
  31.0 0.2 convolution_add_fusion.1
  31.3 2.2 %collective-permute-start.3 = (bf16[256,256]{1,0:T(8,128)(2,1)S(1)}, bf16[256,256]{1,0:T(8,128)(2,1)S(1)}, u32[]{:S(2)}, u32[]{:S(2)}) collective-permute-start(bf16[256,256]{1,0:T(8,128)(2,1)S(1)} %pad_maximum_fusion.3), channel_id=1, source_target_pairs={{0,8},{1,9},{2,10},{3,11},{4,12},{5,13},{6,14},{7,15},{8,0},{9,1},... | collective-permute-start | bytes 393224 | tf_op jit(solution)/shard_map/ppermute | solution.py:17
  33.5 0.2 fusion.6
  33.7 0.0 collective-permute-done.6.lent_ref
  33.7 0.0 copy-start
  33.7 0.4 lent_maps.1
  34.2 0.4 copy-done
  34.7 2.8 %collective-permute-start.7 = (bf16[512,256]{1,0:T(8,128)(2,1)S(1)}, bf16[512,256]{1,0:T(8,128)(2,1)S(1)}, u32[]{:S(2)}, u32[]{:S(2)}) collective-permute-start(bf16[512,256]{1,0:T(8,128)(2,1)S(1)} %pad_maximum_fusion), channel_id=1, source_target_pairs={{0,1},{1,0},{2,3},{3,2},{4,5},{5,4},{6,7},{7,6},{8,9},{9,8},{10,11... | collective-permute-start | bytes 786440 | tf_op jit(solution)/shard_map/ppermute | solution.py:17
  37.5 4.3 %collective-permute-done.3 = bf16[256,256]{1,0:T(8,128)(2,1)S(1)} collective-permute-done((bf16[256,256]{1,0:T(8,128)(2,1)S(1)}, bf16[256,256]{1,0:T(8,128)(2,1)S(1)}, u32[]{:S(2)}, u32[]{:S(2)}) %collective-permute-start.3) | collective-permute-done | bytes 131104 | tf_op jit(solution)/shard_map/ppermute | solution.py:17
  41.7 0.2 subtract_convert_fusion
  41.9 0.2 convolution_convert_fusion.1
  42.2 2.6 %collective-permute-start.4 = (bf16[256,256]{1,0:T(8,128)(2,1)S(1)}, bf16[256,256]{1,0:T(8,128)(2,1)S(1)}, u32[]{:S(2)}, u32[]{:S(2)}) collective-permute-start(bf16[256,256]{1,0:T(8,128)(2,1)S(1)} %convolution_convert_fusion.1), channel_id=1, source_target_pairs={{0,8},{1,9},{2,10},{3,11},{4,12},{5,13},{6,14},{7,15},{8,0},{9,1},... | collective-permute-start | bytes 393224 | tf_op jit(solution)/shard_map/ppermute | solution.py:17
  44.8 0.2 fusion.4
  45.0 0.2 convolution_bitcast_fusion
  45.2 7.0 %collective-permute-done.4 = bf16[256,256]{1,0:T(8,128)(2,1)S(1)} collective-permute-done((bf16[256,256]{1,0:T(8,128)(2,1)S(1)}, bf16[256,256]{1,0:T(8,128)(2,1)S(1)}, u32[]{:S(2)}, u32[]{:S(2)}) %collective-permute-start.4) | collective-permute-done | bytes 131104 | tf_op jit(solution)/shard_map/ppermute | solution.py:17
  52.3 0.2 convolution_convert_fusion
  52.5 1.9 %collective-permute-start.5 = (bf16[256,256]{1,0:T(8,128)(2,1)S(1)}, bf16[256,256]{1,0:T(8,128)(2,1)S(1)}, u32[]{:S(2)}, u32[]{:S(2)}) collective-permute-start(bf16[256,256]{1,0:T(8,128)(2,1)S(1)} %convolution_convert_fusion), channel_id=1, source_target_pairs={{0,4},{1,5},{2,6},{3,7},{4,0},{5,1},{6,2},{7,3},{8,12},{9,13},{10,... | collective-permute-start | bytes 393224 | tf_op jit(solution)/shard_map/ppermute | solution.py:17
  54.4 0.2 fusion.8
  54.7 4.5 %collective-permute-done.5 = bf16[256,256]{1,0:T(8,128)(2,1)S(1)} collective-permute-done((bf16[256,256]{1,0:T(8,128)(2,1)S(1)}, bf16[256,256]{1,0:T(8,128)(2,1)S(1)}, u32[]{:S(2)}, u32[]{:S(2)}) %collective-permute-start.5) | collective-permute-done | bytes 131104 | tf_op jit(solution)/shard_map/ppermute | solution.py:17
  59.2 0.0 collective-permute-done.7.across_ref
  59.2 1.4 %last_terms.1 = f32[128,1,256]{2,1,0:T(1,128)} custom-call(bf16[256,256]{1,0:T(8,128)(2,1)S(1)} %pad_maximum_fusion.5.turned_ref, bf16[256,256]{1,0:T(8,128)(2,1)S(1)} %get-tuple-element.50.near_1_ref, bf16[256,256]{1,0:T(8,128)(2,1)S(1)} %get-tuple-element.49.far_1_ref, bf16[256,256]{1,0:T(8,128)(2,1)S(1)} %get-tuple-element.19.near_ref, ...), custom_call_target="tpu_custom_call" | custom-call | tf_op jit(solution)/shard_map/last_terms/pallas_call | solution.py:284
  60.6 16.9 %all-to-all-start = ((f32[128,1,256]{2,1,0:T(1,128)}), f32[128,1,256]{2,1,0:T(1,128)S(1)}, u32[]{:S(2)}, u32[]{:S(2)}) async-start(f32[128,1,256]{2,1,0:T(1,128)} %last_terms.1), calls=%async_computation | async-start | bytes 262144 | tf_op jit(solution)/shard_map/all_to_all | solution.py:296
  77.5 0.0 copy-start.2
  77.5 0.2 convolution_bitcast_fusion.1
  77.7 0.7 copy-done.2
  78.4 0.7 maximum_subtract_fusion
  79.1 9.4 %all-to-all-done = f32[128,1,256]{2,1,0:T(1,128)S(1)} async-done(((f32[128,1,256]{2,1,0:T(1,128)}), f32[128,1,256]{2,1,0:T(1,128)S(1)}, u32[]{:S(2)}, u32[]{:S(2)}) %all-to-all-start) | async-done | bytes 131104 | tf_op jit(solution)/shard_map/all_to_all | solution.py:296
  88.6 0.2 reduce_sum.9
  88.7 0.5 rsqrt_multiply_fusion
  (14 shorter events, 0.4 us)
Async XLA Ops:
  1.6 10.4 %collective-permute-start = (bf16[256,256]{1,0:T(8,128)(2,1)S(1)}, bf16[256,256]{1,0:T(8,128)(2,1)S(1)}, u32[]{:S(2)}, u32[]{:S(2)}) collective-permute-start(bf16[256,256]{1,0:T(8,128)(2,1)S(1)} %first_field.1), channel_id=1, source_target_pairs={{0,1},{1,0},{2,3},{3,2},{4,5},{5,4},{6,7},{7,6},{8,9},{9,8},{10,11... | collective-permute-start | bytes 393224 | tf_op jit(solution)/shard_map/ppermute | solution.py:17
  12.3 7.6 %collective-permute-start.1 = (bf16[256,256]{1,0:T(8,128)(2,1)S(1)}, bf16[256,256]{1,0:T(8,128)(2,1)S(1)}, u32[]{:S(2)}, u32[]{:S(2)}) collective-permute-start(bf16[256,256]{1,0:T(8,128)(2,1)S(1)} %pad_maximum_fusion.1), channel_id=1, source_target_pairs={{0,2},{1,3},{2,0},{3,1},{4,6},{5,7},{6,4},{7,5},{8,10},{9,11},{10,... | collective-permute-start | bytes 393224 | tf_op jit(solution)/shard_map/ppermute | solution.py:17
  14.3 3.4 %copy-start.1 = (s32[128]{0:T(128)S(1)}, s32[128]{0:T(128)}, u32[]{:S(2)}) copy-start(s32[128]{0:T(128)} %param.10) | copy-start | bytes 1540
  14.3 19.4 %collective-permute-start.6 = (bf16[528,256]{1,0:T(8,128)(2,1)S(1)}, bf16[528,256]{1,0:T(8,128)(2,1)S(1)}, u32[]{:S(2)}, u32[]{:S(2)}) collective-permute-start(bf16[528,256]{1,0:T(8,128)(2,1)S(1)} %get-tuple-element.28), channel_id=1, source_target_pairs={{0,2},{1,3},{2,0},{3,1},{4,6},{5,7},{6,4},{7,5},{8,10},{9,11},{10,... | collective-permute-start | bytes 811016 | tf_op jit(solution)/shard_map/ppermute | solution.py:17
  20.2 10.8 %collective-permute-start.2 = (bf16[256,256]{1,0:T(8,128)(2,1)S(1)}, bf16[256,256]{1,0:T(8,128)(2,1)S(1)}, u32[]{:S(2)}, u32[]{:S(2)}) collective-permute-start(bf16[256,256]{1,0:T(8,128)(2,1)S(1)} %pad_maximum_fusion.2), channel_id=1, source_target_pairs={{0,4},{1,5},{2,6},{3,7},{4,0},{5,1},{6,2},{7,3},{8,12},{9,13},{10,... | collective-permute-start | bytes 393224 | tf_op jit(solution)/shard_map/ppermute | solution.py:17
  31.3 10.5 %collective-permute-start.3 = (bf16[256,256]{1,0:T(8,128)(2,1)S(1)}, bf16[256,256]{1,0:T(8,128)(2,1)S(1)}, u32[]{:S(2)}, u32[]{:S(2)}) collective-permute-start(bf16[256,256]{1,0:T(8,128)(2,1)S(1)} %pad_maximum_fusion.3), channel_id=1, source_target_pairs={{0,8},{1,9},{2,10},{3,11},{4,12},{5,13},{6,14},{7,15},{8,0},{9,1},... | collective-permute-start | bytes 393224 | tf_op jit(solution)/shard_map/ppermute | solution.py:17
  33.7 0.9 %copy-start = (bf16[2,128,256]{2,1,0:T(8,128)(2,1)S(1)}, bf16[2,128,256]{2,1,0:T(8,128)(2,1)}, u32[]{:S(2)}) copy-start(bf16[2,128,256]{2,1,0:T(8,128)(2,1)} %sources_ref.3) | copy-start | bytes 393220
  34.7 24.6 %collective-permute-start.7 = (bf16[512,256]{1,0:T(8,128)(2,1)S(1)}, bf16[512,256]{1,0:T(8,128)(2,1)S(1)}, u32[]{:S(2)}, u32[]{:S(2)}) collective-permute-start(bf16[512,256]{1,0:T(8,128)(2,1)S(1)} %pad_maximum_fusion), channel_id=1, source_target_pairs={{0,1},{1,0},{2,3},{3,2},{4,5},{5,4},{6,7},{7,6},{8,9},{9,8},{10,11... | collective-permute-start | bytes 786440 | tf_op jit(solution)/shard_map/ppermute | solution.py:17
  42.2 10.0 %collective-permute-start.4 = (bf16[256,256]{1,0:T(8,128)(2,1)S(1)}, bf16[256,256]{1,0:T(8,128)(2,1)S(1)}, u32[]{:S(2)}, u32[]{:S(2)}) collective-permute-start(bf16[256,256]{1,0:T(8,128)(2,1)S(1)} %convolution_convert_fusion.1), channel_id=1, source_target_pairs={{0,8},{1,9},{2,10},{3,11},{4,12},{5,13},{6,14},{7,15},{8,0},{9,1},... | collective-permute-start | bytes 393224 | tf_op jit(solution)/shard_map/ppermute | solution.py:17
  52.5 6.6 %collective-permute-start.5 = (bf16[256,256]{1,0:T(8,128)(2,1)S(1)}, bf16[256,256]{1,0:T(8,128)(2,1)S(1)}, u32[]{:S(2)}, u32[]{:S(2)}) collective-permute-start(bf16[256,256]{1,0:T(8,128)(2,1)S(1)} %convolution_convert_fusion), channel_id=1, source_target_pairs={{0,4},{1,5},{2,6},{3,7},{4,0},{5,1},{6,2},{7,3},{8,12},{9,13},{10,... | collective-permute-start | bytes 393224 | tf_op jit(solution)/shard_map/ppermute | solution.py:17
  60.6 27.9 %all-to-all-start = ((f32[128,1,256]{2,1,0:T(1,128)}), f32[128,1,256]{2,1,0:T(1,128)S(1)}, u32[]{:S(2)}, u32[]{:S(2)}) async-start(f32[128,1,256]{2,1,0:T(1,128)} %last_terms.1), calls=%async_computation | async-start | bytes 262144 | tf_op jit(solution)/shard_map/all_to_all | solution.py:296
  77.5 0.9 %copy-start.2 = (bf16[2,128,256]{2,1,0:T(8,128)(2,1)S(1)}, bf16[2,128,256]{2,1,0:T(8,128)(2,1)}, u32[]{:S(2)}) copy-start(bf16[2,128,256]{2,1,0:T(8,128)(2,1)} %observed_ref.1) | copy-start | bytes 393220

commit v4 on v3

--- a/solution.py
+++ b/solution.py
@@ -15,6 +15,13 @@
     count = lax.axis_size("bfly")
     route = [(place, place ^ 1 << stride) for place in range(count)]
     return lax.ppermute(block, "bfly", route)
+
+
+def traded(block, stride):
+    count = lax.axis_size("bfly")
+    pairs = [[low, low | 1 << stride] for low in range(count) if not low >> stride & 1]
+    both = lax.all_gather(block, "bfly", axis_index_groups=pairs)
+    return jnp.where((lax.axis_index("bfly") >> stride & 1) == 0, both[1], both[0])
 
 
 def after(values, *done):
@@ -119,15 +126,21 @@
     far_out[...] = stacked([real[:, rows:], imag[:, rows:]])
 
 
+def middle_maps(near_ref, far_ref, pattern_ref, phases_ref, near_out, far_out, waves_out):
+    near_out[...] = stacked(masked(near_ref[0], pattern_ref, 1, 0))
+    far_out[...] = stacked(masked(far_ref[0], pattern_ref, 1, 1))
+    waves_out[...] = waves(phases_ref[0], waves_out.shape[-1] // 2)
+
+
 def later_maps(
     near_ref, far_ref, pattern_ref, phases_ref, observed_ref, receivers_ref,
     near_out, far_out, waves_out, select_out, counts_out, data_out,
 ):
     rows, columns = observed_ref.shape[1:]
-    for level in range(1, 4):
-        near_out[level - 1] = stacked(masked(near_ref[level], pattern_ref, level, 0))
-        far_out[level - 1] = stacked(masked(far_ref[level], pattern_ref, level, 1))
-        waves_out[level - 1] = waves(phases_ref[level], columns)
+    for level in range(2, 4):
+        near_out[level - 2] = stacked(masked(near_ref[level - 2], pattern_ref, level, 0))
+        far_out[level - 2] = stacked(masked(far_ref[level - 2], pattern_ref, level, 1))
+        waves_out[level - 2] = waves(phases_ref[level - 2], columns)
     select = receivers_ref[...] == lax.broadcasted_iota(jnp.int32, (rows, rows), 0)
     select = select.astype(f32)
     counts = jnp.broadcast_to(jnp.sum(select, axis=1, keepdims=True), (rows, columns))
@@ -135,13 +148,13 @@
     select = select.astype(bf16)
     select_out[...] = select
     spread = jnp.concatenate([mul(select, observed_ref[0]), mul(select, observed_ref[1])])
-    cosine, sine = waves_out[2, :, :columns], waves_out[2, :, columns:]
+    cosine, sine = waves_out[1, :, :columns], waves_out[1, :, columns:]
     data_out[...] = turn_back(spread, cosine, sine)
 
 
 def last_terms(
     turned_ref, near_1_ref, far_1_ref, near_ref, far_ref, waves_ref, near_2_ref, far_2_ref,
-    waves_2_ref, sources_ref, lent_ref, across_ref, place_ref, terms_out,
+    waves_2_ref, sources_ref, lent_ref, across_ref, across_lent_ref, place_ref, terms_out,
 ):
     rows = sources_ref.shape[0] // 2
     columns = sources_ref.shape[1]
@@ -161,9 +174,9 @@
     other = turned_by(mul_t(far_1_ref[...], turned), waves_2_ref)
     terms = [
         term(sources_ref[...], near_ref, own),
-        term(across_ref[: 2 * rows], far_ref, own),
+        term(across_ref[...], far_ref, own),
         term(lent_ref[: 2 * rows], near_2_ref, other),
-        term(across_ref[2 * rows :], far_2_ref, other),
+        term(across_lent_ref[...], far_2_ref, other),
     ]
     wide = sources_ref[...].astype(f32)
     light = row_sums(wide * wide)
@@ -177,6 +190,12 @@
     terms_out[...] = jnp.concatenate([quad[None]] * n_freq).reshape(terms_out.shape)
 
 
+def last_ratio(terms_ref, gradient_out):
+    rows = gradient_out.shape[-1]
+    total = jnp.sum(terms_ref[...], axis=0)
+    gradient_out[...] = total[:, :rows] / jnp.sqrt(total[:, rows:] + epsilon)
+
+
 def in_hbm(values):
     return pltpu.with_memory_space_constraint(values, pltpu.HBM)
 
@@ -222,37 +241,59 @@
 
     partner = swapped(field, 1)
     lent = swapped(after(lend, field), 1)
+    blocks = pl.BlockSpec((1, 2, rows, rows), lambda step: (1, 0, 0, 0))
+    angles = pl.BlockSpec((1, *phases.shape[1:]), lambda step: (1, 0, 0))
+    near_1, far_1, waves_1 = pl.pallas_call(
+        middle_maps,
+        out_shape=(
+            shape((2 * rows, 2 * rows), bf16),
+            shape((2 * rows, 2 * rows), bf16),
+            shape((rows, 2 * columns), f32),
+        ),
+        grid=(1,),
+        in_specs=[blocks, blocks, VMEM, angles],
+        out_specs=(VMEM,) * 3,
+        compiler_params=pltpu.CompilerParams(vmem_limit_bytes=16 << 20),
+        name="middle_maps",
+    )(*map(in_hbm, (near_blocks, far_blocks)), after(pattern, field), in_hbm(phases))
+    cosine_1, sine_1 = waves_1[:, :columns], waves_1[:, columns:]
+    mixed = mul(near_1, field) + mul(far_1, partner)
+    field = turn(mixed, cosine_1, sine_1).astype(bf16)
+
+    partner = swapped(field, 2)
+    blocks = pl.BlockSpec((2, 2, rows, rows), lambda step: (1, 0, 0, 0))
+    angles = pl.BlockSpec((2, *phases.shape[1:]), lambda step: (1, 0, 0))
     near, far, wave, select, counts, data = pl.pallas_call(
         later_maps,
         out_shape=(
-            shape((3, 2 * rows, 2 * rows), bf16),
-            shape((3, 2 * rows, 2 * rows), bf16),
-            shape((3, rows, 2 * columns), f32),
+            shape((2, 2 * rows, 2 * rows), bf16),
+            shape((2, 2 * rows, 2 * rows), bf16),
+            shape((2, rows, 2 * columns), f32),
             shape((rows, rows), bf16),
             shape((2 * rows, columns), f32),
             shape((2 * rows, columns), f32),
         ),
-        in_specs=[VMEM] * 6,
+        grid=(1,),
+        in_specs=[blocks, blocks, VMEM, angles, VMEM, VMEM],
         out_specs=(VMEM,) * 6,
         compiler_params=pltpu.CompilerParams(vmem_limit_bytes=16 << 20),
         name="later_maps",
-    )(*map(in_hbm, (near_blocks, far_blocks, pattern, phases, observed)), after(receivers, field)[None])
-    near_1, near_2, near_3 = near
-    far_1, far_2, far_3 = far
-    (cosine_1, sine_1), (cosine_2, sine_2), (cosine_3, sine_3) = (
+    )(
+        *map(in_hbm, (near_blocks, far_blocks, pattern, phases, observed)),
+        after(receivers, field)[None],
+    )
+    near_2, near_3 = near
+    far_2, far_3 = far
+    (cosine_2, sine_2), (cosine_3, sine_3) = (
         (each[:, :columns], each[:, columns:]) for each in wave
     )
-    mixed = mul(near_1, field) + mul(far_1, partner)
-    field = turn(mixed, cosine_1, sine_1).astype(bf16)
-
-    partner = swapped(field, 2)
     mixed = mul(near_2, field) + mul(far_2, partner)
     field = turn(mixed, cosine_2, sine_2).astype(bf16)
 
     partner = swapped(field, 3)
     sources = sources.reshape(2 * rows, columns)
     lent = after(lent, field)
-    across = swapped(jnp.concatenate([sources, lent[: 2 * rows]]), 0)
+    across, across_lent = swapped(after(sources, field), 0), swapped(lent[: 2 * rows], 0)
     near_lent, far_lent, waves_lent = pl.pallas_call(
         lent_maps,
         out_shape=(
@@ -268,14 +309,15 @@
     mixed = mul(near_3, field) + mul(far_3, partner)
     turned = (counts * mixed - data).astype(bf16)
 
-    far_term = swapped(mul_t(far_3, turned).astype(bf16), 3)
+    turned = after(turned, across, across_lent, near_lent)
+    far_term = traded(mul_t(far_3, turned).astype(bf16), 3)
     last = turn(mixed, cosine_3, sine_3).astype(bf16)
     picked = jnp.stack([mul_t(select, last[:rows]), mul_t(select, last[rows:])])
     residual = picked - observed.astype(f32)
     adjoint = lax.optimization_barrier(mul_t(near_3, turned)) + far_term.astype(f32)
     turned = turn_back(adjoint, cosine_2, sine_2).astype(bf16)
 
-    far_term = swapped(mul_t(far_2, turned).astype(bf16), 2)
+    far_term = traded(mul_t(far_2, turned).astype(bf16), 2)
     adjoint = lax.optimization_barrier(mul_t(near_2, turned)) + far_term.astype(f32)
     turned = turn_back(adjoint, cosine_1, sine_1).astype(bf16)
 
@@ -284,19 +326,25 @@
     terms = pl.pallas_call(
         last_terms,
         out_shape=jax.ShapeDtypeStruct((4 * n_freq, 1, 2 * rows), f32),
-        in_specs=[VMEM] * 12 + [SMEM],
+        in_specs=[VMEM] * 13 + [SMEM],
         out_specs=VMEM,
         compiler_params=pltpu.CompilerParams(vmem_limit_bytes=16 << 20),
         name="last_terms",
-    )(*map(in_vmem, (*inputs, sources, lent, across)), (lax.axis_index("bfly") & 3)[None])
+    )(*map(in_vmem, (*inputs, sources, lent, across, across_lent)), (lax.axis_index("bfly") & 3)[None])
     groups = [
         [f * n_bfly + high + low for f in range(n_freq) for low in range(4)]
         for high in range(0, n_bfly, 4)
     ]
     terms = lax.all_to_all(terms, ("freq", "bfly"), 0, 0, axis_index_groups=groups)
-    total = jnp.sum(terms, axis=(0, 1))
-    gradient = total[:rows] / jnp.sqrt(total[rows:] + epsilon)
-    return (gradient, residual)
+    gradient = pl.pallas_call(
+        last_ratio,
+        out_shape=jax.ShapeDtypeStruct((1, rows), f32),
+        in_specs=[VMEM],
+        out_specs=VMEM,
+        compiler_params=pltpu.CompilerParams(vmem_limit_bytes=16 << 20),
+        name="last_ratio",
+    )(in_vmem(terms))
+    return (gradient[0], residual)
 
 
 def solution(mesh):

time: 89.7 us -> 88.8 us (0.990)
  blocking collectives: 0 us -> 17.9 us
  waiting for transfers between devices: 33.8 us -> 19.5 us
  starting transfers between devices: 42.4 us -> 37.1 us
  Pallas kernels: 6.33 us -> 8.12 us
    all_gather x0 -> x2, blocking collectives: none -> 17.9 us  [traded(): both = lax.all_gather(block, 'bfly', axis_index_groups=pairs)]
    ppermute x8 -> x7, waiting for transfers between devices: 24.4 us -> 10.1 us  [swapped(): return lax.ppermute(block, 'bfly', route)]
    ppermute x8 -> x7, starting transfers between devices: 25.5 us -> 22.9 us  [swapped(): return lax.ppermute(block, 'bfly', route)]
    all_to_all x1, starting transfers between devices: 16.9 us -> 14.3 us  [local(): lax.all_to_all(terms, ('freq', 'bfly'), 0, 0, axis_index_groups=groups)]
    pallas_call x1 -> x3, Pallas kernels: 2.03 us -> 3.79 us  [the longest x1 1.78 us: local(): pl.pallas_call(later_maps, out_shape=(shape((2, 2 * rows, 2 * rows), bf16...]
  transfers between devices with their start and end apart: 9 -> 8, of which waited for: 5 -> 4; matrix products, arithmetic and copies ran while one was open for 4% -> 3% of each run, Pallas kernels for 4% -> 6%
where the time goes in v4:
time: 88.8 us; the launch traced here: 88.2 us
  starting transfers between devices  37.1 us (42%)
  waiting for transfers between devices  19.5 us (22%)
  blocking collectives  17.9 us (20%)
  Pallas kernels  8.12 us (9%)
  matrix products  2.75 us (3%)
  other arithmetic  1.08 us (1%)
  between operations  1 us (1%)
    ppermute x7, starting transfers between devices, swapped(): return lax.ppermute(block, 'bfly', route)  22.9 us
    all_gather x2, blocking collectives, traded(): both = lax.all_gather(block, 'bfly', axis_index_groups=pairs)  17.9 us
    all_to_all x1, starting transfers between devices, local(): lax.all_to_all(terms, ('freq', 'bfly'), 0, 0, axis_index_groups=groups)  14.3 us
    ppermute x7, waiting for transfers between devices, swapped(): return lax.ppermute(block, 'bfly', route)  10.1 us
    all_to_all x1, waiting for transfers between devices, local(): lax.all_to_all(terms, ('freq', 'bfly'), 0, 0, axis_index_groups=groups)  9.45 us
    pallas_call x1, Pallas kernels, local(): pl.pallas_call(later_maps, out_shape=(shape((2, 2 * rows, 2 * rows), bf16...  1.78 us
  transfers between devices with their start and end apart: 8, of which 4 were waited for; matrix products, arithmetic and copies ran while one was open for 3% of the time, Pallas kernels for 6%

profile of v4, /device:TPU:1, one launch (start us, length us, event | category | flops | bytes accessed | tf_op | source)
XLA Modules:
  0.0 88.2 jit_solution(11561905730565689275)
XLA Ops:
  0.6 1.0 %first_field.1 = bf16[256,256]{1,0:T(8,128)(2,1)S(1)} custom-call(bf16[2,128,256]{2,1,0:T(8,128)(2,1)} %sources_ref.3, f32[1,128]{1,0:T(1,128)} %bitcast.59), custom_call_target="tpu_custom_call" | custom-call | tf_op jit(solution)/shard_map/first_field/pallas_call | solution.py:213
  1.6 8.8 %collective-permute-start = (bf16[256,256]{1,0:T(8,128)(2,1)S(1)}, bf16[256,256]{1,0:T(8,128)(2,1)S(1)}, u32[]{:S(2)}, u32[]{:S(2)}) collective-permute-start(bf16[256,256]{1,0:T(8,128)(2,1)S(1)} %first_field.1), channel_id=1, source_target_pairs={{0,1},{1,0},{2,3},{3,2},{4,5},{5,4},{6,7},{7,6},{8,9},{9,8},{10,11... | collective-permute-start | bytes 393224 | tf_op jit(solution)/shard_map/ppermute | solution.py:17
  10.4 1.4 %first_maps.1 = (bf16[256,256]{1,0:T(8,128)(2,1)S(1)}, bf16[256,256]{1,0:T(8,128)(2,1)S(1)}, f32[128,512]{1,0:T(8,128)S(1)}, bf16[528,256]{1,0:T(8,128)(2,1)S(1)}) custom-call(bf16[2,128,256]{2,1,0:T(8,128)(2,1)} %sources_ref.3, bf16[4,2,128,128]{3,2,1,0:T(8,128)(2,1)} %near_ref.5, bf16[4,2,128,128]{3,2,1,0:T(8,128)(2,1)} %far_ref.5, ...), custom_call_target="tpu_custom_call" | custom-call | tf_op jit(solution)/shard_map/first_maps/pallas_call | solution.py:224
  11.9 0.2 fusion.23
  12.1 0.0 collective-permute-done
  12.1 0.2 convolution_add_fusion.3
  12.3 0.0 copy-start.1
  12.4 1.9 %collective-permute-start.1 = (bf16[256,256]{1,0:T(8,128)(2,1)S(1)}, bf16[256,256]{1,0:T(8,128)(2,1)S(1)}, u32[]{:S(2)}, u32[]{:S(2)}) collective-permute-start(bf16[256,256]{1,0:T(8,128)(2,1)S(1)} %pad_maximum_fusion), channel_id=1, source_target_pairs={{0,2},{1,3},{2,0},{3,1},{4,6},{5,7},{6,4},{7,5},{8,10},{9,11},{10,... | collective-permute-start | bytes 393224 | tf_op jit(solution)/shard_map/ppermute | solution.py:17
  14.3 0.0 copy-done.1
  14.3 1.3 %middle_maps.1 = (bf16[256,256]{1,0:T(8,128)(2,1)S(1)}, bf16[256,256]{1,0:T(8,128)(2,1)S(1)}, f32[128,512]{1,0:T(8,128)S(1)}) custom-call(bf16[4,2,128,128]{3,2,1,0:T(8,128)(2,1)} %near_ref.5, bf16[4,2,128,128]{3,2,1,0:T(8,128)(2,1)} %far_ref.5, s32[2,2,2,4]{3,2,1,0:T(2,128)S(1)} %bitcast.54, f32[4,4,128]{2,1,0:T(4,128)} %bitcast.57), custom_call_target="tpu_custom_call" | custom-call | tf_op jit(solution)/shard_map/middle_maps/pallas_call | solution.py:246
  15.6 3.3 %collective-permute-start.5 = (bf16[528,256]{1,0:T(8,128)(2,1)S(1)}, bf16[528,256]{1,0:T(8,128)(2,1)S(1)}, u32[]{:S(2)}, u32[]{:S(2)}) collective-permute-start(bf16[528,256]{1,0:T(8,128)(2,1)S(1)} %get-tuple-element.39), channel_id=1, source_target_pairs={{0,2},{1,3},{2,0},{3,1},{4,6},{5,7},{6,4},{7,5},{8,10},{9,11},{10,... | collective-permute-start | bytes 811016 | tf_op jit(solution)/shard_map/ppermute | solution.py:17
  19.0 0.2 fusion.22
  19.2 0.2 collective-permute-done.1
  19.4 0.2 convolution_add_fusion.2
  19.6 0.0 copy-start.2
  19.6 1.9 %collective-permute-start.2 = (bf16[256,256]{1,0:T(8,128)(2,1)S(1)}, bf16[256,256]{1,0:T(8,128)(2,1)S(1)}, u32[]{:S(2)}, u32[]{:S(2)}) collective-permute-start(bf16[256,256]{1,0:T(8,128)(2,1)S(1)} %pad_maximum_fusion.1), channel_id=1, source_target_pairs={{0,4},{1,5},{2,6},{3,7},{4,0},{5,1},{6,2},{7,3},{8,12},{9,13},{10,... | collective-permute-start | bytes 393224 | tf_op jit(solution)/shard_map/ppermute | solution.py:17
  21.6 0.0 copy-done.2
  21.6 1.8 %later_maps.1 = (bf16[2,256,256]{2,1,0:T(8,128)(2,1)S(1)}, bf16[2,256,256]{2,1,0:T(8,128)(2,1)S(1)}, f32[2,128,512]{2,1,0:T(8,128)S(1)}, bf16[128,128]{1,0:T(8,1...) custom-call(bf16[4,2,128,128]{3,2,1,0:T(8,128)(2,1)} %near_ref.5, bf16[4,2,128,128]{3,2,1,0:T(8,128)(2,1)} %far_ref.5, ...), custom_call_target="tpu_custom_call" | custom-call | tf_op jit(solution)/shard_map/later_maps/pallas_call | solution.py:266
  23.4 0.2 fusion.10
  23.6 7.0 %collective-permute-done.2 = bf16[256,256]{1,0:T(8,128)(2,1)S(1)} collective-permute-done((bf16[256,256]{1,0:T(8,128)(2,1)S(1)}, bf16[256,256]{1,0:T(8,128)(2,1)S(1)}, u32[]{:S(2)}, u32[]{:S(2)}) %collective-permute-start.2) | collective-permute-done | bytes 131104 | tf_op jit(solution)/shard_map/ppermute | solution.py:17
  30.6 0.2 convolution_add_fusion.1
  30.8 0.1 subtract_convert_fusion.4
  30.8 0.0 copy-start
  30.9 2.1 %collective-permute-start.3 = (bf16[256,256]{1,0:T(8,128)(2,1)S(1)}, bf16[256,256]{1,0:T(8,128)(2,1)S(1)}, u32[]{:S(2)}, u32[]{:S(2)}) collective-permute-start(bf16[256,256]{1,0:T(8,128)(2,1)S(1)} %pad_maximum_fusion.2), channel_id=1, source_target_pairs={{0,8},{1,9},{2,10},{3,11},{4,12},{5,13},{6,14},{7,15},{8,0},{9,1},... | collective-permute-start | bytes 393224 | tf_op jit(solution)/shard_map/ppermute | solution.py:17
  32.9 2.9 %collective-permute-start.4 = (bf16[256,256]{1,0:T(8,128)(2,1)S(1)}, bf16[256,256]{1,0:T(8,128)(2,1)S(1)}, u32[]{:S(2)}, u32[]{:S(2)}) collective-permute-start(bf16[256,256]{1,0:T(8,128)(2,1)S(1)} %bitcast.50), channel_id=1, source_target_pairs={{0,1},{1,0},{2,3},{3,2},{4,5},{5,4},{6,7},{7,6},{8,9},{9,8},{10,11... | collective-permute-start | bytes 393224 | tf_op jit(solution)/shard_map/ppermute | solution.py:17
  35.9 0.2 fusion.6
  36.1 0.0 collective-permute-done.5.lent_ref
  36.1 0.5 lent_maps.1
  36.6 1.9 %collective-permute-start.6 = (bf16[256,256]{1,0:T(8,128)(2,1)S(1)}, bf16[256,256]{1,0:T(8,128)(2,1)S(1)}, u32[]{:S(2)}, u32[]{:S(2)}) collective-permute-start(bf16[256,256]{1,0:T(8,128)(2,1)S(1)} %slice.93), channel_id=1, source_target_pairs={{0,1},{1,0},{2,3},{3,2},{4,5},{5,4},{6,7},{7,6},{8,9},{9,8},{10,11... | collective-permute-start | bytes 393224 | tf_op jit(solution)/shard_map/ppermute | solution.py:17
  38.5 2.9 %collective-permute-done.3 = bf16[256,256]{1,0:T(8,128)(2,1)S(1)} collective-permute-done((bf16[256,256]{1,0:T(8,128)(2,1)S(1)}, bf16[256,256]{1,0:T(8,128)(2,1)S(1)}, u32[]{:S(2)}, u32[]{:S(2)}) %collective-permute-start.3) | collective-permute-done | bytes 131104 | tf_op jit(solution)/shard_map/ppermute | solution.py:17
  41.4 0.2 subtract_convert_fusion
  41.6 0.2 convolution_bitcast_fusion.1
  41.8 0.0 collective-permute-done.4.across_ref
  41.8 0.0 collective-permute-done.6.across_lent_ref
  41.8 0.2 convolution_convert_fusion.1
  42.0 0.2 fusion.4
  42.2 10.6 %all-gather = bf16[512,256]{1,0:T(8,128)(2,1)S(1)} all-gather(bf16[256,256]{1,0:T(8,128)(2,1)S(1)} %convolution_convert_fusion.1), channel_id=2, replica_groups={{0,8},{1,9},{2,10},{3,11},{4,12},{5,13},{6,14},{7,15},{16,24},{17,25},{..., dimensions={0}, use_global_device_ids=true | all-gather | bytes 393216 | tf_op jit(solution)/shard_map/all_gather | solution.py:23
  52.9 0.2 convolution_convert_fusion
  53.2 0.2 fusion.8
  53.4 7.3 %all-gather.1 = bf16[512,256]{1,0:T(8,128)(2,1)S(1)} all-gather(bf16[256,256]{1,0:T(8,128)(2,1)S(1)} %convolution_convert_fusion), channel_id=3, replica_groups={{0,4},{1,5},{2,6},{3,7},{8,12},{9,13},{10,14},{11,15},{16,20},{17,21},{..., dimensions={0}, use_global_device_ids=true | all-gather | bytes 393216 | tf_op jit(solution)/shard_map/all_gather | solution.py:23
  60.8 1.4 %last_terms.1 = f32[128,1,256]{2,1,0:T(1,128)} custom-call(bf16[256,256]{1,0:T(8,128)(2,1)S(1)} %pad_maximum_fusion.4.turned_ref, bf16[256,256]{1,0:T(8,128)(2,1)S(1)} %get-tuple-element.29.near_1_ref, bf16[256,256]{1,0:T(8,128)(2,1)S(1)} %get-tuple-element.30.far_1_ref, bf16[256,256]{1,0:T(8,128)(2,1)S(1)} %get-tuple-element.25.near_ref, ...), custom_call_target="tpu_custom_call" | custom-call | tf_op jit(solution)/shard_map/last_terms/pallas_call | solution.py:326
  62.2 14.3 %all-to-all-start = ((f32[128,1,256]{2,1,0:T(1,128)}), f32[128,1,256]{2,1,0:T(1,128)S(1)}, u32[]{:S(2)}, u32[]{:S(2)}) async-start(f32[128,1,256]{2,1,0:T(1,128)} %last_terms.1), calls=%async_computation | async-start | bytes 262144 | tf_op jit(solution)/shard_map/all_to_all | solution.py:338
  76.5 0.0 copy-start.3
  76.5 0.2 convolution_bitcast_fusion
  76.7 0.7 copy-done.3
  77.4 0.7 maximum_subtract_fusion
  78.1 9.5 %all-to-all-done.terms_ref = f32[128,1,256]{2,1,0:T(1,128)S(1)} async-done(((f32[128,1,256]{2,1,0:T(1,128)}), f32[128,1,256]{2,1,0:T(1,128)S(1)}, u32[]{:S(2)}, u32[]{:S(2)}) %all-to-all-start) | async-done | bytes 131104 | tf_op jit(solution)/shard_map/all_to_all | solution.py:338
  87.6 0.7 last_ratio.1
  (13 shorter events, 0.3 us)
Async XLA Ops:
  1.6 10.4 %collective-permute-start = (bf16[256,256]{1,0:T(8,128)(2,1)S(1)}, bf16[256,256]{1,0:T(8,128)(2,1)S(1)}, u32[]{:S(2)}, u32[]{:S(2)}) collective-permute-start(bf16[256,256]{1,0:T(8,128)(2,1)S(1)} %first_field.1), channel_id=1, source_target_pairs={{0,1},{1,0},{2,3},{3,2},{4,5},{5,4},{6,7},{7,6},{8,9},{9,8},{10,11... | collective-permute-start | bytes 393224 | tf_op jit(solution)/shard_map/ppermute | solution.py:17
  12.3 2.0 %copy-start.1 = (s32[4,2,2,2]{0,3,2,1:T(2,128)S(1)}, s32[4,2,2,2]{0,3,2,1:T(2,128)}, u32[]{:S(2)}) copy-start(s32[4,2,2,2]{0,3,2,1:T(2,128)} %param.15) | copy-start | bytes 388
  12.4 7.0 %collective-permute-start.1 = (bf16[256,256]{1,0:T(8,128)(2,1)S(1)}, bf16[256,256]{1,0:T(8,128)(2,1)S(1)}, u32[]{:S(2)}, u32[]{:S(2)}) collective-permute-start(bf16[256,256]{1,0:T(8,128)(2,1)S(1)} %pad_maximum_fusion), channel_id=1, source_target_pairs={{0,2},{1,3},{2,0},{3,1},{4,6},{5,7},{6,4},{7,5},{8,10},{9,11},{10,... | collective-permute-start | bytes 393224 | tf_op jit(solution)/shard_map/ppermute | solution.py:17
  15.6 20.4 %collective-permute-start.5 = (bf16[528,256]{1,0:T(8,128)(2,1)S(1)}, bf16[528,256]{1,0:T(8,128)(2,1)S(1)}, u32[]{:S(2)}, u32[]{:S(2)}) collective-permute-start(bf16[528,256]{1,0:T(8,128)(2,1)S(1)} %get-tuple-element.39), channel_id=1, source_target_pairs={{0,2},{1,3},{2,0},{3,1},{4,6},{5,7},{6,4},{7,5},{8,10},{9,11},{10,... | collective-permute-start | bytes 811016 | tf_op jit(solution)/shard_map/ppermute | solution.py:17
  19.6 1.9 %copy-start.2 = (s32[128]{0:T(128)S(1)}, s32[128]{0:T(128)}, u32[]{:S(2)}) copy-start(s32[128]{0:T(128)} %param.10) | copy-start | bytes 1540
  19.6 11.0 %collective-permute-start.2 = (bf16[256,256]{1,0:T(8,128)(2,1)S(1)}, bf16[256,256]{1,0:T(8,128)(2,1)S(1)}, u32[]{:S(2)}, u32[]{:S(2)}) collective-permute-start(bf16[256,256]{1,0:T(8,128)(2,1)S(1)} %pad_maximum_fusion.1), channel_id=1, source_target_pairs={{0,4},{1,5},{2,6},{3,7},{4,0},{5,1},{6,2},{7,3},{8,12},{9,13},{10,... | collective-permute-start | bytes 393224 | tf_op jit(solution)/shard_map/ppermute | solution.py:17
  30.8 2.1 %copy-start = (bf16[2,128,256]{2,1,0:T(8,128)(2,1)S(1)}, bf16[2,128,256]{2,1,0:T(8,128)(2,1)}, u32[]{:S(2)}) copy-start(bf16[2,128,256]{2,1,0:T(8,128)(2,1)} %sources_ref.3) | copy-start | bytes 393220
  30.9 10.5 %collective-permute-start.3 = (bf16[256,256]{1,0:T(8,128)(2,1)S(1)}, bf16[256,256]{1,0:T(8,128)(2,1)S(1)}, u32[]{:S(2)}, u32[]{:S(2)}) collective-permute-start(bf16[256,256]{1,0:T(8,128)(2,1)S(1)} %pad_maximum_fusion.2), channel_id=1, source_target_pairs={{0,8},{1,9},{2,10},{3,11},{4,12},{5,13},{6,14},{7,15},{8,0},{9,1},... | collective-permute-start | bytes 393224 | tf_op jit(solution)/shard_map/ppermute | solution.py:17
  32.9 8.8 %collective-permute-start.4 = (bf16[256,256]{1,0:T(8,128)(2,1)S(1)}, bf16[256,256]{1,0:T(8,128)(2,1)S(1)}, u32[]{:S(2)}, u32[]{:S(2)}) collective-permute-start(bf16[256,256]{1,0:T(8,128)(2,1)S(1)} %bitcast.50), channel_id=1, source_target_pairs={{0,1},{1,0},{2,3},{3,2},{4,5},{5,4},{6,7},{7,6},{8,9},{9,8},{10,11... | collective-permute-start | bytes 393224 | tf_op jit(solution)/shard_map/ppermute | solution.py:17
  36.6 5.2 %collective-permute-start.6 = (bf16[256,256]{1,0:T(8,128)(2,1)S(1)}, bf16[256,256]{1,0:T(8,128)(2,1)S(1)}, u32[]{:S(2)}, u32[]{:S(2)}) collective-permute-start(bf16[256,256]{1,0:T(8,128)(2,1)S(1)} %slice.93), channel_id=1, source_target_pairs={{0,1},{1,0},{2,3},{3,2},{4,5},{5,4},{6,7},{7,6},{8,9},{9,8},{10,11... | collective-permute-start | bytes 393224 | tf_op jit(solution)/shard_map/ppermute | solution.py:17
  62.2 25.4 %all-to-all-start = ((f32[128,1,256]{2,1,0:T(1,128)}), f32[128,1,256]{2,1,0:T(1,128)S(1)}, u32[]{:S(2)}, u32[]{:S(2)}) async-start(f32[128,1,256]{2,1,0:T(1,128)} %last_terms.1), calls=%async_computation | async-start | bytes 262144 | tf_op jit(solution)/shard_map/all_to_all | solution.py:338
  76.5 0.9 %copy-start.3 = (bf16[2,128,256]{2,1,0:T(8,128)(2,1)S(1)}, bf16[2,128,256]{2,1,0:T(8,128)(2,1)}, u32[]{:S(2)}) copy-start(bf16[2,128,256]{2,1,0:T(8,128)(2,1)} %observed_ref.1) | copy-start | bytes 393220

commit v5 on v4

--- a/solution.py
+++ b/solution.py
@@ -161,6 +161,7 @@
 
     def row_sums(product):
         total = product[:rows] + product[rows:]
+        total = total[:, : columns // 2] + total[:, columns // 2 :]
         return jnp.sum(total.T, axis=0, keepdims=True)
 
     def term(sources, maps_ref, turned):
@@ -325,7 +326,7 @@
     inputs = (turned, near_1, far_1, near_0, far_0, waves_0, near_lent, far_lent, waves_lent)
     terms = pl.pallas_call(
         last_terms,
-        out_shape=jax.ShapeDtypeStruct((4 * n_freq, 1, 2 * rows), f32),
+        out_shape=shape((4 * n_freq, 1, 2 * rows), f32),
         in_specs=[VMEM] * 13 + [SMEM],
         out_specs=VMEM,
         compiler_params=pltpu.CompilerParams(vmem_limit_bytes=16 << 20),

time: 88.8 us -> 88.7 us (level)
  no operation moved by 1% of the time
where the time goes in v5:
time: 88.7 us; the launch traced here: 88.2 us
  starting transfers between devices  37.1 us (42%)
  waiting for transfers between devices  19.5 us (22%)
  blocking collectives  17.9 us (20%)
  Pallas kernels  8.08 us (9%)
  matrix products  2.75 us (3%)
  other arithmetic  1.08 us (1%)
  between operations  1 us (1%)
    ppermute x7, starting transfers between devices, swapped(): return lax.ppermute(block, 'bfly', route)  22.9 us
    all_gather x2, blocking collectives, traded(): both = lax.all_gather(block, 'bfly', axis_index_groups=pairs)  17.9 us
    all_to_all x1, starting transfers between devices, local(): lax.all_to_all(terms, ('freq', 'bfly'), 0, 0, axis_index_groups=groups)  14.3 us
    ppermute x7, waiting for transfers between devices, swapped(): return lax.ppermute(block, 'bfly', route)  10.1 us
    all_to_all x1, waiting for transfers between devices, local(): lax.all_to_all(terms, ('freq', 'bfly'), 0, 0, axis_index_groups=groups)  9.45 us
    pallas_call x1, Pallas kernels, local(): pl.pallas_call(later_maps, out_shape=(shape((2, 2 * rows, 2 * rows), bf16...  1.78 us
  transfers between devices with their start and end apart: 8, of which 4 were waited for; matrix products, arithmetic and copies ran while one was open for 3% of the time, Pallas kernels for 6%

profile of v5, /device:TPU:1, one launch (start us, length us, event | category | flops | bytes accessed | tf_op | source)
XLA Modules:
  0.0 88.2 jit_solution(14928145260325455793)
XLA Ops:
  0.6 1.0 %first_field.1 = bf16[256,256]{1,0:T(8,128)(2,1)S(1)} custom-call(bf16[2,128,256]{2,1,0:T(8,128)(2,1)} %sources_ref.3, f32[1,128]{1,0:T(1,128)} %bitcast.59), custom_call_target="tpu_custom_call" | custom-call | tf_op jit(solution)/shard_map/first_field/pallas_call | solution.py:214
  1.6 8.8 %collective-permute-start = (bf16[256,256]{1,0:T(8,128)(2,1)S(1)}, bf16[256,256]{1,0:T(8,128)(2,1)S(1)}, u32[]{:S(2)}, u32[]{:S(2)}) collective-permute-start(bf16[256,256]{1,0:T(8,128)(2,1)S(1)} %first_field.1), channel_id=1, source_target_pairs={{0,1},{1,0},{2,3},{3,2},{4,5},{5,4},{6,7},{7,6},{8,9},{9,8},{10,11... | collective-permute-start | bytes 393224 | tf_op jit(solution)/shard_map/ppermute | solution.py:17
  10.4 1.4 %first_maps.1 = (bf16[256,256]{1,0:T(8,128)(2,1)S(1)}, bf16[256,256]{1,0:T(8,128)(2,1)S(1)}, f32[128,512]{1,0:T(8,128)S(1)}, bf16[528,256]{1,0:T(8,128)(2,1)S(1)}) custom-call(bf16[2,128,256]{2,1,0:T(8,128)(2,1)} %sources_ref.3, bf16[4,2,128,128]{3,2,1,0:T(8,128)(2,1)} %near_ref.5, bf16[4,2,128,128]{3,2,1,0:T(8,128)(2,1)} %far_ref.5, ...), custom_call_target="tpu_custom_call" | custom-call | tf_op jit(solution)/shard_map/first_maps/pallas_call | solution.py:225
  11.9 0.2 fusion.23
  12.1 0.0 collective-permute-done
  12.1 0.2 convolution_add_fusion.3
  12.3 0.0 copy-start.1
  12.4 1.9 %collective-permute-start.1 = (bf16[256,256]{1,0:T(8,128)(2,1)S(1)}, bf16[256,256]{1,0:T(8,128)(2,1)S(1)}, u32[]{:S(2)}, u32[]{:S(2)}) collective-permute-start(bf16[256,256]{1,0:T(8,128)(2,1)S(1)} %pad_maximum_fusion), channel_id=1, source_target_pairs={{0,2},{1,3},{2,0},{3,1},{4,6},{5,7},{6,4},{7,5},{8,10},{9,11},{10,... | collective-permute-start | bytes 393224 | tf_op jit(solution)/shard_map/ppermute | solution.py:17
  14.3 0.0 copy-done.1
  14.3 1.3 %middle_maps.1 = (bf16[256,256]{1,0:T(8,128)(2,1)S(1)}, bf16[256,256]{1,0:T(8,128)(2,1)S(1)}, f32[128,512]{1,0:T(8,128)S(1)}) custom-call(bf16[4,2,128,128]{3,2,1,0:T(8,128)(2,1)} %near_ref.5, bf16[4,2,128,128]{3,2,1,0:T(8,128)(2,1)} %far_ref.5, s32[2,2,2,4]{3,2,1,0:T(2,128)S(1)} %bitcast.54, f32[4,4,128]{2,1,0:T(4,128)} %bitcast.57), custom_call_target="tpu_custom_call" | custom-call | tf_op jit(solution)/shard_map/middle_maps/pallas_call | solution.py:247
  15.6 3.3 %collective-permute-start.5 = (bf16[528,256]{1,0:T(8,128)(2,1)S(1)}, bf16[528,256]{1,0:T(8,128)(2,1)S(1)}, u32[]{:S(2)}, u32[]{:S(2)}) collective-permute-start(bf16[528,256]{1,0:T(8,128)(2,1)S(1)} %get-tuple-element.39), channel_id=1, source_target_pairs={{0,2},{1,3},{2,0},{3,1},{4,6},{5,7},{6,4},{7,5},{8,10},{9,11},{10,... | collective-permute-start | bytes 811016 | tf_op jit(solution)/shard_map/ppermute | solution.py:17
  19.0 0.2 fusion.22
  19.2 0.2 collective-permute-done.1
  19.4 0.2 convolution_add_fusion.2
  19.6 0.0 copy-start.2
  19.6 1.9 %collective-permute-start.2 = (bf16[256,256]{1,0:T(8,128)(2,1)S(1)}, bf16[256,256]{1,0:T(8,128)(2,1)S(1)}, u32[]{:S(2)}, u32[]{:S(2)}) collective-permute-start(bf16[256,256]{1,0:T(8,128)(2,1)S(1)} %pad_maximum_fusion.1), channel_id=1, source_target_pairs={{0,4},{1,5},{2,6},{3,7},{4,0},{5,1},{6,2},{7,3},{8,12},{9,13},{10,... | collective-permute-start | bytes 393224 | tf_op jit(solution)/shard_map/ppermute | solution.py:17
  21.6 0.0 copy-done.2
  21.6 1.8 %later_maps.1 = (bf16[2,256,256]{2,1,0:T(8,128)(2,1)S(1)}, bf16[2,256,256]{2,1,0:T(8,128)(2,1)S(1)}, f32[2,128,512]{2,1,0:T(8,128)S(1)}, bf16[128,128]{1,0:T(8,1...) custom-call(bf16[4,2,128,128]{3,2,1,0:T(8,128)(2,1)} %near_ref.5, bf16[4,2,128,128]{3,2,1,0:T(8,128)(2,1)} %far_ref.5, ...), custom_call_target="tpu_custom_call" | custom-call | tf_op jit(solution)/shard_map/later_maps/pallas_call | solution.py:267
  23.4 0.2 fusion.10
  23.6 7.0 %collective-permute-done.2 = bf16[256,256]{1,0:T(8,128)(2,1)S(1)} collective-permute-done((bf16[256,256]{1,0:T(8,128)(2,1)S(1)}, bf16[256,256]{1,0:T(8,128)(2,1)S(1)}, u32[]{:S(2)}, u32[]{:S(2)}) %collective-permute-start.2) | collective-permute-done | bytes 131104 | tf_op jit(solution)/shard_map/ppermute | solution.py:17
  30.6 0.2 convolution_add_fusion.1
  30.8 0.1 subtract_convert_fusion.4
  30.8 0.0 copy-start
  30.9 2.1 %collective-permute-start.3 = (bf16[256,256]{1,0:T(8,128)(2,1)S(1)}, bf16[256,256]{1,0:T(8,128)(2,1)S(1)}, u32[]{:S(2)}, u32[]{:S(2)}) collective-permute-start(bf16[256,256]{1,0:T(8,128)(2,1)S(1)} %pad_maximum_fusion.2), channel_id=1, source_target_pairs={{0,8},{1,9},{2,10},{3,11},{4,12},{5,13},{6,14},{7,15},{8,0},{9,1},... | collective-permute-start | bytes 393224 | tf_op jit(solution)/shard_map/ppermute | solution.py:17
  32.9 2.9 %collective-permute-start.4 = (bf16[256,256]{1,0:T(8,128)(2,1)S(1)}, bf16[256,256]{1,0:T(8,128)(2,1)S(1)}, u32[]{:S(2)}, u32[]{:S(2)}) collective-permute-start(bf16[256,256]{1,0:T(8,128)(2,1)S(1)} %bitcast.50), channel_id=1, source_target_pairs={{0,1},{1,0},{2,3},{3,2},{4,5},{5,4},{6,7},{7,6},{8,9},{9,8},{10,11... | collective-permute-start | bytes 393224 | tf_op jit(solution)/shard_map/ppermute | solution.py:17
  35.9 0.2 fusion.6
  36.1 0.0 collective-permute-done.5.lent_ref
  36.1 0.5 lent_maps.1
  36.6 1.9 %collective-permute-start.6 = (bf16[256,256]{1,0:T(8,128)(2,1)S(1)}, bf16[256,256]{1,0:T(8,128)(2,1)S(1)}, u32[]{:S(2)}, u32[]{:S(2)}) collective-permute-start(bf16[256,256]{1,0:T(8,128)(2,1)S(1)} %slice.93), channel_id=1, source_target_pairs={{0,1},{1,0},{2,3},{3,2},{4,5},{5,4},{6,7},{7,6},{8,9},{9,8},{10,11... | collective-permute-start | bytes 393224 | tf_op jit(solution)/shard_map/ppermute | solution.py:17
  38.5 2.9 %collective-permute-done.3 = bf16[256,256]{1,0:T(8,128)(2,1)S(1)} collective-permute-done((bf16[256,256]{1,0:T(8,128)(2,1)S(1)}, bf16[256,256]{1,0:T(8,128)(2,1)S(1)}, u32[]{:S(2)}, u32[]{:S(2)}) %collective-permute-start.3) | collective-permute-done | bytes 131104 | tf_op jit(solution)/shard_map/ppermute | solution.py:17
  41.4 0.2 subtract_convert_fusion
  41.6 0.2 convolution_bitcast_fusion.1
  41.8 0.0 collective-permute-done.4.across_ref
  41.8 0.0 collective-permute-done.6.across_lent_ref
  41.8 0.2 convolution_convert_fusion.1
  42.0 0.2 fusion.4
  42.2 10.6 %all-gather = bf16[512,256]{1,0:T(8,128)(2,1)S(1)} all-gather(bf16[256,256]{1,0:T(8,128)(2,1)S(1)} %convolution_convert_fusion.1), channel_id=2, replica_groups={{0,8},{1,9},{2,10},{3,11},{4,12},{5,13},{6,14},{7,15},{16,24},{17,25},{..., dimensions={0}, use_global_device_ids=true | all-gather | bytes 393216 | tf_op jit(solution)/shard_map/all_gather | solution.py:23
  52.9 0.2 convolution_convert_fusion
  53.2 0.2 fusion.8
  53.4 7.3 %all-gather.1 = bf16[512,256]{1,0:T(8,128)(2,1)S(1)} all-gather(bf16[256,256]{1,0:T(8,128)(2,1)S(1)} %convolution_convert_fusion), channel_id=3, replica_groups={{0,4},{1,5},{2,6},{3,7},{8,12},{9,13},{10,14},{11,15},{16,20},{17,21},{..., dimensions={0}, use_global_device_ids=true | all-gather | bytes 393216 | tf_op jit(solution)/shard_map/all_gather | solution.py:23
  60.8 1.4 %last_terms.1 = f32[128,1,256]{2,1,0:T(1,128)} custom-call(bf16[256,256]{1,0:T(8,128)(2,1)S(1)} %pad_maximum_fusion.4.turned_ref, bf16[256,256]{1,0:T(8,128)(2,1)S(1)} %get-tuple-element.29.near_1_ref, bf16[256,256]{1,0:T(8,128)(2,1)S(1)} %get-tuple-element.30.far_1_ref, bf16[256,256]{1,0:T(8,128)(2,1)S(1)} %get-tuple-element.25.near_ref, ...), custom_call_target="tpu_custom_call" | custom-call | tf_op jit(solution)/shard_map/last_terms/pallas_call | solution.py:327
  62.2 14.3 %all-to-all-start = ((f32[128,1,256]{2,1,0:T(1,128)}), f32[128,1,256]{2,1,0:T(1,128)S(1)}, u32[]{:S(2)}, u32[]{:S(2)}) async-start(f32[128,1,256]{2,1,0:T(1,128)} %last_terms.1), calls=%async_computation | async-start | bytes 262144 | tf_op jit(solution)/shard_map/all_to_all | solution.py:339
  76.4 0.0 copy-start.3
  76.5 0.2 convolution_bitcast_fusion
  76.6 0.7 copy-done.3
  77.4 0.7 maximum_subtract_fusion
  78.1 9.5 %all-to-all-done.terms_ref = f32[128,1,256]{2,1,0:T(1,128)S(1)} async-done(((f32[128,1,256]{2,1,0:T(1,128)}), f32[128,1,256]{2,1,0:T(1,128)S(1)}, u32[]{:S(2)}, u32[]{:S(2)}) %all-to-all-start) | async-done | bytes 131104 | tf_op jit(solution)/shard_map/all_to_all | solution.py:339
  87.5 0.7 last_ratio.1
  (13 shorter events, 0.3 us)
Async XLA Ops:
  1.6 10.4 %collective-permute-start = (bf16[256,256]{1,0:T(8,128)(2,1)S(1)}, bf16[256,256]{1,0:T(8,128)(2,1)S(1)}, u32[]{:S(2)}, u32[]{:S(2)}) collective-permute-start(bf16[256,256]{1,0:T(8,128)(2,1)S(1)} %first_field.1), channel_id=1, source_target_pairs={{0,1},{1,0},{2,3},{3,2},{4,5},{5,4},{6,7},{7,6},{8,9},{9,8},{10,11... | collective-permute-start | bytes 393224 | tf_op jit(solution)/shard_map/ppermute | solution.py:17
  12.3 2.0 %copy-start.1 = (s32[4,2,2,2]{0,3,2,1:T(2,128)S(1)}, s32[4,2,2,2]{0,3,2,1:T(2,128)}, u32[]{:S(2)}) copy-start(s32[4,2,2,2]{0,3,2,1:T(2,128)} %param.15) | copy-start | bytes 388
  12.4 7.0 %collective-permute-start.1 = (bf16[256,256]{1,0:T(8,128)(2,1)S(1)}, bf16[256,256]{1,0:T(8,128)(2,1)S(1)}, u32[]{:S(2)}, u32[]{:S(2)}) collective-permute-start(bf16[256,256]{1,0:T(8,128)(2,1)S(1)} %pad_maximum_fusion), channel_id=1, source_target_pairs={{0,2},{1,3},{2,0},{3,1},{4,6},{5,7},{6,4},{7,5},{8,10},{9,11},{10,... | collective-permute-start | bytes 393224 | tf_op jit(solution)/shard_map/ppermute | solution.py:17
  15.6 20.4 %collective-permute-start.5 = (bf16[528,256]{1,0:T(8,128)(2,1)S(1)}, bf16[528,256]{1,0:T(8,128)(2,1)S(1)}, u32[]{:S(2)}, u32[]{:S(2)}) collective-permute-start(bf16[528,256]{1,0:T(8,128)(2,1)S(1)} %get-tuple-element.39), channel_id=1, source_target_pairs={{0,2},{1,3},{2,0},{3,1},{4,6},{5,7},{6,4},{7,5},{8,10},{9,11},{10,... | collective-permute-start | bytes 811016 | tf_op jit(solution)/shard_map/ppermute | solution.py:17
  19.6 1.9 %copy-start.2 = (s32[128]{0:T(128)S(1)}, s32[128]{0:T(128)}, u32[]{:S(2)}) copy-start(s32[128]{0:T(128)} %param.10) | copy-start | bytes 1540
  19.6 11.0 %collective-permute-start.2 = (bf16[256,256]{1,0:T(8,128)(2,1)S(1)}, bf16[256,256]{1,0:T(8,128)(2,1)S(1)}, u32[]{:S(2)}, u32[]{:S(2)}) collective-permute-start(bf16[256,256]{1,0:T(8,128)(2,1)S(1)} %pad_maximum_fusion.1), channel_id=1, source_target_pairs={{0,4},{1,5},{2,6},{3,7},{4,0},{5,1},{6,2},{7,3},{8,12},{9,13},{10,... | collective-permute-start | bytes 393224 | tf_op jit(solution)/shard_map/ppermute | solution.py:17
  30.8 2.1 %copy-start = (bf16[2,128,256]{2,1,0:T(8,128)(2,1)S(1)}, bf16[2,128,256]{2,1,0:T(8,128)(2,1)}, u32[]{:S(2)}) copy-start(bf16[2,128,256]{2,1,0:T(8,128)(2,1)} %sources_ref.3) | copy-start | bytes 393220
  30.9 10.5 %collective-permute-start.3 = (bf16[256,256]{1,0:T(8,128)(2,1)S(1)}, bf16[256,256]{1,0:T(8,128)(2,1)S(1)}, u32[]{:S(2)}, u32[]{:S(2)}) collective-permute-start(bf16[256,256]{1,0:T(8,128)(2,1)S(1)} %pad_maximum_fusion.2), channel_id=1, source_target_pairs={{0,8},{1,9},{2,10},{3,11},{4,12},{5,13},{6,14},{7,15},{8,0},{9,1},... | collective-permute-start | bytes 393224 | tf_op jit(solution)/shard_map/ppermute | solution.py:17
  32.9 8.8 %collective-permute-start.4 = (bf16[256,256]{1,0:T(8,128)(2,1)S(1)}, bf16[256,256]{1,0:T(8,128)(2,1)S(1)}, u32[]{:S(2)}, u32[]{:S(2)}) collective-permute-start(bf16[256,256]{1,0:T(8,128)(2,1)S(1)} %bitcast.50), channel_id=1, source_target_pairs={{0,1},{1,0},{2,3},{3,2},{4,5},{5,4},{6,7},{7,6},{8,9},{9,8},{10,11... | collective-permute-start | bytes 393224 | tf_op jit(solution)/shard_map/ppermute | solution.py:17
  36.6 5.2 %collective-permute-start.6 = (bf16[256,256]{1,0:T(8,128)(2,1)S(1)}, bf16[256,256]{1,0:T(8,128)(2,1)S(1)}, u32[]{:S(2)}, u32[]{:S(2)}) collective-permute-start(bf16[256,256]{1,0:T(8,128)(2,1)S(1)} %slice.93), channel_id=1, source_target_pairs={{0,1},{1,0},{2,3},{3,2},{4,5},{5,4},{6,7},{7,6},{8,9},{9,8},{10,11... | collective-permute-start | bytes 393224 | tf_op jit(solution)/shard_map/ppermute | solution.py:17
  62.2 25.4 %all-to-all-start = ((f32[128,1,256]{2,1,0:T(1,128)}), f32[128,1,256]{2,1,0:T(1,128)S(1)}, u32[]{:S(2)}, u32[]{:S(2)}) async-start(f32[128,1,256]{2,1,0:T(1,128)} %last_terms.1), calls=%async_computation | async-start | bytes 262144 | tf_op jit(solution)/shard_map/all_to_all | solution.py:339
  76.4 0.9 %copy-start.3 = (bf16[2,128,256]{2,1,0:T(8,128)(2,1)S(1)}, bf16[2,128,256]{2,1,0:T(8,128)(2,1)}, u32[]{:S(2)}) copy-start(bf16[2,128,256]{2,1,0:T(8,128)(2,1)} %observed_ref.1) | copy-start | bytes 393220

commit v6 on v5

--- a/solution.py
+++ b/solution.py
@@ -134,12 +134,13 @@
 
 def later_maps(
     near_ref, far_ref, pattern_ref, phases_ref, observed_ref, receivers_ref,
-    near_out, far_out, waves_out, select_out, counts_out, data_out,
+    near_out, far_out, wide_out, waves_out, select_out, counts_out, data_out,
 ):
     rows, columns = observed_ref.shape[1:]
     for level in range(2, 4):
         near_out[level - 2] = stacked(masked(near_ref[level - 2], pattern_ref, level, 0))
         far_out[level - 2] = stacked(masked(far_ref[level - 2], pattern_ref, level, 1))
+        wide_out[level - 2] = jnp.concatenate([far_out[level - 2], near_out[level - 2]], axis=1)
         waves_out[level - 2] = waves(phases_ref[level - 2], columns)
     select = receivers_ref[...] == lax.broadcasted_iota(jnp.int32, (rows, rows), 0)
     select = select.astype(f32)
@@ -264,11 +265,12 @@
     partner = swapped(field, 2)
     blocks = pl.BlockSpec((2, 2, rows, rows), lambda step: (1, 0, 0, 0))
     angles = pl.BlockSpec((2, *phases.shape[1:]), lambda step: (1, 0, 0))
-    near, far, wave, select, counts, data = pl.pallas_call(
+    near, far, wide, wave, select, counts, data = pl.pallas_call(
         later_maps,
         out_shape=(
             shape((2, 2 * rows, 2 * rows), bf16),
             shape((2, 2 * rows, 2 * rows), bf16),
+            shape((2, 2 * rows, 4 * rows), bf16),
             shape((2, rows, 2 * columns), f32),
             shape((rows, rows), bf16),
             shape((2 * rows, columns), f32),
@@ -276,7 +278,7 @@
         ),
         grid=(1,),
         in_specs=[blocks, blocks, VMEM, angles, VMEM, VMEM],
-        out_specs=(VMEM,) * 6,
+        out_specs=(VMEM,) * 7,
         compiler_params=pltpu.CompilerParams(vmem_limit_bytes=16 << 20),
         name="later_maps",
     )(
@@ -311,15 +313,17 @@
     turned = (counts * mixed - data).astype(bf16)
 
     turned = after(turned, across, across_lent, near_lent)
-    far_term = traded(mul_t(far_3, turned).astype(bf16), 3)
+    both = lax.optimization_barrier(mul_t(wide[1], turned))
+    far_term = traded(both[: 2 * rows].astype(bf16), 3)
     last = turn(mixed, cosine_3, sine_3).astype(bf16)
     picked = jnp.stack([mul_t(select, last[:rows]), mul_t(select, last[rows:])])
     residual = picked - observed.astype(f32)
-    adjoint = lax.optimization_barrier(mul_t(near_3, turned)) + far_term.astype(f32)
+    adjoint = both[2 * rows :] + far_term.astype(f32)
     turned = turn_back(adjoint, cosine_2, sine_2).astype(bf16)
 
-    far_term = traded(mul_t(far_2, turned).astype(bf16), 2)
-    adjoint = lax.optimization_barrier(mul_t(near_2, turned)) + far_term.astype(f32)
+    both = lax.optimization_barrier(mul_t(wide[0], turned))
+    far_term = traded(both[: 2 * rows].astype(bf16), 2)
+    adjoint = both[2 * rows :] + far_term.astype(f32)
     turned = turn_back(adjoint, cosine_1, sine_1).astype(bf16)
 
     n_bfly, n_freq = lax.axis_size("bfly"), lax.axis_size("freq")

time: 88.7 us -> 89.5 us (level)
  blocking collectives: 17.9 us -> 18.9 us
    all_gather x2, blocking collectives: 17.9 us -> 18.9 us  [traded(): both = lax.all_gather(block, 'bfly', axis_index_groups=pairs)]
where the time goes in v6:
time: 89.5 us; the launch traced here: 89 us
  starting transfers between devices  37.3 us (42%)
  waiting for transfers between devices  19.5 us (22%)
  blocking collectives  18.9 us (21%)
  Pallas kernels  8.06 us (9%)
  matrix products  2.39 us (3%)
  other arithmetic  1.08 us (1%)
  between operations  0.99 us (1%)
    ppermute x7, starting transfers between devices, swapped(): return lax.ppermute(block, 'bfly', route)  22.9 us
    all_gather x2, blocking collectives, traded(): both = lax.all_gather(block, 'bfly', axis_index_groups=pairs)  18.9 us
    all_to_all x1, starting transfers between devices, local(): lax.all_to_all(terms, ('freq', 'bfly'), 0, 0, axis_index_groups=groups)  14.4 us
    ppermute x7, waiting for transfers between devices, swapped(): return lax.ppermute(block, 'bfly', route)  10.1 us
    all_to_all x1, waiting for transfers between devices, local(): lax.all_to_all(terms, ('freq', 'bfly'), 0, 0, axis_index_groups=groups)  9.45 us
  transfers between devices with their start and end apart: 8, of which 4 were waited for; matrix products, arithmetic and copies ran while one was open for 3% of the time, Pallas kernels for 6%

profile of v6, /device:TPU:1, one launch (start us, length us, event | category | flops | bytes accessed | tf_op | source)
XLA Modules:
  0.0 89.0 jit_solution(14421854712753034950)
XLA Ops:
  0.6 1.0 %first_field.1 = bf16[256,256]{1,0:T(8,128)(2,1)S(1)} custom-call(bf16[2,128,256]{2,1,0:T(8,128)(2,1)} %sources_ref.3, f32[1,128]{1,0:T(1,128)} %bitcast.56), custom_call_target="tpu_custom_call" | custom-call | tf_op jit(solution)/shard_map/first_field/pallas_call | solution.py:215
  1.6 8.8 %collective-permute-start = (bf16[256,256]{1,0:T(8,128)(2,1)S(1)}, bf16[256,256]{1,0:T(8,128)(2,1)S(1)}, u32[]{:S(2)}, u32[]{:S(2)}) collective-permute-start(bf16[256,256]{1,0:T(8,128)(2,1)S(1)} %first_field.1), channel_id=1, source_target_pairs={{0,1},{1,0},{2,3},{3,2},{4,5},{5,4},{6,7},{7,6},{8,9},{9,8},{10,11... | collective-permute-start | bytes 393224 | tf_op jit(solution)/shard_map/ppermute | solution.py:17
  10.4 1.4 %first_maps.1 = (bf16[256,256]{1,0:T(8,128)(2,1)S(1)}, bf16[256,256]{1,0:T(8,128)(2,1)S(1)}, f32[128,512]{1,0:T(8,128)S(1)}, bf16[528,256]{1,0:T(8,128)(2,1)S(1)}) custom-call(bf16[2,128,256]{2,1,0:T(8,128)(2,1)} %sources_ref.3, bf16[4,2,128,128]{3,2,1,0:T(8,128)(2,1)} %near_ref.5, bf16[4,2,128,128]{3,2,1,0:T(8,128)(2,1)} %far_ref.5, ...), custom_call_target="tpu_custom_call" | custom-call | tf_op jit(solution)/shard_map/first_maps/pallas_call | solution.py:226
  11.9 0.2 fusion.21
  12.1 0.0 collective-permute-done
  12.1 0.2 convolution_add_fusion.3
  12.3 0.0 copy-start.1
  12.4 1.9 %collective-permute-start.1 = (bf16[256,256]{1,0:T(8,128)(2,1)S(1)}, bf16[256,256]{1,0:T(8,128)(2,1)S(1)}, u32[]{:S(2)}, u32[]{:S(2)}) collective-permute-start(bf16[256,256]{1,0:T(8,128)(2,1)S(1)} %pad_maximum_fusion), channel_id=1, source_target_pairs={{0,2},{1,3},{2,0},{3,1},{4,6},{5,7},{6,4},{7,5},{8,10},{9,11},{10,... | collective-permute-start | bytes 393224 | tf_op jit(solution)/shard_map/ppermute | solution.py:17
  14.3 3.4 %collective-permute-start.5 = (bf16[528,256]{1,0:T(8,128)(2,1)S(1)}, bf16[528,256]{1,0:T(8,128)(2,1)S(1)}, u32[]{:S(2)}, u32[]{:S(2)}) collective-permute-start(bf16[528,256]{1,0:T(8,128)(2,1)S(1)} %get-tuple-element.41), channel_id=1, source_target_pairs={{0,2},{1,3},{2,0},{3,1},{4,6},{5,7},{6,4},{7,5},{8,10},{9,11},{10,... | collective-permute-start | bytes 811016 | tf_op jit(solution)/shard_map/ppermute | solution.py:17
  17.7 0.0 copy-done.1
  17.7 1.3 %middle_maps.1 = (bf16[256,256]{1,0:T(8,128)(2,1)S(1)}, bf16[256,256]{1,0:T(8,128)(2,1)S(1)}, f32[128,512]{1,0:T(8,128)S(1)}) custom-call(bf16[4,2,128,128]{3,2,1,0:T(8,128)(2,1)} %near_ref.5, bf16[4,2,128,128]{3,2,1,0:T(8,128)(2,1)} %far_ref.5, s32[2,2,2,4]{3,2,1,0:T(2,128)S(1)} %bitcast.51, f32[4,4,128]{2,1,0:T(4,128)} %bitcast.54), custom_call_target="tpu_custom_call" | custom-call | tf_op jit(solution)/shard_map/middle_maps/pallas_call | solution.py:248
  19.0 0.2 fusion.20
  19.2 0.2 collective-permute-done.1
  19.4 0.2 convolution_add_fusion.2
  19.6 0.0 copy-start.2
  19.6 1.9 %collective-permute-start.2 = (bf16[256,256]{1,0:T(8,128)(2,1)S(1)}, bf16[256,256]{1,0:T(8,128)(2,1)S(1)}, u32[]{:S(2)}, u32[]{:S(2)}) collective-permute-start(bf16[256,256]{1,0:T(8,128)(2,1)S(1)} %pad_maximum_fusion.1), channel_id=1, source_target_pairs={{0,4},{1,5},{2,6},{3,7},{4,0},{5,1},{6,2},{7,3},{8,12},{9,13},{10,... | collective-permute-start | bytes 393224 | tf_op jit(solution)/shard_map/ppermute | solution.py:17
  21.6 0.0 copy-done.2
  21.6 1.8 %later_maps.1 = (bf16[2,256,256]{2,1,0:T(8,128)(2,1)S(1)}, bf16[2,256,256]{2,1,0:T(8,128)(2,1)S(1)}, bf16[2,256,512]{2,1,0:T(8,128)(2,1)S(1)}, f32[2,128,512]{2,...) custom-call(bf16[4,2,128,128]{3,2,1,0:T(8,128)(2,1)} %near_ref.5, ...), custom_call_target="tpu_custom_call" | custom-call | tf_op jit(solution)/shard_map/later_maps/pallas_call | solution.py:268
  23.4 0.2 fusion.11
  23.6 7.0 %collective-permute-done.2 = bf16[256,256]{1,0:T(8,128)(2,1)S(1)} collective-permute-done((bf16[256,256]{1,0:T(8,128)(2,1)S(1)}, bf16[256,256]{1,0:T(8,128)(2,1)S(1)}, u32[]{:S(2)}, u32[]{:S(2)}) %collective-permute-start.2) | collective-permute-done | bytes 131104 | tf_op jit(solution)/shard_map/ppermute | solution.py:17
  30.6 0.2 convolution_add_fusion.1
  30.8 0.1 subtract_convert_fusion.4
  30.8 0.0 copy-start
  30.9 2.1 %collective-permute-start.3 = (bf16[256,256]{1,0:T(8,128)(2,1)S(1)}, bf16[256,256]{1,0:T(8,128)(2,1)S(1)}, u32[]{:S(2)}, u32[]{:S(2)}) collective-permute-start(bf16[256,256]{1,0:T(8,128)(2,1)S(1)} %pad_maximum_fusion.2), channel_id=1, source_target_pairs={{0,8},{1,9},{2,10},{3,11},{4,12},{5,13},{6,14},{7,15},{8,0},{9,1},... | collective-permute-start | bytes 393224 | tf_op jit(solution)/shard_map/ppermute | solution.py:17
  32.9 0.0 copy-done
  32.9 2.9 %collective-permute-start.4 = (bf16[256,256]{1,0:T(8,128)(2,1)S(1)}, bf16[256,256]{1,0:T(8,128)(2,1)S(1)}, u32[]{:S(2)}, u32[]{:S(2)}) collective-permute-start(bf16[256,256]{1,0:T(8,128)(2,1)S(1)} %bitcast.47), channel_id=1, source_target_pairs={{0,1},{1,0},{2,3},{3,2},{4,5},{5,4},{6,7},{7,6},{8,9},{9,8},{10,11... | collective-permute-start | bytes 393224 | tf_op jit(solution)/shard_map/ppermute | solution.py:17
  35.9 0.2 fusion.13
  36.1 0.0 collective-permute-done.5.lent_ref
  36.1 0.4 lent_maps.1
  36.5 1.9 %collective-permute-start.6 = (bf16[256,256]{1,0:T(8,128)(2,1)S(1)}, bf16[256,256]{1,0:T(8,128)(2,1)S(1)}, u32[]{:S(2)}, u32[]{:S(2)}) collective-permute-start(bf16[256,256]{1,0:T(8,128)(2,1)S(1)} %slice.115), channel_id=1, source_target_pairs={{0,1},{1,0},{2,3},{3,2},{4,5},{5,4},{6,7},{7,6},{8,9},{9,8},{10,11... | collective-permute-start | bytes 393224 | tf_op jit(solution)/shard_map/ppermute | solution.py:17
  38.5 2.9 %collective-permute-done.3 = bf16[256,256]{1,0:T(8,128)(2,1)S(1)} collective-permute-done((bf16[256,256]{1,0:T(8,128)(2,1)S(1)}, bf16[256,256]{1,0:T(8,128)(2,1)S(1)}, u32[]{:S(2)}, u32[]{:S(2)}) %collective-permute-start.3) | collective-permute-done | bytes 131104 | tf_op jit(solution)/shard_map/ppermute | solution.py:17
  41.4 0.2 subtract_convert_fusion
  41.6 0.2 convolution_bitcast_fusion
  41.8 0.0 collective-permute-done.4.across_ref
  41.8 0.0 collective-permute-done.6.across_lent_ref
  41.8 0.3 fusion
  42.1 12.8 %all-gather = bf16[512,256]{1,0:T(8,128)(2,1)S(1)} all-gather(bf16[256,256]{1,0:T(8,128)(2,1)S(1)} %slice.243), channel_id=2, replica_groups={{0,8},{1,9},{2,10},{3,11},{4,12},{5,13},{6,14},{7,15},{16,24},{17,25},{..., dimensions={0}, use_global_device_ids=true | all-gather | bytes 393216 | tf_op jit(solution)/shard_map/all_gather | solution.py:23
  54.9 0.1 add_convert_fusion.2
  55.0 0.3 fusion.2
  55.3 6.1 %all-gather.1 = bf16[512,256]{1,0:T(8,128)(2,1)S(1)} all-gather(bf16[256,256]{1,0:T(8,128)(2,1)S(1)} %slice.242), channel_id=3, replica_groups={{0,4},{1,5},{2,6},{3,7},{8,12},{9,13},{10,14},{11,15},{16,20},{17,21},{..., dimensions={0}, use_global_device_ids=true | all-gather | bytes 393216 | tf_op jit(solution)/shard_map/all_gather | solution.py:23
  61.5 1.4 %last_terms.1 = f32[128,1,256]{2,1,0:T(1,128)} custom-call(bf16[256,256]{1,0:T(8,128)(2,1)S(1)} %pad_maximum_fusion.3.turned_ref, bf16[256,256]{1,0:T(8,128)(2,1)S(1)} %get-tuple-element.30.near_1_ref, bf16[256,256]{1,0:T(8,128)(2,1)S(1)} %get-tuple-element.31.far_1_ref, bf16[256,256]{1,0:T(8,128)(2,1)S(1)} %get-tuple-element.26.near_ref, ...), custom_call_target="tpu_custom_call" | custom-call | tf_op jit(solution)/shard_map/last_terms/pallas_call | solution.py:331
  62.9 14.4 %all-to-all-start = ((f32[128,1,256]{2,1,0:T(1,128)}), f32[128,1,256]{2,1,0:T(1,128)S(1)}, u32[]{:S(2)}, u32[]{:S(2)}) async-start(f32[128,1,256]{2,1,0:T(1,128)} %last_terms.1), calls=%async_computation | async-start | bytes 262144 | tf_op jit(solution)/shard_map/all_to_all | solution.py:343
  77.3 0.0 copy-start.3
  77.3 0.2 convolution_bitcast_fusion.1
  77.5 0.7 copy-done.3
  78.2 0.7 maximum_subtract_fusion
  78.9 9.5 %all-to-all-done.terms_ref = f32[128,1,256]{2,1,0:T(1,128)S(1)} async-done(((f32[128,1,256]{2,1,0:T(1,128)}), f32[128,1,256]{2,1,0:T(1,128)S(1)}, u32[]{:S(2)}, u32[]{:S(2)}) %all-to-all-start) | async-done | bytes 131104 | tf_op jit(solution)/shard_map/all_to_all | solution.py:343
  88.4 0.7 last_ratio.1
  (13 shorter events, 0.3 us)
Async XLA Ops:
  1.6 10.4 %collective-permute-start = (bf16[256,256]{1,0:T(8,128)(2,1)S(1)}, bf16[256,256]{1,0:T(8,128)(2,1)S(1)}, u32[]{:S(2)}, u32[]{:S(2)}) collective-permute-start(bf16[256,256]{1,0:T(8,128)(2,1)S(1)} %first_field.1), channel_id=1, source_target_pairs={{0,1},{1,0},{2,3},{3,2},{4,5},{5,4},{6,7},{7,6},{8,9},{9,8},{10,11... | collective-permute-start | bytes 393224 | tf_op jit(solution)/shard_map/ppermute | solution.py:17
  12.3 5.3 %copy-start.1 = (s32[4,2,2,2]{0,3,2,1:T(2,128)S(1)}, s32[4,2,2,2]{0,3,2,1:T(2,128)}, u32[]{:S(2)}) copy-start(s32[4,2,2,2]{0,3,2,1:T(2,128)} %param.15) | copy-start | bytes 388
  12.4 7.0 %collective-permute-start.1 = (bf16[256,256]{1,0:T(8,128)(2,1)S(1)}, bf16[256,256]{1,0:T(8,128)(2,1)S(1)}, u32[]{:S(2)}, u32[]{:S(2)}) collective-permute-start(bf16[256,256]{1,0:T(8,128)(2,1)S(1)} %pad_maximum_fusion), channel_id=1, source_target_pairs={{0,2},{1,3},{2,0},{3,1},{4,6},{5,7},{6,4},{7,5},{8,10},{9,11},{10,... | collective-permute-start | bytes 393224 | tf_op jit(solution)/shard_map/ppermute | solution.py:17
  14.3 21.8 %collective-permute-start.5 = (bf16[528,256]{1,0:T(8,128)(2,1)S(1)}, bf16[528,256]{1,0:T(8,128)(2,1)S(1)}, u32[]{:S(2)}, u32[]{:S(2)}) collective-permute-start(bf16[528,256]{1,0:T(8,128)(2,1)S(1)} %get-tuple-element.41), channel_id=1, source_target_pairs={{0,2},{1,3},{2,0},{3,1},{4,6},{5,7},{6,4},{7,5},{8,10},{9,11},{10,... | collective-permute-start | bytes 811016 | tf_op jit(solution)/shard_map/ppermute | solution.py:17
  19.6 1.9 %copy-start.2 = (s32[128]{0:T(128)S(1)}, s32[128]{0:T(128)}, u32[]{:S(2)}) copy-start(s32[128]{0:T(128)} %param.10) | copy-start | bytes 1540
  19.6 11.0 %collective-permute-start.2 = (bf16[256,256]{1,0:T(8,128)(2,1)S(1)}, bf16[256,256]{1,0:T(8,128)(2,1)S(1)}, u32[]{:S(2)}, u32[]{:S(2)}) collective-permute-start(bf16[256,256]{1,0:T(8,128)(2,1)S(1)} %pad_maximum_fusion.1), channel_id=1, source_target_pairs={{0,4},{1,5},{2,6},{3,7},{4,0},{5,1},{6,2},{7,3},{8,12},{9,13},{10,... | collective-permute-start | bytes 393224 | tf_op jit(solution)/shard_map/ppermute | solution.py:17
  30.8 2.1 %copy-start = (bf16[2,128,256]{2,1,0:T(8,128)(2,1)S(1)}, bf16[2,128,256]{2,1,0:T(8,128)(2,1)}, u32[]{:S(2)}) copy-start(bf16[2,128,256]{2,1,0:T(8,128)(2,1)} %sources_ref.3) | copy-start | bytes 393220
  30.9 10.5 %collective-permute-start.3 = (bf16[256,256]{1,0:T(8,128)(2,1)S(1)}, bf16[256,256]{1,0:T(8,128)(2,1)S(1)}, u32[]{:S(2)}, u32[]{:S(2)}) collective-permute-start(bf16[256,256]{1,0:T(8,128)(2,1)S(1)} %pad_maximum_fusion.2), channel_id=1, source_target_pairs={{0,8},{1,9},{2,10},{3,11},{4,12},{5,13},{6,14},{7,15},{8,0},{9,1},... | collective-permute-start | bytes 393224 | tf_op jit(solution)/shard_map/ppermute | solution.py:17
  32.9 8.8 %collective-permute-start.4 = (bf16[256,256]{1,0:T(8,128)(2,1)S(1)}, bf16[256,256]{1,0:T(8,128)(2,1)S(1)}, u32[]{:S(2)}, u32[]{:S(2)}) collective-permute-start(bf16[256,256]{1,0:T(8,128)(2,1)S(1)} %bitcast.47), channel_id=1, source_target_pairs={{0,1},{1,0},{2,3},{3,2},{4,5},{5,4},{6,7},{7,6},{8,9},{9,8},{10,11... | collective-permute-start | bytes 393224 | tf_op jit(solution)/shard_map/ppermute | solution.py:17
  36.5 5.2 %collective-permute-start.6 = (bf16[256,256]{1,0:T(8,128)(2,1)S(1)}, bf16[256,256]{1,0:T(8,128)(2,1)S(1)}, u32[]{:S(2)}, u32[]{:S(2)}) collective-permute-start(bf16[256,256]{1,0:T(8,128)(2,1)S(1)} %slice.115), channel_id=1, source_target_pairs={{0,1},{1,0},{2,3},{3,2},{4,5},{5,4},{6,7},{7,6},{8,9},{9,8},{10,11... | collective-permute-start | bytes 393224 | tf_op jit(solution)/shard_map/ppermute | solution.py:17
  62.9 25.5 %all-to-all-start = ((f32[128,1,256]{2,1,0:T(1,128)}), f32[128,1,256]{2,1,0:T(1,128)S(1)}, u32[]{:S(2)}, u32[]{:S(2)}) async-start(f32[128,1,256]{2,1,0:T(1,128)} %last_terms.1), calls=%async_computation | async-start | bytes 262144 | tf_op jit(solution)/shard_map/all_to_all | solution.py:343
  77.3 0.9 %copy-start.3 = (bf16[2,128,256]{2,1,0:T(8,128)(2,1)S(1)}, bf16[2,128,256]{2,1,0:T(8,128)(2,1)}, u32[]{:S(2)}) copy-start(bf16[2,128,256]{2,1,0:T(8,128)(2,1)} %observed_ref.1) | copy-start | bytes 393220

commit v7 on v5

--- a/solution.py
+++ b/solution.py
@@ -318,7 +318,7 @@
     adjoint = lax.optimization_barrier(mul_t(near_3, turned)) + far_term.astype(f32)
     turned = turn_back(adjoint, cosine_2, sine_2).astype(bf16)
 
-    far_term = traded(mul_t(far_2, turned).astype(bf16), 2)
+    far_term = swapped(mul_t(far_2, turned).astype(bf16), 2)
     adjoint = lax.optimization_barrier(mul_t(near_2, turned)) + far_term.astype(f32)
     turned = turn_back(adjoint, cosine_1, sine_1).astype(bf16)
 

time: 88.7 us -> 90.8 us (1.024)
  waiting for transfers between devices: 19.5 us -> 25.8 us
  blocking collectives: 17.9 us -> 12.8 us
    ppermute x7 -> x8, waiting for transfers between devices: 10.1 us -> 16.4 us  [swapped(): return lax.ppermute(block, 'bfly', route)]
    all_gather x2 -> x1, blocking collectives: 17.9 us -> 12.8 us  [traded(): both = lax.all_gather(block, 'bfly', axis_index_groups=pairs)]
    ppermute x7 -> x8, starting transfers between devices: 22.9 us -> 24.8 us  [swapped(): return lax.ppermute(block, 'bfly', route)]
    all_to_all x1, starting transfers between devices: 14.3 us -> 13.3 us  [local(): lax.all_to_all(terms, ('freq', 'bfly'), 0, 0, axis_index_groups=groups)]
  transfers between devices with their start and end apart: 8 -> 9, of which waited for: 4 -> 5; matrix products, arithmetic and copies ran while one was open for 3% -> 3% of each run, Pallas kernels for 6% -> 6%
where the time goes in v7:
time: 90.8 us; the launch traced here: 90.3 us
  starting transfers between devices  38 us (42%)
  waiting for transfers between devices  25.8 us (28%)
  blocking collectives  12.8 us (14%)
  Pallas kernels  8.07 us (9%)
  matrix products  2.75 us (3%)
  other arithmetic  1.07 us (1%)
  between operations  1 us (1%)
    ppermute x8, starting transfers between devices, swapped(): return lax.ppermute(block, 'bfly', route)  24.8 us
    ppermute x8, waiting for transfers between devices, swapped(): return lax.ppermute(block, 'bfly', route)  16.4 us
    all_to_all x1, starting transfers between devices, local(): lax.all_to_all(terms, ('freq', 'bfly'), 0, 0, axis_index_groups=groups)  13.3 us
    all_gather x1, blocking collectives, traded(): both = lax.all_gather(block, 'bfly', axis_index_groups=pairs)  12.8 us
    all_to_all x1, waiting for transfers between devices, local(): lax.all_to_all(terms, ('freq', 'bfly'), 0, 0, axis_index_groups=groups)  9.45 us
  transfers between devices with their start and end apart: 9, of which 5 were waited for; matrix products, arithmetic and copies ran while one was open for 3% of the time, Pallas kernels for 6%

profile of v7, /device:TPU:1, one launch (start us, length us, event | category | flops | bytes accessed | tf_op | source)
XLA Modules:
  0.0 90.3 jit_solution(12761534775920934819)
XLA Ops:
  0.6 1.0 %first_field.1 = bf16[256,256]{1,0:T(8,128)(2,1)S(1)} custom-call(bf16[2,128,256]{2,1,0:T(8,128)(2,1)} %sources_ref.3, f32[1,128]{1,0:T(1,128)} %bitcast.59), custom_call_target="tpu_custom_call" | custom-call | tf_op jit(solution)/shard_map/first_field/pallas_call | solution.py:214
  1.6 8.8 %collective-permute-start = (bf16[256,256]{1,0:T(8,128)(2,1)S(1)}, bf16[256,256]{1,0:T(8,128)(2,1)S(1)}, u32[]{:S(2)}, u32[]{:S(2)}) collective-permute-start(bf16[256,256]{1,0:T(8,128)(2,1)S(1)} %first_field.1), channel_id=1, source_target_pairs={{0,1},{1,0},{2,3},{3,2},{4,5},{5,4},{6,7},{7,6},{8,9},{9,8},{10,11... | collective-permute-start | bytes 393224 | tf_op jit(solution)/shard_map/ppermute | solution.py:17
  10.4 1.4 %first_maps.1 = (bf16[256,256]{1,0:T(8,128)(2,1)S(1)}, bf16[256,256]{1,0:T(8,128)(2,1)S(1)}, f32[128,512]{1,0:T(8,128)S(1)}, bf16[528,256]{1,0:T(8,128)(2,1)S(1)}) custom-call(bf16[2,128,256]{2,1,0:T(8,128)(2,1)} %sources_ref.3, bf16[4,2,128,128]{3,2,1,0:T(8,128)(2,1)} %near_ref.5, bf16[4,2,128,128]{3,2,1,0:T(8,128)(2,1)} %far_ref.5, ...), custom_call_target="tpu_custom_call" | custom-call | tf_op jit(solution)/shard_map/first_maps/pallas_call | solution.py:225
  11.9 0.2 fusion.23
  12.1 0.0 collective-permute-done
  12.1 0.2 convolution_add_fusion.3
  12.3 0.0 copy-start.1
  12.4 1.9 %collective-permute-start.1 = (bf16[256,256]{1,0:T(8,128)(2,1)S(1)}, bf16[256,256]{1,0:T(8,128)(2,1)S(1)}, u32[]{:S(2)}, u32[]{:S(2)}) collective-permute-start(bf16[256,256]{1,0:T(8,128)(2,1)S(1)} %pad_maximum_fusion), channel_id=1, source_target_pairs={{0,2},{1,3},{2,0},{3,1},{4,6},{5,7},{6,4},{7,5},{8,10},{9,11},{10,... | collective-permute-start | bytes 393224 | tf_op jit(solution)/shard_map/ppermute | solution.py:17
  14.3 3.4 %collective-permute-start.5 = (bf16[528,256]{1,0:T(8,128)(2,1)S(1)}, bf16[528,256]{1,0:T(8,128)(2,1)S(1)}, u32[]{:S(2)}, u32[]{:S(2)}) collective-permute-start(bf16[528,256]{1,0:T(8,128)(2,1)S(1)} %get-tuple-element.39), channel_id=1, source_target_pairs={{0,2},{1,3},{2,0},{3,1},{4,6},{5,7},{6,4},{7,5},{8,10},{9,11},{10,... | collective-permute-start | bytes 811016 | tf_op jit(solution)/shard_map/ppermute | solution.py:17
  17.7 1.3 %middle_maps.1 = (bf16[256,256]{1,0:T(8,128)(2,1)S(1)}, bf16[256,256]{1,0:T(8,128)(2,1)S(1)}, f32[128,512]{1,0:T(8,128)S(1)}) custom-call(bf16[4,2,128,128]{3,2,1,0:T(8,128)(2,1)} %near_ref.5, bf16[4,2,128,128]{3,2,1,0:T(8,128)(2,1)} %far_ref.5, s32[2,2,2,4]{3,2,1,0:T(2,128)S(1)} %bitcast.54, f32[4,4,128]{2,1,0:T(4,128)} %bitcast.57), custom_call_target="tpu_custom_call" | custom-call | tf_op jit(solution)/shard_map/middle_maps/pallas_call | solution.py:247
  19.0 0.2 fusion.22
  19.2 0.2 collective-permute-done.1
  19.4 0.2 convolution_add_fusion.2
  19.7 0.0 copy-start.2
  19.7 1.9 %collective-permute-start.2 = (bf16[256,256]{1,0:T(8,128)(2,1)S(1)}, bf16[256,256]{1,0:T(8,128)(2,1)S(1)}, u32[]{:S(2)}, u32[]{:S(2)}) collective-permute-start(bf16[256,256]{1,0:T(8,128)(2,1)S(1)} %pad_maximum_fusion.1), channel_id=1, source_target_pairs={{0,4},{1,5},{2,6},{3,7},{4,0},{5,1},{6,2},{7,3},{8,12},{9,13},{10,... | collective-permute-start | bytes 393224 | tf_op jit(solution)/shard_map/ppermute | solution.py:17
  21.6 0.0 copy-done.2
  21.6 1.8 %later_maps.1 = (bf16[2,256,256]{2,1,0:T(8,128)(2,1)S(1)}, bf16[2,256,256]{2,1,0:T(8,128)(2,1)S(1)}, f32[2,128,512]{2,1,0:T(8,128)S(1)}, bf16[128,128]{1,0:T(8,1...) custom-call(bf16[4,2,128,128]{3,2,1,0:T(8,128)(2,1)} %near_ref.5, bf16[4,2,128,128]{3,2,1,0:T(8,128)(2,1)} %far_ref.5, ...), custom_call_target="tpu_custom_call" | custom-call | tf_op jit(solution)/shard_map/later_maps/pallas_call | solution.py:267
  23.4 0.2 fusion.10
  23.6 7.0 %collective-permute-done.2 = bf16[256,256]{1,0:T(8,128)(2,1)S(1)} collective-permute-done((bf16[256,256]{1,0:T(8,128)(2,1)S(1)}, bf16[256,256]{1,0:T(8,128)(2,1)S(1)}, u32[]{:S(2)}, u32[]{:S(2)}) %collective-permute-start.2) | collective-permute-done | bytes 131104 | tf_op jit(solution)/shard_map/ppermute | solution.py:17
  30.6 0.2 convolution_add_fusion.1
  30.8 0.1 subtract_convert_fusion.4
  30.9 0.0 copy-start
  30.9 2.1 %collective-permute-start.3 = (bf16[256,256]{1,0:T(8,128)(2,1)S(1)}, bf16[256,256]{1,0:T(8,128)(2,1)S(1)}, u32[]{:S(2)}, u32[]{:S(2)}) collective-permute-start(bf16[256,256]{1,0:T(8,128)(2,1)S(1)} %pad_maximum_fusion.2), channel_id=1, source_target_pairs={{0,8},{1,9},{2,10},{3,11},{4,12},{5,13},{6,14},{7,15},{8,0},{9,1},... | collective-permute-start | bytes 393224 | tf_op jit(solution)/shard_map/ppermute | solution.py:17
  33.0 2.9 %collective-permute-start.4 = (bf16[256,256]{1,0:T(8,128)(2,1)S(1)}, bf16[256,256]{1,0:T(8,128)(2,1)S(1)}, u32[]{:S(2)}, u32[]{:S(2)}) collective-permute-start(bf16[256,256]{1,0:T(8,128)(2,1)S(1)} %bitcast.50), channel_id=1, source_target_pairs={{0,1},{1,0},{2,3},{3,2},{4,5},{5,4},{6,7},{7,6},{8,9},{9,8},{10,11... | collective-permute-start | bytes 393224 | tf_op jit(solution)/shard_map/ppermute | solution.py:17
  35.9 0.2 fusion.6
  36.0 0.0 collective-permute-done.5.lent_ref
  36.1 0.5 lent_maps.1
  36.5 1.9 %collective-permute-start.6 = (bf16[256,256]{1,0:T(8,128)(2,1)S(1)}, bf16[256,256]{1,0:T(8,128)(2,1)S(1)}, u32[]{:S(2)}, u32[]{:S(2)}) collective-permute-start(bf16[256,256]{1,0:T(8,128)(2,1)S(1)} %slice.87), channel_id=1, source_target_pairs={{0,1},{1,0},{2,3},{3,2},{4,5},{5,4},{6,7},{7,6},{8,9},{9,8},{10,11... | collective-permute-start | bytes 393224 | tf_op jit(solution)/shard_map/ppermute | solution.py:17
  38.5 2.9 %collective-permute-done.3 = bf16[256,256]{1,0:T(8,128)(2,1)S(1)} collective-permute-done((bf16[256,256]{1,0:T(8,128)(2,1)S(1)}, bf16[256,256]{1,0:T(8,128)(2,1)S(1)}, u32[]{:S(2)}, u32[]{:S(2)}) %collective-permute-start.3) | collective-permute-done | bytes 131104 | tf_op jit(solution)/shard_map/ppermute | solution.py:17
  41.4 0.2 subtract_convert_fusion
  41.6 0.2 convolution_bitcast_fusion
  41.8 0.0 collective-permute-done.4.across_ref
  41.8 0.0 collective-permute-done.6.across_lent_ref
  41.8 0.2 convolution_convert_fusion.1
  42.1 0.2 fusion.4
  42.3 12.8 %all-gather = bf16[512,256]{1,0:T(8,128)(2,1)S(1)} all-gather(bf16[256,256]{1,0:T(8,128)(2,1)S(1)} %convolution_convert_fusion.1), channel_id=2, replica_groups={{0,8},{1,9},{2,10},{3,11},{4,12},{5,13},{6,14},{7,15},{16,24},{17,25},{..., dimensions={0}, use_global_device_ids=true | all-gather | bytes 393216 | tf_op jit(solution)/shard_map/all_gather | solution.py:23
  55.2 0.2 convolution_convert_fusion
  55.4 1.9 %collective-permute-start.7 = (bf16[256,256]{1,0:T(8,128)(2,1)S(1)}, bf16[256,256]{1,0:T(8,128)(2,1)S(1)}, u32[]{:S(2)}, u32[]{:S(2)}) collective-permute-start(bf16[256,256]{1,0:T(8,128)(2,1)S(1)} %convolution_convert_fusion), channel_id=1, source_target_pairs={{0,4},{1,5},{2,6},{3,7},{4,0},{5,1},{6,2},{7,3},{8,12},{9,13},{10,... | collective-permute-start | bytes 393224 | tf_op jit(solution)/shard_map/ppermute | solution.py:17
  57.3 0.2 fusion.8
  57.6 6.2 %collective-permute-done.7 = bf16[256,256]{1,0:T(8,128)(2,1)S(1)} collective-permute-done((bf16[256,256]{1,0:T(8,128)(2,1)S(1)}, bf16[256,256]{1,0:T(8,128)(2,1)S(1)}, u32[]{:S(2)}, u32[]{:S(2)}) %collective-permute-start.7) | collective-permute-done | bytes 131104 | tf_op jit(solution)/shard_map/ppermute | solution.py:17
  63.9 1.4 %last_terms.1 = f32[128,1,256]{2,1,0:T(1,128)} custom-call(bf16[256,256]{1,0:T(8,128)(2,1)S(1)} %pad_maximum_fusion.4.turned_ref, bf16[256,256]{1,0:T(8,128)(2,1)S(1)} %get-tuple-element.29.near_1_ref, bf16[256,256]{1,0:T(8,128)(2,1)S(1)} %get-tuple-element.30.far_1_ref, bf16[256,256]{1,0:T(8,128)(2,1)S(1)} %get-tuple-element.25.near_ref, ...), custom_call_target="tpu_custom_call" | custom-call | tf_op jit(solution)/shard_map/last_terms/pallas_call | solution.py:327
  65.3 13.3 %all-to-all-start = ((f32[128,1,256]{2,1,0:T(1,128)}), f32[128,1,256]{2,1,0:T(1,128)S(1)}, u32[]{:S(2)}, u32[]{:S(2)}) async-start(f32[128,1,256]{2,1,0:T(1,128)} %last_terms.1), calls=%async_computation | async-start | bytes 262144 | tf_op jit(solution)/shard_map/all_to_all | solution.py:339
  78.6 0.0 copy-start.3
  78.6 0.2 convolution_bitcast_fusion.1
  78.8 0.7 copy-done.3
  79.5 0.7 maximum_subtract_fusion
  80.2 9.4 %all-to-all-done.terms_ref = f32[128,1,256]{2,1,0:T(1,128)S(1)} async-done(((f32[128,1,256]{2,1,0:T(1,128)}), f32[128,1,256]{2,1,0:T(1,128)S(1)}, u32[]{:S(2)}, u32[]{:S(2)}) %all-to-all-start) | async-done | bytes 131104 | tf_op jit(solution)/shard_map/all_to_all | solution.py:339
  89.6 0.7 last_ratio.1
  (14 shorter events, 0.3 us)
Async XLA Ops:
  1.6 10.4 %collective-permute-start = (bf16[256,256]{1,0:T(8,128)(2,1)S(1)}, bf16[256,256]{1,0:T(8,128)(2,1)S(1)}, u32[]{:S(2)}, u32[]{:S(2)}) collective-permute-start(bf16[256,256]{1,0:T(8,128)(2,1)S(1)} %first_field.1), channel_id=1, source_target_pairs={{0,1},{1,0},{2,3},{3,2},{4,5},{5,4},{6,7},{7,6},{8,9},{9,8},{10,11... | collective-permute-start | bytes 393224 | tf_op jit(solution)/shard_map/ppermute | solution.py:17
  12.3 5.3 %copy-start.1 = (s32[4,2,2,2]{0,3,2,1:T(2,128)S(1)}, s32[4,2,2,2]{0,3,2,1:T(2,128)}, u32[]{:S(2)}) copy-start(s32[4,2,2,2]{0,3,2,1:T(2,128)} %param.15) | copy-start | bytes 388
  12.4 7.0 %collective-permute-start.1 = (bf16[256,256]{1,0:T(8,128)(2,1)S(1)}, bf16[256,256]{1,0:T(8,128)(2,1)S(1)}, u32[]{:S(2)}, u32[]{:S(2)}) collective-permute-start(bf16[256,256]{1,0:T(8,128)(2,1)S(1)} %pad_maximum_fusion), channel_id=1, source_target_pairs={{0,2},{1,3},{2,0},{3,1},{4,6},{5,7},{6,4},{7,5},{8,10},{9,11},{10,... | collective-permute-start | bytes 393224 | tf_op jit(solution)/shard_map/ppermute | solution.py:17
  14.3 21.7 %collective-permute-start.5 = (bf16[528,256]{1,0:T(8,128)(2,1)S(1)}, bf16[528,256]{1,0:T(8,128)(2,1)S(1)}, u32[]{:S(2)}, u32[]{:S(2)}) collective-permute-start(bf16[528,256]{1,0:T(8,128)(2,1)S(1)} %get-tuple-element.39), channel_id=1, source_target_pairs={{0,2},{1,3},{2,0},{3,1},{4,6},{5,7},{6,4},{7,5},{8,10},{9,11},{10,... | collective-permute-start | bytes 811016 | tf_op jit(solution)/shard_map/ppermute | solution.py:17
  19.7 1.9 %copy-start.2 = (s32[128]{0:T(128)S(1)}, s32[128]{0:T(128)}, u32[]{:S(2)}) copy-start(s32[128]{0:T(128)} %param.10) | copy-start | bytes 1540
  19.7 11.0 %collective-permute-start.2 = (bf16[256,256]{1,0:T(8,128)(2,1)S(1)}, bf16[256,256]{1,0:T(8,128)(2,1)S(1)}, u32[]{:S(2)}, u32[]{:S(2)}) collective-permute-start(bf16[256,256]{1,0:T(8,128)(2,1)S(1)} %pad_maximum_fusion.1), channel_id=1, source_target_pairs={{0,4},{1,5},{2,6},{3,7},{4,0},{5,1},{6,2},{7,3},{8,12},{9,13},{10,... | collective-permute-start | bytes 393224 | tf_op jit(solution)/shard_map/ppermute | solution.py:17
  30.9 2.1 %copy-start = (bf16[2,128,256]{2,1,0:T(8,128)(2,1)S(1)}, bf16[2,128,256]{2,1,0:T(8,128)(2,1)}, u32[]{:S(2)}) copy-start(bf16[2,128,256]{2,1,0:T(8,128)(2,1)} %sources_ref.3) | copy-start | bytes 393220
  30.9 10.5 %collective-permute-start.3 = (bf16[256,256]{1,0:T(8,128)(2,1)S(1)}, bf16[256,256]{1,0:T(8,128)(2,1)S(1)}, u32[]{:S(2)}, u32[]{:S(2)}) collective-permute-start(bf16[256,256]{1,0:T(8,128)(2,1)S(1)} %pad_maximum_fusion.2), channel_id=1, source_target_pairs={{0,8},{1,9},{2,10},{3,11},{4,12},{5,13},{6,14},{7,15},{8,0},{9,1},... | collective-permute-start | bytes 393224 | tf_op jit(solution)/shard_map/ppermute | solution.py:17
  33.0 8.8 %collective-permute-start.4 = (bf16[256,256]{1,0:T(8,128)(2,1)S(1)}, bf16[256,256]{1,0:T(8,128)(2,1)S(1)}, u32[]{:S(2)}, u32[]{:S(2)}) collective-permute-start(bf16[256,256]{1,0:T(8,128)(2,1)S(1)} %bitcast.50), channel_id=1, source_target_pairs={{0,1},{1,0},{2,3},{3,2},{4,5},{5,4},{6,7},{7,6},{8,9},{9,8},{10,11... | collective-permute-start | bytes 393224 | tf_op jit(solution)/shard_map/ppermute | solution.py:17
  36.5 5.3 %collective-permute-start.6 = (bf16[256,256]{1,0:T(8,128)(2,1)S(1)}, bf16[256,256]{1,0:T(8,128)(2,1)S(1)}, u32[]{:S(2)}, u32[]{:S(2)}) collective-permute-start(bf16[256,256]{1,0:T(8,128)(2,1)S(1)} %slice.87), channel_id=1, source_target_pairs={{0,1},{1,0},{2,3},{3,2},{4,5},{5,4},{6,7},{7,6},{8,9},{9,8},{10,11... | collective-permute-start | bytes 393224 | tf_op jit(solution)/shard_map/ppermute | solution.py:17
  55.4 8.4 %collective-permute-start.7 = (bf16[256,256]{1,0:T(8,128)(2,1)S(1)}, bf16[256,256]{1,0:T(8,128)(2,1)S(1)}, u32[]{:S(2)}, u32[]{:S(2)}) collective-permute-start(bf16[256,256]{1,0:T(8,128)(2,1)S(1)} %convolution_convert_fusion), channel_id=1, source_target_pairs={{0,4},{1,5},{2,6},{3,7},{4,0},{5,1},{6,2},{7,3},{8,12},{9,13},{10,... | collective-permute-start | bytes 393224 | tf_op jit(solution)/shard_map/ppermute | solution.py:17
  65.3 24.4 %all-to-all-start = ((f32[128,1,256]{2,1,0:T(1,128)}), f32[128,1,256]{2,1,0:T(1,128)S(1)}, u32[]{:S(2)}, u32[]{:S(2)}) async-start(f32[128,1,256]{2,1,0:T(1,128)} %last_terms.1), calls=%async_computation | async-start | bytes 262144 | tf_op jit(solution)/shard_map/all_to_all | solution.py:339
  78.6 0.9 %copy-start.3 = (bf16[2,128,256]{2,1,0:T(8,128)(2,1)S(1)}, bf16[2,128,256]{2,1,0:T(8,128)(2,1)}, u32[]{:S(2)}) copy-start(bf16[2,128,256]{2,1,0:T(8,128)(2,1)} %observed_ref.1) | copy-start | bytes 393220

commit v8 on v5

--- a/solution.py
+++ b/solution.py
@@ -261,7 +261,7 @@
     mixed = mul(near_1, field) + mul(far_1, partner)
     field = turn(mixed, cosine_1, sine_1).astype(bf16)
 
-    partner = swapped(field, 2)
+    partner = traded(field, 2)
     blocks = pl.BlockSpec((2, 2, rows, rows), lambda step: (1, 0, 0, 0))
     angles = pl.BlockSpec((2, *phases.shape[1:]), lambda step: (1, 0, 0))
     near, far, wave, select, counts, data = pl.pallas_call(

time: 88.7 us -> 91.1 us (1.027)
  blocking collectives: 17.9 us -> 27.3 us
  waiting for transfers between devices: 19.5 us -> 12.8 us
    all_gather x2 -> x3, blocking collectives: 17.9 us -> 27.3 us  [traded(): both = lax.all_gather(block, 'bfly', axis_index_groups=pairs)]
    ppermute x7 -> x6, waiting for transfers between devices: 10.1 us -> 3.34 us  [swapped(): return lax.ppermute(block, 'bfly', route)]
    ppermute x7 -> x6, starting transfers between devices: 22.9 us -> 21.2 us  [swapped(): return lax.ppermute(block, 'bfly', route)]
  transfers between devices with their start and end apart: 8 -> 7, of which waited for: 4 -> 3; matrix products, arithmetic and copies ran while one was open for 3% -> 3% of each run, Pallas kernels for 6% -> 6%
where the time goes in v8:
time: 91.1 us; the launch traced here: 90.6 us
  starting transfers between devices  36.2 us (40%)
  blocking collectives  27.3 us (30%)
  waiting for transfers between devices  12.8 us (14%)
  Pallas kernels  8.06 us (9%)
  matrix products  2.74 us (3%)
  local copies, waits for them, and re-layouts  1.42 us (2%)
  other arithmetic  1.1 us (1%)
  between operations  0.98 us (1%)
    all_gather x3, blocking collectives, traded(): both = lax.all_gather(block, 'bfly', axis_index_groups=pairs)  27.3 us
    ppermute x6, starting transfers between devices, swapped(): return lax.ppermute(block, 'bfly', route)  21.2 us
    all_to_all x1, starting transfers between devices, local(): lax.all_to_all(terms, ('freq', 'bfly'), 0, 0, axis_index_groups=groups)  15.1 us
    all_to_all x1, waiting for transfers between devices, local(): lax.all_to_all(terms, ('freq', 'bfly'), 0, 0, axis_index_groups=groups)  9.45 us
    ppermute x6, waiting for transfers between devices, swapped(): return lax.ppermute(block, 'bfly', route)  3.34 us
  transfers between devices with their start and end apart: 7, of which 3 were waited for; matrix products, arithmetic and copies ran while one was open for 3% of the time, Pallas kernels for 6%

profile of v8, /device:TPU:1, one launch (start us, length us, event | category | flops | bytes accessed | tf_op | source)
XLA Modules:
  0.0 90.6 jit_solution(16163302025907279790)
XLA Ops:
  0.6 1.0 %first_field.1 = bf16[256,256]{1,0:T(8,128)(2,1)S(1)} custom-call(bf16[2,128,256]{2,1,0:T(8,128)(2,1)} %sources_ref.3, f32[1,128]{1,0:T(1,128)} %bitcast.65), custom_call_target="tpu_custom_call" | custom-call | tf_op jit(solution)/shard_map/first_field/pallas_call | solution.py:214
  1.6 8.8 %collective-permute-start = (bf16[256,256]{1,0:T(8,128)(2,1)S(1)}, bf16[256,256]{1,0:T(8,128)(2,1)S(1)}, u32[]{:S(2)}, u32[]{:S(2)}) collective-permute-start(bf16[256,256]{1,0:T(8,128)(2,1)S(1)} %first_field.1), channel_id=1, source_target_pairs={{0,1},{1,0},{2,3},{3,2},{4,5},{5,4},{6,7},{7,6},{8,9},{9,8},{10,11... | collective-permute-start | bytes 393224 | tf_op jit(solution)/shard_map/ppermute | solution.py:17
  10.4 1.4 %first_maps.1 = (bf16[256,256]{1,0:T(8,128)(2,1)S(1)}, bf16[256,256]{1,0:T(8,128)(2,1)S(1)}, f32[128,512]{1,0:T(8,128)S(1)}, bf16[528,256]{1,0:T(8,128)(2,1)S(1)}) custom-call(bf16[2,128,256]{2,1,0:T(8,128)(2,1)} %sources_ref.3, bf16[4,2,128,128]{3,2,1,0:T(8,128)(2,1)} %near_ref.5, bf16[4,2,128,128]{3,2,1,0:T(8,128)(2,1)} %far_ref.5, ...), custom_call_target="tpu_custom_call" | custom-call | tf_op jit(solution)/shard_map/first_maps/pallas_call | solution.py:225
  11.9 0.0 copy-start.2
  11.9 0.6 copy-done.2
  12.5 1.8 %later_maps.1 = (bf16[2,256,256]{2,1,0:T(8,128)(2,1)S(1)}, bf16[2,256,256]{2,1,0:T(8,128)(2,1)S(1)}, f32[2,128,512]{2,1,0:T(8,128)S(1)}, bf16[128,128]{1,0:T(8,1...) custom-call(bf16[4,2,128,128]{3,2,1,0:T(8,128)(2,1)} %near_ref.5, bf16[4,2,128,128]{3,2,1,0:T(8,128)(2,1)} %far_ref.5, ...), custom_call_target="tpu_custom_call" | custom-call | tf_op jit(solution)/shard_map/later_maps/pallas_call | solution.py:267
  14.4 0.2 fusion.27
  14.6 0.0 collective-permute-done
  14.6 0.2 convolution_add_fusion.3
  14.8 0.0 copy-start.1
  14.8 1.9 %collective-permute-start.1 = (bf16[256,256]{1,0:T(8,128)(2,1)S(1)}, bf16[256,256]{1,0:T(8,128)(2,1)S(1)}, u32[]{:S(2)}, u32[]{:S(2)}) collective-permute-start(bf16[256,256]{1,0:T(8,128)(2,1)S(1)} %pad_maximum_fusion), channel_id=1, source_target_pairs={{0,2},{1,3},{2,0},{3,1},{4,6},{5,7},{6,4},{7,5},{8,10},{9,11},{10,... | collective-permute-start | bytes 393224 | tf_op jit(solution)/shard_map/ppermute | solution.py:17
  16.8 3.4 %collective-permute-start.4 = (bf16[528,256]{1,0:T(8,128)(2,1)S(1)}, bf16[528,256]{1,0:T(8,128)(2,1)S(1)}, u32[]{:S(2)}, u32[]{:S(2)}) collective-permute-start(bf16[528,256]{1,0:T(8,128)(2,1)S(1)} %get-tuple-element.39), channel_id=1, source_target_pairs={{0,2},{1,3},{2,0},{3,1},{4,6},{5,7},{6,4},{7,5},{8,10},{9,11},{10,... | collective-permute-start | bytes 811016 | tf_op jit(solution)/shard_map/ppermute | solution.py:17
  20.1 0.0 copy-done.1
  20.1 1.3 %middle_maps.1 = (bf16[256,256]{1,0:T(8,128)(2,1)S(1)}, bf16[256,256]{1,0:T(8,128)(2,1)S(1)}, f32[128,512]{1,0:T(8,128)S(1)}) custom-call(bf16[4,2,128,128]{3,2,1,0:T(8,128)(2,1)} %near_ref.5, bf16[4,2,128,128]{3,2,1,0:T(8,128)(2,1)} %far_ref.5, s32[2,2,2,4]{3,2,1,0:T(2,128)S(1)} %bitcast.58, f32[4,4,128]{2,1,0:T(4,128)} %bitcast.64), custom_call_target="tpu_custom_call" | custom-call | tf_op jit(solution)/shard_map/middle_maps/pallas_call | solution.py:247
  21.5 0.2 fusion.26
  21.7 0.2 collective-permute-done.1
  21.8 0.2 convolution_add_fusion.2
  22.1 9.7 %all_gather.16 = bf16[2,256,256]{2,1,0:T(8,128)(2,1)S(1)} all-gather(bf16[1,256,256]{2,1,0:T(8,128)(2,1)S(1)} %pad_maximum_fusion.2), channel_id=1, replica_groups={{0,4},{1,5},{2,6},{3,7},{8,12},{9,13},{10,14},{11,15},{16,20},{17,21},{..., dimensions={0}, use_global_device_ids=true | all-gather | bytes 393216 | tf_op jit(solution)/shard_map/all_gather | solution.py:23
  31.8 0.2 fusion.13
  32.0 0.2 convolution_add_fusion.1
  32.2 0.1 subtract_convert_fusion.4
  32.3 0.0 copy-start
  32.3 2.1 %collective-permute-start.2 = (bf16[256,256]{1,0:T(8,128)(2,1)S(1)}, bf16[256,256]{1,0:T(8,128)(2,1)S(1)}, u32[]{:S(2)}, u32[]{:S(2)}) collective-permute-start(bf16[256,256]{1,0:T(8,128)(2,1)S(1)} %pad_maximum_fusion.3), channel_id=1, source_target_pairs={{0,8},{1,9},{2,10},{3,11},{4,12},{5,13},{6,14},{7,15},{8,0},{9,1},... | collective-permute-start | bytes 393224 | tf_op jit(solution)/shard_map/ppermute | solution.py:17
  34.4 3.1 %collective-permute-start.3 = (bf16[256,256]{1,0:T(8,128)(2,1)S(1)}, bf16[256,256]{1,0:T(8,128)(2,1)S(1)}, u32[]{:S(2)}, u32[]{:S(2)}) collective-permute-start(bf16[256,256]{1,0:T(8,128)(2,1)S(1)} %bitcast.54), channel_id=1, source_target_pairs={{0,1},{1,0},{2,3},{3,2},{4,5},{5,4},{6,7},{7,6},{8,9},{9,8},{10,11... | collective-permute-start | bytes 393224 | tf_op jit(solution)/shard_map/ppermute | solution.py:17
  37.5 0.2 fusion.9
  37.7 0.0 collective-permute-done.4.lent_ref
  37.7 1.9 %collective-permute-start.5 = (bf16[256,256]{1,0:T(8,128)(2,1)S(1)}, bf16[256,256]{1,0:T(8,128)(2,1)S(1)}, u32[]{:S(2)}, u32[]{:S(2)}) collective-permute-start(bf16[256,256]{1,0:T(8,128)(2,1)S(1)} %slice.101), channel_id=1, source_target_pairs={{0,1},{1,0},{2,3},{3,2},{4,5},{5,4},{6,7},{7,6},{8,9},{9,8},{10,11... | collective-permute-start | bytes 393224 | tf_op jit(solution)/shard_map/ppermute | solution.py:17
  39.6 3.2 %collective-permute-done.2 = bf16[256,256]{1,0:T(8,128)(2,1)S(1)} collective-permute-done((bf16[256,256]{1,0:T(8,128)(2,1)S(1)}, bf16[256,256]{1,0:T(8,128)(2,1)S(1)}, u32[]{:S(2)}, u32[]{:S(2)}) %collective-permute-start.2) | collective-permute-done | bytes 131104 | tf_op jit(solution)/shard_map/ppermute | solution.py:17
  42.8 0.2 subtract_convert_fusion
  43.0 0.2 convolution_bitcast_fusion
  43.2 0.5 lent_maps.1
  43.7 0.0 collective-permute-done.3.across_ref
  43.7 0.0 collective-permute-done.5.across_lent_ref
  43.7 0.2 convolution_convert_fusion.1
  43.9 0.2 fusion.7
  44.1 11.1 %all-gather = bf16[512,256]{1,0:T(8,128)(2,1)S(1)} all-gather(bf16[256,256]{1,0:T(8,128)(2,1)S(1)} %convolution_convert_fusion.1), channel_id=2, replica_groups={{0,8},{1,9},{2,10},{3,11},{4,12},{5,13},{6,14},{7,15},{16,24},{17,25},{..., dimensions={0}, use_global_device_ids=true | all-gather | bytes 393216 | tf_op jit(solution)/shard_map/all_gather | solution.py:23
  55.4 0.2 convolution_convert_fusion
  55.6 0.2 fusion.11
  55.8 6.4 %all-gather.1 = bf16[512,256]{1,0:T(8,128)(2,1)S(1)} all-gather(bf16[256,256]{1,0:T(8,128)(2,1)S(1)} %convolution_convert_fusion), channel_id=3, replica_groups={{0,4},{1,5},{2,6},{3,7},{8,12},{9,13},{10,14},{11,15},{16,20},{17,21},{..., dimensions={0}, use_global_device_ids=true | all-gather | bytes 393216 | tf_op jit(solution)/shard_map/all_gather | solution.py:23
  62.3 0.1 add_convert_fusion.1
  62.3 1.4 %last_terms.1 = f32[128,1,256]{2,1,0:T(1,128)} custom-call(bf16[256,256]{1,0:T(8,128)(2,1)S(1)} %pad_maximum_fusion.5.turned_ref, bf16[256,256]{1,0:T(8,128)(2,1)S(1)} %get-tuple-element.29.near_1_ref, bf16[256,256]{1,0:T(8,128)(2,1)S(1)} %get-tuple-element.30.far_1_ref, bf16[256,256]{1,0:T(8,128)(2,1)S(1)} %get-tuple-element.25.near_ref, ...), custom_call_target="tpu_custom_call" | custom-call | tf_op jit(solution)/shard_map/last_terms/pallas_call | solution.py:327
  63.7 15.1 %all-to-all-start = ((f32[128,1,256]{2,1,0:T(1,128)}), f32[128,1,256]{2,1,0:T(1,128)S(1)}, u32[]{:S(2)}, u32[]{:S(2)}) async-start(f32[128,1,256]{2,1,0:T(1,128)} %last_terms.1), calls=%async_computation | async-start | bytes 262144 | tf_op jit(solution)/shard_map/all_to_all | solution.py:339
  78.8 0.0 copy-start.3
  78.8 0.2 convolution_bitcast_fusion.1
  79.0 0.7 copy-done.3
  79.7 0.7 maximum_subtract_fusion
  80.5 9.4 %all-to-all-done.terms_ref = f32[128,1,256]{2,1,0:T(1,128)S(1)} async-done(((f32[128,1,256]{2,1,0:T(1,128)}), f32[128,1,256]{2,1,0:T(1,128)S(1)}, u32[]{:S(2)}, u32[]{:S(2)}) %all-to-all-start) | async-done | bytes 131104 | tf_op jit(solution)/shard_map/all_to_all | solution.py:339
  89.9 0.7 last_ratio.1
  (12 shorter events, 0.3 us)
Async XLA Ops:
  1.6 12.9 %collective-permute-start = (bf16[256,256]{1,0:T(8,128)(2,1)S(1)}, bf16[256,256]{1,0:T(8,128)(2,1)S(1)}, u32[]{:S(2)}, u32[]{:S(2)}) collective-permute-start(bf16[256,256]{1,0:T(8,128)(2,1)S(1)} %first_field.1), channel_id=1, source_target_pairs={{0,1},{1,0},{2,3},{3,2},{4,5},{5,4},{6,7},{7,6},{8,9},{9,8},{10,11... | collective-permute-start | bytes 393224 | tf_op jit(solution)/shard_map/ppermute | solution.py:17
  11.9 0.7 copy-start.2
  14.8 5.3 %copy-start.1 = (s32[4,2,2,2]{0,3,2,1:T(2,128)S(1)}, s32[4,2,2,2]{0,3,2,1:T(2,128)}, u32[]{:S(2)}) copy-start(s32[4,2,2,2]{0,3,2,1:T(2,128)} %param.15) | copy-start | bytes 388
  14.8 7.0 %collective-permute-start.1 = (bf16[256,256]{1,0:T(8,128)(2,1)S(1)}, bf16[256,256]{1,0:T(8,128)(2,1)S(1)}, u32[]{:S(2)}, u32[]{:S(2)}) collective-permute-start(bf16[256,256]{1,0:T(8,128)(2,1)S(1)} %pad_maximum_fusion), channel_id=1, source_target_pairs={{0,2},{1,3},{2,0},{3,1},{4,6},{5,7},{6,4},{7,5},{8,10},{9,11},{10,... | collective-permute-start | bytes 393224 | tf_op jit(solution)/shard_map/ppermute | solution.py:17
  16.8 20.9 %collective-permute-start.4 = (bf16[528,256]{1,0:T(8,128)(2,1)S(1)}, bf16[528,256]{1,0:T(8,128)(2,1)S(1)}, u32[]{:S(2)}, u32[]{:S(2)}) collective-permute-start(bf16[528,256]{1,0:T(8,128)(2,1)S(1)} %get-tuple-element.39), channel_id=1, source_target_pairs={{0,2},{1,3},{2,0},{3,1},{4,6},{5,7},{6,4},{7,5},{8,10},{9,11},{10,... | collective-permute-start | bytes 811016 | tf_op jit(solution)/shard_map/ppermute | solution.py:17
  32.3 2.1 %copy-start = (bf16[2,128,256]{2,1,0:T(8,128)(2,1)S(1)}, bf16[2,128,256]{2,1,0:T(8,128)(2,1)}, u32[]{:S(2)}) copy-start(bf16[2,128,256]{2,1,0:T(8,128)(2,1)} %sources_ref.3) | copy-start | bytes 393220
  32.3 10.5 %collective-permute-start.2 = (bf16[256,256]{1,0:T(8,128)(2,1)S(1)}, bf16[256,256]{1,0:T(8,128)(2,1)S(1)}, u32[]{:S(2)}, u32[]{:S(2)}) collective-permute-start(bf16[256,256]{1,0:T(8,128)(2,1)S(1)} %pad_maximum_fusion.3), channel_id=1, source_target_pairs={{0,8},{1,9},{2,10},{3,11},{4,12},{5,13},{6,14},{7,15},{8,0},{9,1},... | collective-permute-start | bytes 393224 | tf_op jit(solution)/shard_map/ppermute | solution.py:17
  34.4 9.3 %collective-permute-start.3 = (bf16[256,256]{1,0:T(8,128)(2,1)S(1)}, bf16[256,256]{1,0:T(8,128)(2,1)S(1)}, u32[]{:S(2)}, u32[]{:S(2)}) collective-permute-start(bf16[256,256]{1,0:T(8,128)(2,1)S(1)} %bitcast.54), channel_id=1, source_target_pairs={{0,1},{1,0},{2,3},{3,2},{4,5},{5,4},{6,7},{7,6},{8,9},{9,8},{10,11... | collective-permute-start | bytes 393224 | tf_op jit(solution)/shard_map/ppermute | solution.py:17
  37.7 6.0 %collective-permute-start.5 = (bf16[256,256]{1,0:T(8,128)(2,1)S(1)}, bf16[256,256]{1,0:T(8,128)(2,1)S(1)}, u32[]{:S(2)}, u32[]{:S(2)}) collective-permute-start(bf16[256,256]{1,0:T(8,128)(2,1)S(1)} %slice.101), channel_id=1, source_target_pairs={{0,1},{1,0},{2,3},{3,2},{4,5},{5,4},{6,7},{7,6},{8,9},{9,8},{10,11... | collective-permute-start | bytes 393224 | tf_op jit(solution)/shard_map/ppermute | solution.py:17
  63.7 26.2 %all-to-all-start = ((f32[128,1,256]{2,1,0:T(1,128)}), f32[128,1,256]{2,1,0:T(1,128)S(1)}, u32[]{:S(2)}, u32[]{:S(2)}) async-start(f32[128,1,256]{2,1,0:T(1,128)} %last_terms.1), calls=%async_computation | async-start | bytes 262144 | tf_op jit(solution)/shard_map/all_to_all | solution.py:339
  78.8 0.9 %copy-start.3 = (bf16[2,128,256]{2,1,0:T(8,128)(2,1)S(1)}, bf16[2,128,256]{2,1,0:T(8,128)(2,1)}, u32[]{:S(2)}) copy-start(bf16[2,128,256]{2,1,0:T(8,128)(2,1)} %observed_ref.1) | copy-start | bytes 393220
